TPU v7x, 32 devices: a whole 2x2x4 slice. The times are simulated.
32 devices in a mesh: dp: 8 (over z, x), row: 2 (over core), col: 2 (over y).
Axes of the slice: x: 2, y: 2, z: 4, core: 2. Of those that a mesh axis runs over, the one named last changes fastest.
Arguments:
- inputs: bfloat16 [32768, 576], P(('dp', 'row', 'col')), may hold values from -6 to 6
- seq_ids: int32 [32768], P(('dp', 'row', 'col')), may hold values from 0 to 127, as said below
- norm_one: float32 [576], replicated, may hold values from 0.25 to 1.75
- w_qkv: bfloat16 [576, 960], replicated, may hold values from -0.25 to 0.25
- w_out: bfloat16 [576, 576], replicated, may hold values from -1 to 1
- norm_two: float32 [576], replicated, may hold values from 0.25 to 1.75
- w_gate: bfloat16 [576, 1536], P('col', 'row'), may hold values from -0.25 to 0.25
- w_up: bfloat16 [576, 1536], P('col', 'row'), may hold values from -0.25 to 0.25
- w_down: bfloat16 [1536, 576], P('row', 'col'), may hold values from -0.3125 to 0.3125
- out_grad: bfloat16 [32768, 576], P(('dp', 'row', 'col')), may hold values from -6 to 6
Outputs:
- outputs: bfloat16 [32768, 576], P(('dp', 'row', 'col'))
- input_grad: float32 [32768, 576], P(('dp', 'row', 'col'))
- grad_norm_one: float32 [576], replicated
- grad_qkv: float32 [576, 960], replicated
- grad_out: float32 [576, 576], replicated
- grad_norm_two: float32 [576], replicated
- grad_gate: float32 [576, 1536], P('col', 'row')
- grad_up: float32 [576, 1536], P('col', 'row')
- grad_down: float32 [1536, 576], P('row', 'col')
Inputs may be any that keep to these rules, and one draw needn't show every extreme that they name: `seq_ids`: within each block of 1024 consecutive tokens (the tokens of one device) the numbers start at 0 and rise by one where a new sequence starts; sequences start only at positions of the block that are multiples of 8; each sequence has 1 to 1024 tokens and lies inside one block; in some of the blocks (one at least), chosen from the seed, the first sequence has exactly 1024 tokens, and in one other block a sequence starts at every eighth position.
All inputs are finite; a program needn't handle non-finite values.
Results may differ from a plain program's by a relative error of at most 0.02.
Values may be sent and summed in bfloat16 or wider, within the bound.
No kernel may reach another device: no remote copies, remote signals or barrier semaphores. Data moves between devices by JAX's collectives and lax.ppermute only.
A program may use at most 192 MiB of HBM per device.

v0:
```python
import jax
import jax.numpy as jnp
from jax import lax
from jax.sharding import PartitionSpec as P

HEADS = 9
KV_HEADS = 3
HEAD = 64
MAXLEN = 1024
QBLOCK = 512


EPS = 1e-05
THETA = 100000.0


def places(seq_ids):
    token_count = seq_ids.shape[0]
    position = jnp.arange(token_count, dtype=jnp.int32)
    previous = jnp.concatenate([seq_ids[:1] - 1, seq_ids[:-1]])
    starts = jnp.where(seq_ids != previous, position, 0)
    return (position - lax.cummax(starts, axis=0)).astype(jnp.float32)


def tables(place, head_size):
    halfway = head_size // 2
    frequency = THETA ** (-2.0 * jnp.arange(halfway, dtype=jnp.float32) / head_size)
    angles = place[:, None] * frequency[None, :]
    return (jnp.cos(angles)[:, None, :], jnp.sin(angles)[:, None, :])


def rotate(values, cosine, sine_table):
    halfway = values.shape[-1] // 2
    front_half = values[..., :halfway]
    back_half = values[..., halfway:]
    return jnp.concatenate(
        [
            front_half * cosine - back_half * sine_table,
            back_half * cosine + front_half * sine_table,
        ],
        axis=-1,
    )


def rotate_back(grad_rows, cosine, sine_table):
    halfway = grad_rows.shape[-1] // 2
    front_half = grad_rows[..., :halfway]
    back_half = grad_rows[..., halfway:]
    return jnp.concatenate(
        [
            front_half * cosine + back_half * sine_table,
            back_half * cosine - front_half * sine_table,
        ],
        axis=-1,
    )


def contract_rows(left_side, right_side):
    return lax.dot_general(
        left_side, right_side, (((0,), (0,)), ((), ())), preferred_element_type=jnp.float32
    )


def contract_cols(left_side, right_side):
    return lax.dot_general(
        left_side, right_side, (((1,), (1,)), ((), ())), preferred_element_type=jnp.float32
    )


def norm_back(values, scale_rows, gain_vec, grad_in):
    weighted = grad_in * gain_vec
    gain_grad = jnp.sum(grad_in * values * scale_rows, axis=0)
    inner_sum = jnp.sum(weighted * values, axis=-1, keepdims=True)
    value_grad = (
        scale_rows * weighted
        - values * (scale_rows * scale_rows * scale_rows) * inner_sum / values.shape[-1]
    )
    return (value_grad, gain_grad)


def swiglu_back(hidden_grad, gate_pre, up_pre):
    grad_low = hidden_grad.astype(jnp.bfloat16).astype(jnp.float32)
    squashed = jax.nn.sigmoid(gate_pre)
    gate_low = (grad_low * up_pre * squashed * (1.0 + gate_pre * (1.0 - squashed))).astype(
        jnp.bfloat16
    )
    up_low = (grad_low * gate_pre * squashed).astype(jnp.bfloat16)
    return (gate_low, up_low)


def block_layout(token_count):
    block_rows = min(QBLOCK, token_count)
    window = min(token_count, block_rows + MAXLEN)
    return (block_rows, window)


def masked_scores(
    query_rows, key_rows, id_query, id_key, block_start, window_start, block_rows, window
):
    raw_dot = jnp.einsum("qgjd,kgd->gjqk", query_rows, key_rows, preferred_element_type=jnp.float32)
    scores = raw_dot * HEAD ** (-0.5)
    rows_at = block_start + jnp.arange(block_rows, dtype=jnp.int32)
    cols_at = window_start + jnp.arange(window, dtype=jnp.int32)
    allowed = (id_query[:, None] == id_key[None, :]) & (cols_at[None, :] <= rows_at[:, None])
    return jnp.where(allowed[None, None], scores, -1e30)


def attend_forward(queries, key_heads, value_heads, seq_ids):
    token_count = queries.shape[0]
    block_rows, window = block_layout(token_count)

    def one_block(block_index):
        block_start = block_index * block_rows
        window_start = jnp.clip(block_start + block_rows - window, 0, token_count - window)
        query_rows = lax.dynamic_slice_in_dim(queries, block_start, block_rows, 0)
        scores = masked_scores(
            query_rows,
            key_heads,
            lax.dynamic_slice_in_dim(seq_ids, block_start, block_rows, 0),
            seq_ids,
            block_start,
            window_start,
            block_rows,
            window,
        )
        peak_score = jnp.max(scores, axis=-1, keepdims=True)
        exponent = jnp.exp(scores - peak_score)
        summed = jnp.sum(exponent, axis=-1, keepdims=True)
        attn_probs = (exponent / summed).astype(jnp.bfloat16)
        mixed_rows = jnp.einsum(
            "gjqk,kgd->qgjd", attn_probs, value_heads, preferred_element_type=jnp.float32
        )
        return (
            mixed_rows.astype(jnp.bfloat16).reshape(block_rows, HEADS * HEAD),
            (peak_score + jnp.log(summed))[..., 0],
        )

    mixed_all, logsums = lax.map(one_block, jnp.arange(token_count // block_rows, dtype=jnp.int32))
    return (mixed_all.reshape(token_count, HEADS * HEAD), logsums)


def attend_backward(queries, key_heads, value_heads, seq_ids, logsums, attended_low):
    token_count = queries.shape[0]
    block_rows, window = block_layout(token_count)

    def one_block(totals_kv, pieces):
        block_index, logsum_rows = pieces
        key_total, value_total = totals_kv
        block_start = block_index * block_rows
        window_start = jnp.clip(block_start + block_rows - window, 0, token_count - window)
        query_rows = lax.dynamic_slice_in_dim(queries, block_start, block_rows, 0)
        scores = masked_scores(
            query_rows,
            key_heads,
            lax.dynamic_slice_in_dim(seq_ids, block_start, block_rows, 0),
            seq_ids,
            block_start,
            window_start,
            block_rows,
            window,
        )
        soft_probs = jnp.exp(scores - logsum_rows[..., None])
        grad_rows = lax.dynamic_slice_in_dim(attended_low, block_start, block_rows, 0)
        prob_grad = jnp.einsum(
            "qgjd,kgd->gjqk", grad_rows, value_heads, preferred_element_type=jnp.float32
        )
        inner_sum = jnp.sum(soft_probs * prob_grad, axis=-1, keepdims=True)
        score_low = (soft_probs * (prob_grad - inner_sum) * HEAD ** (-0.5)).astype(jnp.bfloat16)
        query_grad = jnp.einsum(
            "gjqk,kgd->qgjd", score_low, key_heads, preferred_element_type=jnp.float32
        )
        key_part = jnp.einsum(
            "gjqk,qgjd->kgd", score_low, query_rows, preferred_element_type=jnp.float32
        )
        value_part = jnp.einsum(
            "gjqk,qgjd->kgd",
            soft_probs.astype(jnp.bfloat16),
            grad_rows,
            preferred_element_type=jnp.float32,
        )
        key_total = key_total + key_part
        value_total = value_total + value_part
        return ((key_total, value_total), query_grad)

    zeros_kv = jnp.zeros(key_heads.shape, jnp.float32)
    block_ids = jnp.arange(token_count // block_rows, dtype=jnp.int32)
    (key_grad, value_grad), query_grads = lax.scan(
        one_block, (zeros_kv, zeros_kv), (block_ids, logsums)
    )
    return (query_grads.reshape(token_count, HEADS, HEAD), key_grad, value_grad)


def per_device(inputs, seq_ids, norm_one, w_qkv, w_out, norm_two, w_gate, w_up, w_down, out_grad):
    token_count = inputs.shape[0]
    group_size = HEADS // KV_HEADS
    query_width = HEADS * HEAD
    key_width = KV_HEADS * HEAD
    hidden_half = w_gate.shape[1]
    inputs_wide = inputs.astype(jnp.float32)
    scale_one = lax.rsqrt(jnp.mean(inputs_wide * inputs_wide, axis=-1, keepdims=True) + EPS)
    normed_one = (inputs_wide * scale_one * norm_one).astype(jnp.bfloat16)
    joined_qkv = jnp.dot(normed_one, w_qkv, preferred_element_type=jnp.float32)
    cosine, sine_table = tables(places(seq_ids), HEAD)
    queries = (
        rotate(joined_qkv[:, :query_width].reshape(token_count, HEADS, HEAD), cosine, sine_table)
        .astype(jnp.bfloat16)
        .reshape(token_count, KV_HEADS, group_size, HEAD)
    )
    key_heads = rotate(
        joined_qkv[:, query_width : query_width + key_width].reshape(token_count, KV_HEADS, HEAD),
        cosine,
        sine_table,
    ).astype(jnp.bfloat16)
    value_heads = (
        joined_qkv[:, query_width + key_width :]
        .reshape(token_count, KV_HEADS, HEAD)
        .astype(jnp.bfloat16)
    )
    attended, logsums = attend_forward(queries, key_heads, value_heads, seq_ids)
    middle = inputs_wide + jnp.dot(attended, w_out, preferred_element_type=jnp.float32)
    scale_two = lax.rsqrt(jnp.mean(middle * middle, axis=-1, keepdims=True) + EPS)
    normed_two = (middle * scale_two * norm_two).astype(jnp.bfloat16)
    w_pair = jnp.concatenate([w_gate, w_up], axis=1)
    halves = lax.all_to_all(normed_two, "col", split_axis=1, concat_axis=0, tiled=True)
    spread = lax.all_gather(halves, "row", axis=0, tiled=True)
    pair_out = lax.psum_scatter(
        jnp.dot(spread, w_pair, preferred_element_type=jnp.float32).astype(jnp.bfloat16),
        "col",
        scatter_dimension=0,
        tiled=True,
    ).astype(jnp.float32)
    gate_pre = pair_out[:, :hidden_half]
    up_pre = pair_out[:, hidden_half:]
    hidden = (gate_pre * jax.nn.sigmoid(gate_pre) * up_pre).astype(jnp.bfloat16)
    hidden_all = lax.all_gather(hidden, "col", axis=0, tiled=True)
    block_out = lax.psum_scatter(
        jnp.dot(hidden_all, w_down, preferred_element_type=jnp.float32).astype(jnp.bfloat16),
        "row",
        scatter_dimension=0,
        tiled=True,
    ).astype(jnp.float32)
    mlp_out = lax.all_to_all(
        block_out.astype(jnp.bfloat16), "col", split_axis=0, concat_axis=1, tiled=True
    ).astype(block_out.dtype)
    outputs = (middle + mlp_out).astype(jnp.bfloat16)
    grad_halves = lax.all_to_all(out_grad, "col", split_axis=1, concat_axis=0, tiled=True)
    grad_all = lax.all_gather(grad_halves, "row", axis=0, tiled=True)
    down_grad = contract_rows(hidden_all, grad_all)
    hidden_grad = lax.psum_scatter(
        contract_cols(grad_all, w_down).astype(jnp.bfloat16), "col", scatter_dimension=0, tiled=True
    ).astype(jnp.float32)
    gate_low, up_low = swiglu_back(hidden_grad, gate_pre, up_pre)
    pair_grad = jnp.concatenate([gate_low, up_low], axis=1)
    pair_all = lax.all_gather(pair_grad, "col", axis=0, tiled=True)
    pair_weight_grad = contract_rows(spread, pair_all)
    block_grad = lax.psum_scatter(
        contract_cols(pair_all, w_pair).astype(jnp.bfloat16), "row", scatter_dimension=0, tiled=True
    ).astype(jnp.float32)
    normed_two_grad = lax.all_to_all(
        block_grad.astype(jnp.bfloat16), "col", split_axis=0, concat_axis=1, tiled=True
    ).astype(block_grad.dtype)
    block_sums = lax.psum(
        (pair_weight_grad[:, :hidden_half], pair_weight_grad[:, hidden_half:], down_grad), "dp"
    )
    middle_part, gain_two_grad = norm_back(middle, scale_two, norm_two, normed_two_grad)
    middle_grad = out_grad.astype(jnp.float32) + middle_part
    middle_low = middle_grad.astype(jnp.bfloat16)
    out_weight_grad = contract_rows(attended, middle_low)
    attended_low = contract_cols(middle_low, w_out).astype(jnp.bfloat16)
    query_grad, key_grad, value_grad = attend_backward(
        queries,
        key_heads,
        value_heads,
        seq_ids,
        logsums,
        attended_low.reshape(token_count, KV_HEADS, group_size, HEAD),
    )
    joined_low = jnp.concatenate(
        [
            rotate_back(query_grad, cosine, sine_table).reshape(token_count, query_width),
            rotate_back(key_grad, cosine, sine_table).reshape(token_count, key_width),
            value_grad.reshape(token_count, key_width),
        ],
        axis=1,
    ).astype(jnp.bfloat16)
    qkv_grad = contract_rows(normed_one, joined_low)
    normed_one_grad = contract_cols(joined_low, w_qkv)
    input_part, gain_one_grad = norm_back(inputs_wide, scale_one, norm_one, normed_one_grad)
    input_grad = middle_grad + input_part
    shared = lax.psum(
        (qkv_grad, out_weight_grad, gain_one_grad, gain_two_grad), ("dp", "row", "col")
    )
    grad_gate, grad_up, grad_down = block_sums
    grad_qkv, grad_out, grad_norm_one, grad_norm_two = shared
    return (
        outputs,
        input_grad,
        grad_norm_one,
        grad_qkv,
        grad_out,
        grad_norm_two,
        grad_gate,
        grad_up,
        grad_down,
    )


def solution(mesh):
    placed = (
        P(("dp", "row", "col"), None),
        P(("dp", "row", "col")),
        P(),
        P(),
        P(),
        P(),
        P("col", "row"),
        P("col", "row"),
        P("row", "col"),
        P(("dp", "row", "col"), None),
    )
    return jax.shard_map(
        per_device,
        mesh=mesh,
        in_specs=placed,
        out_specs=(
            P(("dp", "row", "col"), None),
            P(("dp", "row", "col"), None),
            P(),
            P(),
            P(),
            P(),
            P("col", "row"),
            P("col", "row"),
            P("row", "col"),
        ),
        check_vma=False,
    )
```

profile of v0, /device:TPU:0, one launch (start us, length us, event | category | flops | bytes accessed | tf_op | source)
XLA Modules:
  0.0 1067.5 jit_solution(18418936468185688066)
XLA Ops:
  20.8 38.4 %while.35 = (s32[]{:T(128)}, bf16[2,512,576]{1,2,0:T(8,128)(2,1)}, f32[2,3,3,512]{3,2,1,0:T(4,128)}, s32[2]{0:T(128)S(1)}, s32[1024]{0:T(1024)S(1)}, /*index=5*/...) while((s32[]{:T(128)}, bf16[2,512,576]{1,2,0:T(8,128)(2,1)}, ...), condition=%wide.region_6.7_spmd, body=%wide.region_3.6_spmd.sunk | while | flops 1266447360 | bytes 62042360 | solution.py:138
  62.6 19.1 %all_to_all.64 = bf16[1024,2,288]{0,2,1:T(8,128)(2,1)S(1)} all-to-all(bf16[1024,2,288]{0,2,1:T(8,128)(2,1)S(1)} %bitcast.262), channel_id=1, replica_groups=mesh['dp'=8,'row'=2,'col'=2] {'col'}, dimensions={1} | all-to-all | bytes 2359296 | tf_op jit(solution)/shard_map/all_to_all | solution.py:224
  83.3 16.6 %all_to_all.65 = bf16[1024,2,288]{0,2,1:T(8,128)(2,1)S(1)} all-to-all(bf16[1024,2,288]{0,2,1:T(8,128)(2,1)S(1)} %bitcast.269), channel_id=1, replica_groups=mesh['dp'=8,'row'=2,'col'=2] {'col'}, dimensions={1} | all-to-all | bytes 2359296 | tf_op jit(solution)/shard_map/all_to_all | solution.py:246
  102.7 11.3 %convolution_convert_fusion = bf16[4096,1536]{1,0:T(8,128)(2,1)} fusion(bf16[4096,288]{0,1:T(8,128)(2,1)} %all-gather.5.cloned.1.call-done, bf16[288,1536]{1,0:T(8,128)(2,1)} %constant_dynamic-update-slice_fusion.1), kind=kOutput, calls=%fused_computation.64 | convolution fusion | flops 3630170112 | bytes 15826944 | tf_op jit(solution)/shard_map/dot_general | solution.py:227
  115.1 8.2 convolution_convert_fusion.1
  123.4 137.5 %reduce-scatter.5.cloned.1.call-done = bf16[2048,1536]{1,0:T(8,128)(2,1)} async-done(((bf16[4096,1536]{1,0:T(8,128)(2,1)}), bf16[2048,1536]{1,0:T(8,128)(2,1)}) %reduce-scatter.5.cloned.1.call-update) | async-done | bytes 6291472 | tf_op jit(solution)/shard_map/reduce_scatter | solution.py:226
  260.9 9.8 convert_element_type.132
  270.7 69.6 %reduce-scatter.9.cloned.1.call-done = bf16[2048,768]{1,0:T(8,128)(2,1)} async-done(((bf16[4096,768]{1,0:T(8,128)(2,1)}), bf16[2048,768]{1,0:T(8,128)(2,1)}) %reduce-scatter.9.cloned.1.call-update) | async-done | bytes 3145744 | tf_op jit(solution)/shard_map/reduce_scatter | solution.py:249
  340.2 9.7 fusion.59
  356.1 74.4 %all-gather.7.cloned.1.call-done = bf16[4096,768]{1,0:T(8,128)(2,1)} async-done(((bf16[2048,768]{1,0:T(8,128)(2,1)}), bf16[4096,768]{1,0:T(8,128)(2,1)}) %all-gather.7.cloned.1.call-update) | async-done | bytes 6291472 | tf_op jit(solution)/shard_map/all_gather | solution.py:235
  437.2 147.2 %all-gather.11.cloned.1.call-done = bf16[4096,1536]{1,0:T(8,128)(2,1)} async-done(((bf16[2048,1536]{1,0:T(8,128)(2,1)}), bf16[4096,1536]{1,0:T(8,128)(2,1)}) %all-gather.11.cloned.1.call-update) | async-done | bytes 12582928 | tf_op jit(solution)/shard_map/all_gather | solution.py:254
  584.4 10.0 convolution_convert_fusion.3
  623.0 7.5 fusion.90
  647.4 249.9 %while.36 = (s32[]{:T(128)}, f32[1024,3,64]{0,2,1:T(8,128)}, f32[1024,3,64]{0,2,1:T(8,128)S(1)}, f32[2,512,3,3,64]{1,0,4,3,2:T(2,128)}, s32[2]{0:T(128)S(1)}, /*...) while((s32[]{:T(128)}, f32[1024,3,64]{0,2,1:T(8,128)}, ...), condition=%wide.region_15.16_spmd.clone, body=%wide.region_13.15_spmd.clone.sunk | while | flops 3144954368 | bytes 260716880 | solution.py:187
  660.7 10.3 fusion.137
  670.9 43.3 %fusion.139 = f32[1024,3,64]{0,2,1:T(8,128)} fusion(f32[3,512,3,1024]{3,1,2,0:T(8,128)} %fusion.137, f32[3,512,3,1024]{3,1,2,0:T(8,128)} %copy-done.1, f32[3,3,512]{2,1,0:T(4,128)S(1)} %dynamic-slice_bitcast_fusion.2, pred[512,1024]{1,0:T(8,128)(4,1)S(1)} %compare_and_fusion.5, f32[1024,3,64]{0,2,1:T(8,128)} %get-tuple-element.682, ...), kind=kOutput, calls=%fused_computation.37.clone.1 | convolution fusion | flops 656283136 | bytes 78757896 | tf_op jit(solution)/shard_map/while/body/eval_jaxpr/gjqk,qgjd->kgd/dot_general | solution.py:172
  714.3 34.2 %fusion.141 = f32[1,512,3,3,64]{1,4,3,2,0:T(8,128)} fusion(f32[3,512,3,1024]{3,1,2,0:T(8,128)} %fusion.137, f32[3,512,3,1024]{3,1,2,0:T(8,128)} %copy-done.1, f32[3,3,512]{2,1,0:T(4,128)S(1)} %dynamic-slice_bitcast_fusion.2, pred[512,1024]{1,0:T(8,128)(4,1)S(1)} %compare_and_fusion.5, bf16[1024,3,64]{0,2,1:T(8,128)(2,1)S(1)} %get-tuple-element.704), kind=kOutput, calls=%fused_computation.35.clone.1 | convolution fusion | flops 655889920 | bytes 39864320 | tf_op jit(solution)/shard_map/while/body/eval_jaxpr/gjqk,kgd->qgjd/dot_general | solution.py:169
  750.9 21.9 %dynamic_update_slice.38 = f32[2,512,3,3,64]{1,0,4,3,2:T(2,128)} dynamic-update-slice(f32[2,512,3,3,64]{1,0,4,3,2:T(2,128)} %get-tuple-element.684, f32[1,512,3,3,64]{1,0,4,3,2:T(1,128)S(1)} %copy.57, s32[]{:T(128)S(6)} %copy.75, s32[]{:T(128)} %constant.179.clone.1..sunk.1, s32[]{:T(128)} %constant.179.clone.1..sunk.1, s32[]{:T(128)} %constant.179.clone.1..sunk.1, s32[]{:T(128)} %constant.179.clone.1..sunk.1) | dynamic-update-slice | bytes 2359300 | tf_op jit(solution)/shard_map/while/body/jit(dynamic_update_index_in_dim)/dynamic_update_slice | solution.py:187
  785.7 10.3 fusion.137
  796.0 43.5 %fusion.139 = f32[1024,3,64]{0,2,1:T(8,128)} fusion(f32[3,512,3,1024]{3,1,2,0:T(8,128)} %fusion.137, f32[3,512,3,1024]{3,1,2,0:T(8,128)} %copy-done.1, f32[3,3,512]{2,1,0:T(4,128)S(1)} %dynamic-slice_bitcast_fusion.2, pred[512,1024]{1,0:T(8,128)(4,1)S(1)} %compare_and_fusion.5, f32[1024,3,64]{0,2,1:T(8,128)} %get-tuple-element.682, ...), kind=kOutput, calls=%fused_computation.37.clone.1 | convolution fusion | flops 656283136 | bytes 78757896 | tf_op jit(solution)/shard_map/while/body/eval_jaxpr/gjqk,qgjd->kgd/dot_general | solution.py:172
  839.5 33.2 %fusion.141 = f32[1,512,3,3,64]{1,4,3,2,0:T(8,128)} fusion(f32[3,512,3,1024]{3,1,2,0:T(8,128)} %fusion.137, f32[3,512,3,1024]{3,1,2,0:T(8,128)} %copy-done.1, f32[3,3,512]{2,1,0:T(4,128)S(1)} %dynamic-slice_bitcast_fusion.2, pred[512,1024]{1,0:T(8,128)(4,1)S(1)} %compare_and_fusion.5, bf16[1024,3,64]{0,2,1:T(8,128)(2,1)S(1)} %get-tuple-element.704), kind=kOutput, calls=%fused_computation.35.clone.1 | convolution fusion | flops 655889920 | bytes 39864320 | tf_op jit(solution)/shard_map/while/body/eval_jaxpr/gjqk,kgd->qgjd/dot_general | solution.py:169
  875.2 21.9 %dynamic_update_slice.38 = f32[2,512,3,3,64]{1,0,4,3,2:T(2,128)} dynamic-update-slice(f32[2,512,3,3,64]{1,0,4,3,2:T(2,128)} %get-tuple-element.684, f32[1,512,3,3,64]{1,0,4,3,2:T(1,128)S(1)} %copy.57, s32[]{:T(128)S(6)} %copy.75, s32[]{:T(128)} %constant.179.clone.1..sunk.1, s32[]{:T(128)} %constant.179.clone.1..sunk.1, s32[]{:T(128)} %constant.179.clone.1..sunk.1, s32[]{:T(128)} %constant.179.clone.1..sunk.1) | dynamic-update-slice | bytes 2359300 | tf_op jit(solution)/shard_map/while/body/jit(dynamic_update_index_in_dim)/dynamic_update_slice | solution.py:187
  915.9 40.1 %all-reduce = (f32[576]{0:T(1024)}, f32[576]{0:T(1024)}) all-reduce(f32[576]{0:T(1024)S(1)} %get-tuple-element.430, f32[576]{0:T(1024)S(1)} %copy-done.33), channel_id=1, replica_groups=mesh['dp'=8,'row'=2,'col'=2] {'dp','row','col'}, use_global_device_ids=true, to_apply=%region_18.19 | all-reduce | flops 1152 | bytes 9216 | tf_op jit(solution)/shard_map/psum | solution.py:290
  960.4 92.1 %all-reduce.6.cloned.1.call-done = (f32[576,960]{1,0:T(8,128)}, f32[576,576]{1,0:T(8,128)}) async-done(((f32[576,960]{1,0:T(8,128)}, f32[576,576]{1,0:T(8,128)}), (f32[576,960]{1,0:T(8,128)}, f32[576,576]{1,0:T(8,128)})) %all-reduce.6.cloned.1.call-update) | async-done | bytes 3538960 | tf_op jit(solution)/shard_map/psum | solution.py:290
  (203 shorter events, 177.0 us)
Async XLA Ops:
  7.2 95.5 %all-gather.5.cloned.1.call-start = ((), (), s32[]{:S(2)}) async-start(), calls=%async_computation.8 | async-start | bytes 3538944 | tf_op jit(solution)/shard_map/all_gather | solution.py:225
  62.3 19.3 %copy-start.2 = (f32[1024,576]{0,1:T(8,128)}, f32[1024,576]{0,1:T(8,128)S(1)}, u32[]{:S(2)}) copy-start(f32[1024,576]{0,1:T(8,128)S(1)} %get-tuple-element.504) | copy-start | bytes 7077892
  82.8 31.4 %all-gather.9.cloned.1.call-start = ((), (), s32[]{:S(2)}) async-start(), calls=%async_computation.12 | async-start | bytes 3538944 | tf_op jit(solution)/shard_map/all_gather | solution.py:247
  101.1 159.8 %reduce-scatter.5.cloned.1.call-start = ((), (), s32[]{:S(2)}) async-start(), calls=%async_computation.9 | async-start | bytes 18874368 | tf_op jit(solution)/shard_map/reduce_scatter | solution.py:226
  114.1 226.1 %reduce-scatter.9.cloned.1.call-start = ((), (), s32[]{:S(2)}) async-start(), calls=%async_computation.13 | async-start | bytes 9437184 | tf_op jit(solution)/shard_map/reduce_scatter | solution.py:249
  123.3 307.1 %all-gather.7.cloned.1.call-start = ((), (), s32[]{:S(2)}) async-start(), calls=%async_computation.10 | async-start | bytes 9437184 | tf_op jit(solution)/shard_map/all_gather | solution.py:235
  349.9 234.4 %all-gather.11.cloned.1.call-start = ((), (), s32[]{:S(2)}) async-start(), calls=%async_computation.14 | async-start | bytes 18874368 | tf_op jit(solution)/shard_map/all_gather | solution.py:254
  356.0 240.6 %reduce-scatter.7.cloned.1.call-start = ((), (), s32[]{:S(2)}) async-start(), calls=%async_computation.11 | async-start | bytes 3538944 | tf_op jit(solution)/shard_map/reduce_scatter | solution.py:236
  436.7 174.0 %reduce-scatter.11.cloned.1.call-start = ((), (), s32[]{:S(2)}) async-start(), calls=%async_computation.15 | async-start | bytes 3538944 | tf_op jit(solution)/shard_map/reduce_scatter | solution.py:256
  599.0 19.3 %all-to-all-start.1 = ((bf16[2,1024,288]{1,2,0:T(8,128)(2,1)}), bf16[2,1024,288]{1,2,0:T(8,128)(2,1)S(1)}, u32[]{:S(2)}, u32[]{:S(2)}) async-start(bf16[2,1024,288]{1,2,0:T(8,128)(2,1)} %bitcast.266), calls=%async_computation.3 | async-start | bytes 2359296 | tf_op jit(solution)/shard_map/all_to_all | solution.py:242
  619.4 18.5 %all-to-all-start.3 = ((bf16[2,1024,288]{1,2,0:T(8,128)(2,1)}), bf16[2,1024,288]{1,2,0:T(8,128)(2,1)S(1)}, u32[]{:S(2)}, u32[]{:S(2)}) async-start(bf16[2,1024,288]{1,2,0:T(8,128)(2,1)} %bitcast.263), calls=%async_computation.7 | async-start | bytes 2359296 | tf_op jit(solution)/shard_map/all_to_all | solution.py:259
  623.0 337.4 %all-reduce.8.cloned.1.call-start = ((), (), s32[]{:S(2)}) async-start(), calls=%async_computation.17 | async-start | bytes 5308416 | tf_op jit(solution)/shard_map/psum | solution.py:262
  631.9 420.6 %all-reduce.6.cloned.1.call-start = ((), (), s32[]{:S(2)}) async-start(), calls=%async_computation.16 | async-start | bytes 7667712 | tf_op jit(solution)/shard_map/psum | solution.py:290
  637.8 4.4 copy-start.3
  637.8 4.4 copy-start.11
  654.0 6.7 copy-start.1
  779.3 6.4 copy-start.1
  897.3 4.4 copy-start.15
  897.3 4.4 copy-start.17
  897.3 4.4 copy-start.24
  901.7 6.0 copy-start.27
  911.7 4.3 copy-start.33
  911.7 44.3 %copy-start.30 = (f32[1024]{0:T(1024)S(1)}, f32[1024]{0:T(1024)}, u32[]{:S(2)}) copy-start(f32[1024]{0:T(1024)} %get-tuple-element.499) | copy-start | bytes 12292
  1052.5 3.5 copy-start.18
  (27 other events, 50.7 us)
Sparse Core Ops, SparseCore 0:
  82.9 11.4 all-gather.4
  101.2 11.5 all-gather.8
  115.1 145.7 reduce-scatter.4
  263.0 77.1 reduce-scatter.8
  350.1 80.3 all-gather.6
  431.8 152.4 all-gather.10
  586.6 9.9 reduce-scatter.6
  599.4 11.1 reduce-scatter.10
  632.0 118.2 all-reduce.7
  910.8 141.6 all-reduce.5
where the time goes:
time: 1080 us; the launch traced here: 1070 us
  waiting for transfers between devices  536 us (50%)
  matrix products  282 us (26%)
  local copies, waits for them, and re-layouts  90.2 us (8%)
  blocking collectives  75.7 us (7%)
  other arithmetic  56.4 us (5%)
  between operations  15.5 us (1%)
    all_gather x1, waiting for transfers between devices, per_device(): pair_all = lax.all_gather(pair_grad, 'col', axis=0, tiled=True)  147 us
    reduce_scatter x1, waiting for transfers between devices, per_device(): lax.psum_scatter(jnp.dot(spread, w_pair, preferred_element_type=jnp.float...  138 us
    psum x1, waiting for transfers between devices, per_device(): lax.psum((qkv_grad, out_weight_grad, gain_one_grad, gain_two_grad), ('dp'...  92.1 us
    dot_general x2, matrix products, one_block(): jnp.einsum('gjqk,qgjd->kgd', score_low, query_rows, preferred_element_typ...  86.8 us
    all_gather x1, waiting for transfers between devices, per_device(): hidden_all = lax.all_gather(hidden, 'col', axis=0, tiled=True)  74.4 us
    reduce_scatter x1, waiting for transfers between devices, per_device(): lax.psum_scatter(contract_cols(grad_all, w_down).astype(jnp.bfloat16), 'c...  69.6 us
    dot_general x2, matrix products, one_block(): jnp.einsum('gjqk,kgd->qgjd', score_low, key_heads, preferred_element_type...  67.4 us
    dynamic_update_slice x4, local copies, waits for them, and re-layouts, attend_backward(): lax.scan(one_block, (zeros_kv, zeros_kv), (block_ids, logsums))  48.8 us
  transfers between devices with their start and end apart: 12, of which 9 were waited for; matrix products, arithmetic and copies ran while one was open for 33% of the time, Pallas kernels for 0%

commit v1 on v0

v1 whole, which is shorter than its diff:
```python
import functools

import jax
import jax.numpy as jnp
from jax import lax
from jax.experimental import pallas as pl
from jax.experimental.pallas import tpu as pltpu
from jax.sharding import PartitionSpec as P

HEADS = 9
KV_HEADS = 3
GROUP = HEADS // KV_HEADS
HEAD = 64
BLOCK = 256
LANES = 128
LOG2E = 1.4426950408889634
EPS = 1e-05
THETA = 100000.0
NEG = -1e30
F32 = jnp.float32
BF16 = jnp.bfloat16


def dot_nn(a, b):
    return lax.dot_general(a, b, (((1,), (0,)), ((), ())), preferred_element_type=F32)


def dot_nt(a, b):
    return lax.dot_general(a, b, (((1,), (1,)), ((), ())), preferred_element_type=F32)


def dot_tn(a, b):
    return lax.dot_general(a, b, (((0,), (0,)), ((), ())), preferred_element_type=F32)


def partner_lanes(x):
    lane = lax.broadcasted_iota(jnp.int32, x.shape, 1)
    front = lax.rem(lane, HEAD) < HEAD // 2
    return jnp.where(
        front, pltpu.roll(x, LANES - HEAD // 2, 1), pltpu.roll(x, HEAD // 2, 1)
    )


def allowed_tile(start_row, key_start, query_start, diagonal):
    shape = (BLOCK, start_row.shape[1])
    keys = key_start + lax.broadcasted_iota(jnp.int32, shape, 0)
    mask = keys >= start_row
    if diagonal:
        rows = query_start + lax.rem(lax.broadcasted_iota(jnp.int32, shape, 1), BLOCK)
        mask = mask & (keys <= rows)
    return mask


def front_kernel(
    inputs_ref, start_ref, cos_ref, sin_ref, norm_ref, w_qkv_ref, w_out_ref,
    q_ref, k_ref, v_ref, lse_ref, att_ref, mid_ref,
    k_all, vt_all, acc, stat_m, stat_l,
):
    i = pl.program_id(0)
    x = inputs_ref[...].astype(F32)
    scale = lax.rsqrt(jnp.mean(x * x, axis=-1, keepdims=True) + EPS)
    normed = (x * scale * norm_ref[...]).astype(BF16)
    joined = dot_nn(normed, w_qkv_ref[...])
    width = (HEADS + KV_HEADS) * HEAD
    cosine, sine = cos_ref[...], sin_ref[...]
    for c in range(width // LANES):
        part = joined[:, c * LANES:(c + 1) * LANES]
        turned = (part * cosine + partner_lanes(part) * sine).astype(BF16)
        for half in range(2):
            h = 2 * c + half
            piece = turned[:, half * HEAD:(half + 1) * HEAD]
            if h < HEADS:
                q_ref[h] = piece * BF16(HEAD ** -0.5)
            else:
                k_ref[h - HEADS] = piece
                k_all[h - HEADS, pl.ds(pl.multiple_of(i * BLOCK, BLOCK), BLOCK), :] = piece
    values = joined[:, width:]
    values_t = values.T.astype(BF16)
    for g in range(KV_HEADS):
        v_ref[g] = values[:, g * HEAD:(g + 1) * HEAD].astype(BF16)
        vt_all[g, i] = values_t[g * HEAD:(g + 1) * HEAD, :]
    start = start_ref[...]
    start_row = jnp.concatenate([start] * GROUP, axis=1)
    stat_m[...] = jnp.full(stat_m.shape, NEG, F32)
    stat_l[...] = jnp.zeros(stat_l.shape, F32)
    acc[...] = jnp.zeros(acc.shape, F32)

    def tile(j, diagonal):
        mask = allowed_tile(start_row, j * BLOCK, i * BLOCK, diagonal)
        for g in range(KV_HEADS):
            queries = q_ref[g * GROUP:(g + 1) * GROUP].reshape(GROUP * BLOCK, HEAD)
            keys = k_all[g, pl.ds(pl.multiple_of(j * BLOCK, BLOCK), BLOCK), :]
            scores = jnp.where(mask, dot_nt(keys, queries) * LOG2E, NEG)
            peak_old = stat_m[g:g + 1]
            peak = jnp.maximum(peak_old, jnp.max(scores, axis=0, keepdims=True))
            expo = jnp.exp2(scores - peak)
            expo = jnp.where(mask, expo, 0.0)
            fade = jnp.exp2(peak_old - peak)
            stat_m[g:g + 1] = peak
            stat_l[g:g + 1] = stat_l[g:g + 1] * fade + jnp.sum(expo, axis=0, keepdims=True)
            acc[g] = acc[g] * fade + dot_nn(vt_all[g, j], expo.astype(BF16))

    def step(j, carry):
        tile(j, False)
        return carry

    lax.fori_loop(0, i, step, 0)
    tile(i, True)
    pieces = []
    for g in range(KV_HEADS):
        total = stat_l[g:g + 1]
        mixed = acc[g] / total
        logsum = stat_m[g:g + 1] + jnp.log2(total)
        for h in range(GROUP):
            lse_ref[g * GROUP + h:g * GROUP + h + 1, :] = logsum[:, h * BLOCK:(h + 1) * BLOCK]
            pieces.append(mixed[:, h * BLOCK:(h + 1) * BLOCK])
    attended = jnp.concatenate(pieces, axis=0).T.astype(BF16)
    att_ref[...] = attended
    mid_ref[...] = x + dot_nn(attended, w_out_ref[...])


def front(inputs, start, cosine, sine, norm_one, w_qkv, w_out):
    tokens, width = inputs.shape
    blocks = tokens // BLOCK
    whole = lambda i: (0, 0)
    rows = lambda i: (i, 0)
    return pl.pallas_call(
        front_kernel,
        grid=(blocks,),
        in_specs=[
            pl.BlockSpec((BLOCK, width), rows),
            pl.BlockSpec((1, BLOCK), lambda i: (0, i)),
            pl.BlockSpec((BLOCK, LANES), rows),
            pl.BlockSpec((BLOCK, LANES), rows),
            pl.BlockSpec((1, width), whole),
            pl.BlockSpec(w_qkv.shape, whole),
            pl.BlockSpec(w_out.shape, whole),
        ],
        out_specs=[
            pl.BlockSpec((HEADS, BLOCK, HEAD), lambda i: (0, i, 0)),
            pl.BlockSpec((KV_HEADS, BLOCK, HEAD), lambda i: (0, i, 0)),
            pl.BlockSpec((KV_HEADS, BLOCK, HEAD), lambda i: (0, i, 0)),
            pl.BlockSpec((16, BLOCK), lambda i: (0, i)),
            pl.BlockSpec((BLOCK, width), rows),
            pl.BlockSpec((BLOCK, width), rows),
        ],
        out_shape=[
            jax.ShapeDtypeStruct((HEADS, tokens, HEAD), BF16),
            jax.ShapeDtypeStruct((KV_HEADS, tokens, HEAD), BF16),
            jax.ShapeDtypeStruct((KV_HEADS, tokens, HEAD), BF16),
            jax.ShapeDtypeStruct((16, tokens), F32),
            jax.ShapeDtypeStruct((tokens, width), BF16),
            jax.ShapeDtypeStruct((tokens, width), F32),
        ],
        scratch_shapes=[
            pltpu.VMEM((KV_HEADS, tokens, HEAD), BF16),
            pltpu.VMEM((KV_HEADS, blocks, HEAD, BLOCK), BF16),
            pltpu.VMEM((KV_HEADS, HEAD, GROUP * BLOCK), F32),
            pltpu.VMEM((8, GROUP * BLOCK), F32),
            pltpu.VMEM((8, GROUP * BLOCK), F32),
        ],
        cost_estimate=pl.CostEstimate(flops=6 * 10**9, bytes_accessed=12 * 10**6, transcendentals=6 * 10**6),
        name="front",
    )(inputs, start, cosine, sine, norm_one, w_qkv, w_out)


def mlp_kernel(
    place_ref, mid_ref, og_ref, att_ref, norm_ref, w_out_ref, own_ref, side_ref, row_ref, far_ref, sel_ref,
    out_ref, mg_ref, do_ref, delta_ref, g3_ref, gout_ref, gain_ref,
    weights, acc3, acc_out, acc_gain,
):
    i = pl.program_id(0)
    rows_half, cols_half = own_ref.shape[1], own_ref.shape[2]
    col, row = place_ref[0], place_ref[1]

    @pl.when(i == 0)
    def _():
        for ref, c, r in ((own_ref, col, row), (side_ref, 1 - col, row), (row_ref, col, 1 - row), (far_ref, 1 - col, 1 - row)):
            at_row = pl.multiple_of(c * rows_half, 32)
            at_col = pl.multiple_of(r * cols_half, LANES)
            for t in range(3):
                weights[t, pl.ds(at_row, rows_half), pl.ds(at_col, cols_half)] = ref[t]
        acc3[...] = jnp.zeros(acc3.shape, F32)
        acc_out[...] = jnp.zeros(acc_out.shape, F32)
        acc_gain[...] = jnp.zeros(acc_gain.shape, F32)

    middle = mid_ref[...]
    og = og_ref[...]
    gain = norm_ref[...]
    scale = lax.rsqrt(jnp.mean(middle * middle, axis=-1, keepdims=True) + EPS)
    normed = (middle * scale * gain).astype(BF16)
    og_t = og.astype(F32).T.astype(BF16)
    normed_t = normed.astype(F32).T.astype(BF16)
    chunk = cols_half // 2
    mlp_out = jnp.zeros(middle.shape, F32)
    normed_grad = jnp.zeros(middle.shape, F32)
    for c in range(2 * cols_half // chunk):
        at = slice(c * chunk, (c + 1) * chunk)
        gate_pre = dot_nn(normed, weights[0, :, at])
        up_pre = dot_nn(normed, weights[1, :, at])
        hidden_low = dot_nn(og, weights[2, :, at]).astype(BF16).astype(F32)
        squashed = 1.0 / (1.0 + jnp.exp(-gate_pre))
        active = gate_pre * squashed
        hidden = (active * up_pre).astype(BF16)
        gate_low = (hidden_low * up_pre * squashed * (1.0 + gate_pre * (1.0 - squashed))).astype(BF16)
        up_low = (hidden_low * active).astype(BF16)
        mlp_out += dot_nt(hidden, weights[2, :, at])
        normed_grad += dot_nt(gate_low, weights[0, :, at]) + dot_nt(up_low, weights[1, :, at])
        acc3[0, :, at] += dot_nn(normed_t, gate_low)
        acc3[1, :, at] += dot_nn(normed_t, up_low)
        acc3[2, :, at] += dot_nn(og_t, hidden)
    out_ref[...] = (middle + mlp_out).astype(BF16)
    acc_gain[...] += jnp.sum((normed_grad * middle * scale).reshape(BLOCK // 8, 8, middle.shape[1]), axis=0)
    weighted = normed_grad * gain
    inner = jnp.sum(weighted * middle, axis=-1, keepdims=True)
    middle_grad = (
        og.astype(F32) + scale * weighted
        - middle * (scale * scale * scale) * inner / middle.shape[1]
    )
    mg_ref[...] = middle_grad
    middle_low = middle_grad.astype(BF16)
    attended = att_ref[...]
    acc_out[...] += dot_tn(attended, middle_low)
    att_low = dot_nt(middle_low, w_out_ref[...]).astype(BF16)
    for h in range(HEADS):
        do_ref[h] = att_low[:, h * HEAD:(h + 1) * HEAD]
    product = att_low.astype(F32) * attended.astype(F32)
    coarse = product.astype(BF16)
    fine = (product - coarse.astype(F32)).astype(BF16)
    delta_ref[...] = dot_nt(sel_ref[...], coarse) + dot_nt(sel_ref[...], fine)

    @pl.when(i == pl.num_programs(0) - 1)
    def _():
        for r in range(2):
            for c in range(2):
                for t in range(3):
                    for part in range(cols_half // LANES):
                        lane = r * cols_half + part * LANES
                        g3_ref[r, c, t, part] = acc3[t, c * rows_half:(c + 1) * rows_half, lane:lane + LANES].astype(BF16)
        gout_ref[...] = acc_out[...].astype(BF16)
        gain_ref[...] = acc_gain[...]


def mlp(place, middle, out_grad, attended, norm_two, w_out, own, side, across, far, selector):
    tokens, width = middle.shape
    rows_half, cols_half = own.shape[1:]
    blocks = tokens // BLOCK
    parts = cols_half // LANES
    rows = lambda i: (i, 0)
    whole = lambda i: (0, 0)
    whole3 = lambda i: (0, 0, 0)
    once = pl.Buffered(1)
    return pl.pallas_call(
        mlp_kernel,
        grid=(blocks,),
        in_specs=[
            pl.BlockSpec(memory_space=pltpu.SMEM),
            pl.BlockSpec((BLOCK, width), rows),
            pl.BlockSpec((BLOCK, width), rows),
            pl.BlockSpec((BLOCK, width), rows),
            pl.BlockSpec((1, width), whole),
            pl.BlockSpec(w_out.shape, whole, pipeline_mode=once),
            pl.BlockSpec(own.shape, whole3, pipeline_mode=once),
            pl.BlockSpec(own.shape, whole3, pipeline_mode=once),
            pl.BlockSpec(own.shape, whole3, pipeline_mode=once),
            pl.BlockSpec(own.shape, whole3, pipeline_mode=once),
            pl.BlockSpec(selector.shape, whole),
        ],
        out_specs=[
            pl.BlockSpec((BLOCK, width), rows),
            pl.BlockSpec((BLOCK, width), rows),
            pl.BlockSpec((HEADS, BLOCK, HEAD), lambda i: (0, i, 0)),
            pl.BlockSpec((16, BLOCK), lambda i: (0, i)),
            pl.BlockSpec((2, 2, 3, parts, rows_half, LANES), lambda i: (0,) * 6, pipeline_mode=once),
            pl.BlockSpec(w_out.shape, whole, pipeline_mode=once),
            pl.BlockSpec((8, width), whole),
        ],
        out_shape=[
            jax.ShapeDtypeStruct((tokens, width), BF16),
            jax.ShapeDtypeStruct((tokens, width), F32),
            jax.ShapeDtypeStruct((HEADS, tokens, HEAD), BF16),
            jax.ShapeDtypeStruct((16, tokens), F32),
            jax.ShapeDtypeStruct((2, 2, 3, parts, rows_half, LANES), BF16),
            jax.ShapeDtypeStruct(w_out.shape, BF16),
            jax.ShapeDtypeStruct((8, width), F32),
        ],
        scratch_shapes=[
            pltpu.VMEM((3, 2 * rows_half, 2 * cols_half), BF16),
            pltpu.VMEM((3, 2 * rows_half, 2 * cols_half), F32),
            pltpu.VMEM(w_out.shape, F32),
            pltpu.VMEM((8, width), F32),
        ],
        cost_estimate=pl.CostEstimate(flops=18 * 10**9, bytes_accessed=24 * 10**6, transcendentals=2 * 10**6),
        name="mlp",
    )(place, middle, out_grad, attended, norm_two, w_out, own, side, across, far, selector)


def back_kernel(
    q_ref, k_ref, v_ref, do_ref, lse_ref, delta_ref, start_ref, cos_ref, sin_ref,
    inputs_ref, mg_ref, norm_ref, w_qkv_ref,
    ig_ref, gqkv_ref, gain_ref,
    dq_all, dk, dv, acc_qkv, acc_gain,
):
    j = pl.program_id(0)
    blocks = pl.num_programs(0)

    @pl.when(j == 0)
    def _():
        dq_all[...] = jnp.zeros(dq_all.shape, F32)
        acc_qkv[...] = jnp.zeros(acc_qkv.shape, F32)
        acc_gain[...] = jnp.zeros(acc_gain.shape, F32)

    dk[...] = jnp.zeros(dk.shape, F32)
    dv[...] = jnp.zeros(dv.shape, F32)
    keys_t = [k_ref[g].astype(F32).T.astype(BF16) for g in range(KV_HEADS)]

    def tile(i, diagonal):
        at = pl.multiple_of(i * BLOCK, BLOCK)
        span = pl.ds(at, BLOCK)
        start_row = jnp.concatenate([start_ref[:, span]] * GROUP, axis=1)
        mask = allowed_tile(start_row, j * BLOCK, i * BLOCK, diagonal)
        for g in range(KV_HEADS):
            heads = range(g * GROUP, (g + 1) * GROUP)
            queries = q_ref[g * GROUP:(g + 1) * GROUP, span, :].reshape(GROUP * BLOCK, HEAD)
            grads = do_ref[g * GROUP:(g + 1) * GROUP, span, :].reshape(GROUP * BLOCK, HEAD)
            lse_row = jnp.concatenate([lse_ref[h:h + 1, span] for h in heads], axis=1)
            delta_row = jnp.concatenate([delta_ref[h:h + 1, span] for h in heads], axis=1)
            keys, values = k_ref[g], v_ref[g]
            soft = jnp.where(mask, jnp.exp2(dot_nt(keys, queries) * LOG2E - lse_row), 0.0)
            prob_grad = dot_nt(values, grads)
            score_low = (soft * (prob_grad - delta_row)).astype(BF16)
            dv[g] += dot_nn(soft.astype(BF16), grads)
            dk[g] += dot_nn(score_low, queries)
            dq_all[i, g] += dot_nn(keys_t[g], score_low)

    def step(i, carry):
        tile(i, False)
        return carry

    tile(j, True)
    lax.fori_loop(j + 1, blocks, step, 0)

    cosine, sine = cos_ref[...], sin_ref[...]
    pieces = []
    for g in range(KV_HEADS):
        part = dq_all[j, g] * (HEAD ** -0.5)
        pieces += [part[:, h * BLOCK:(h + 1) * BLOCK] for h in range(GROUP)]
    query_grad = jnp.concatenate(pieces, axis=0).T
    turned = jnp.concatenate([query_grad, dk[0], dk[1], dk[2]], axis=1)
    columns = []
    for c in range(turned.shape[1] // LANES):
        part = turned[:, c * LANES:(c + 1) * LANES]
        columns.append((part * cosine - partner_lanes(part) * sine).astype(BF16))
    values_low = jnp.concatenate([dv[0], dv[1], dv[2]], axis=1).astype(BF16)
    joined_low = jnp.concatenate(columns + [values_low], axis=1)

    x = inputs_ref[...].astype(F32)
    gain = norm_ref[...]
    scale = lax.rsqrt(jnp.mean(x * x, axis=-1, keepdims=True) + EPS)
    normed = (x * scale * gain).astype(BF16)
    acc_qkv[...] += dot_tn(normed, joined_low)
    normed_grad = dot_nt(joined_low, w_qkv_ref[...])
    acc_gain[...] += jnp.sum((normed_grad * x * scale).reshape(BLOCK // 8, 8, x.shape[1]), axis=0)
    weighted = normed_grad * gain
    inner = jnp.sum(weighted * x, axis=-1, keepdims=True)
    ig_ref[...] = mg_ref[...] + scale * weighted - x * (scale * scale * scale) * inner / x.shape[1]

    @pl.when(j == blocks - 1)
    def _():
        gqkv_ref[...] = acc_qkv[...].astype(BF16)
        gain_ref[...] = acc_gain[...]


def back(q, k, v, do, lse, delta, start, cosine, sine, inputs, middle_grad, norm_one, w_qkv):
    tokens, width = inputs.shape
    blocks = tokens // BLOCK
    rows = lambda j: (j, 0)
    whole = lambda j: (0, 0)
    whole3 = lambda j: (0, 0, 0)
    mine3 = lambda j: (0, j, 0)
    return pl.pallas_call(
        back_kernel,
        grid=(blocks,),
        in_specs=[
            pl.BlockSpec(q.shape, whole3),
            pl.BlockSpec((KV_HEADS, BLOCK, HEAD), mine3),
            pl.BlockSpec((KV_HEADS, BLOCK, HEAD), mine3),
            pl.BlockSpec(do.shape, whole3),
            pl.BlockSpec(lse.shape, whole),
            pl.BlockSpec(delta.shape, whole),
            pl.BlockSpec(start.shape, whole),
            pl.BlockSpec((BLOCK, LANES), rows),
            pl.BlockSpec((BLOCK, LANES), rows),
            pl.BlockSpec((BLOCK, width), rows),
            pl.BlockSpec((BLOCK, width), rows),
            pl.BlockSpec((1, width), whole),
            pl.BlockSpec(w_qkv.shape, whole),
        ],
        out_specs=[
            pl.BlockSpec((BLOCK, width), rows),
            pl.BlockSpec(w_qkv.shape, whole),
            pl.BlockSpec((8, width), whole),
        ],
        out_shape=[
            jax.ShapeDtypeStruct((tokens, width), F32),
            jax.ShapeDtypeStruct(w_qkv.shape, BF16),
            jax.ShapeDtypeStruct((8, width), F32),
        ],
        scratch_shapes=[
            pltpu.VMEM((blocks, KV_HEADS, HEAD, GROUP * BLOCK), F32),
            pltpu.VMEM((KV_HEADS, BLOCK, HEAD), F32),
            pltpu.VMEM((KV_HEADS, BLOCK, HEAD), F32),
            pltpu.VMEM(w_qkv.shape, F32),
            pltpu.VMEM((8, width), F32),
        ],
        cost_estimate=pl.CostEstimate(flops=8 * 10**9, bytes_accessed=16 * 10**6, transcendentals=6 * 10**6),
        name="back",
    )(q, k, v, do, lse, delta, start, cosine, sine, inputs, middle_grad, norm_one, w_qkv)


def places(seq_ids):
    position = jnp.arange(seq_ids.shape[0], dtype=jnp.int32)
    previous = jnp.concatenate([seq_ids[:1] - 1, seq_ids[:-1]])
    start = lax.cummax(jnp.where(seq_ids != previous, position, 0), axis=0)
    return start, (position - start).astype(F32)


def tables(place):
    half = HEAD // 2
    frequency = THETA ** (-2.0 * jnp.arange(half, dtype=F32) / HEAD)
    angles = frequency[:, None] * place[None, :]
    cosine, sine = jnp.cos(angles).T, jnp.sin(angles).T
    copies = LANES // HEAD
    return (
        jnp.concatenate([cosine, cosine] * copies, axis=1),
        jnp.concatenate([-sine, sine] * copies, axis=1),
    )


SWAP = [(0, 1), (1, 0)]


def halve(data, axis, bit, size):
    pairs = [(n, n ^ bit) for n in range(size)]
    mine = (lax.axis_index(axis) // bit) % 2
    halves = data.reshape((2, data.shape[0] // 2) + data.shape[1:])
    sent = lax.dynamic_index_in_dim(halves, 1 - mine, 0, keepdims=False)
    kept = lax.dynamic_index_in_dim(halves, mine, 0, keepdims=False)
    arrived = lax.ppermute(sent, axis, pairs)
    return (kept.astype(F32) + arrived.astype(F32)).astype(BF16)


def double(data, axis, bit, size):
    pairs = [(n, n ^ bit) for n in range(size)]
    mine = (lax.axis_index(axis) // bit) % 2
    arrived = lax.ppermute(data, axis, pairs)
    lower = mine == 0
    return jnp.concatenate([jnp.where(lower, data, arrived), jnp.where(lower, arrived, data)], axis=0)


def bits(size):
    out, bit = [], 1
    while bit < size:
        out.append(bit)
        bit *= 2
    return out


def per_device(inputs, seq_ids, norm_one, w_qkv, w_out, norm_two, w_gate, w_up, w_down, out_grad):
    dp_size, row_size, col_size = (lax.axis_size(name) for name in ("dp", "row", "col"))
    width = inputs.shape[1]
    own = jnp.stack([w_gate, w_up, w_down.T])
    side = lax.ppermute(own, "col", SWAP)
    across = lax.ppermute(own, "row", SWAP)
    far = lax.ppermute(side, "row", SWAP)
    start, place = places(seq_ids)
    start = start[None, :]
    cosine, sine = tables(place)
    gain_one, gain_two = norm_one[None, :], norm_two[None, :]
    q, k, v, lse, attended, middle = front(inputs, start, cosine, sine, gain_one, w_qkv, w_out)
    selector = (jnp.arange(16)[:, None] == jnp.arange(width)[None, :] // HEAD).astype(BF16)
    spot = jnp.stack([lax.axis_index("col"), lax.axis_index("row")]).astype(jnp.int32)
    outputs, middle_grad, do, delta, grads, gout, gain_two_part = mlp(
        spot, middle, out_grad, attended, gain_two, w_out, own, side, across, far, selector
    )
    grads = grads.reshape(-1, LANES)
    grads = halve(grads, "row", 1, row_size)
    grads = halve(grads, "col", 1, col_size)
    for bit in bits(dp_size):
        grads = halve(grads, "dp", bit, dp_size)
    for bit in reversed(bits(dp_size)):
        grads = double(grads, "dp", bit, dp_size)
    input_grad, gqkv, gain_one_part = back(
        q, k, v, do, lse, delta, start, cosine, sine, inputs, middle_grad, gain_one, w_qkv
    )
    gains = lax.psum((jnp.sum(gain_one_part, axis=0), jnp.sum(gain_two_part, axis=0)), ("dp", "row", "col"))
    shared = jnp.concatenate([gqkv.reshape(-1, LANES), gout.reshape(-1, LANES)], axis=0)
    extra = -shared.shape[0] % (8 * dp_size * row_size * col_size)
    rows_shared = shared.shape[0]
    shared = jnp.pad(shared, ((0, extra), (0, 0)))
    shared = halve(shared, "row", 1, row_size)
    shared = halve(shared, "col", 1, col_size)
    for bit in bits(dp_size):
        shared = halve(shared, "dp", bit, dp_size)
    for bit in reversed(bits(dp_size)):
        shared = double(shared, "dp", bit, dp_size)
    shared = double(shared, "col", 1, col_size)
    shared = double(shared, "row", 1, row_size)
    cut = gqkv.size // LANES
    grad_qkv = shared[:cut].reshape(gqkv.shape).astype(F32)
    grad_out = shared[cut:rows_shared].reshape(gout.shape).astype(F32)
    parts = w_gate.shape[1] // LANES
    grads = grads.reshape(3, parts, w_gate.shape[0], LANES).astype(F32)
    grad_gate = grads[0].transpose(1, 0, 2).reshape(w_gate.shape)
    grad_up = grads[1].transpose(1, 0, 2).reshape(w_up.shape)
    grad_down = grads[2].transpose(0, 2, 1).reshape(w_down.shape)
    return (outputs, input_grad, gains[0], grad_qkv, grad_out, gains[1], grad_gate, grad_up, grad_down)


def solution(mesh):
    tokens = P(("dp", "row", "col"), None)
    grid, turned = P("col", "row"), P("row", "col")
    return jax.shard_map(
        per_device,
        mesh=mesh,
        in_specs=(tokens, P(("dp", "row", "col")), P(), P(), P(), P(), grid, grid, turned, tokens),
        out_specs=(tokens, tokens, P(), P(), P(), P(), grid, grid, turned),
        check_vma=False,
    )
```

time: 1080 us -> 341 us (0.32); the launches traced: 1070 us -> 340 us
  waiting for transfers between devices: 536 us -> 113 us
  matrix products: 282 us -> 0 us
  Pallas kernels: 0 us -> 102 us
  local copies, waits for them, and re-layouts: 90.2 us -> 28.8 us
  blocking collectives: 75.7 us -> 41.5 us
  other arithmetic: 56.4 us -> 24.5 us
  starting transfers between devices: 8.08 us -> 29.7 us
  between operations: 15.5 us -> 1.63 us
    dot_general x26 -> x0, matrix products: 282 us -> none  [the longest x2 86.8 us: one_block(): jnp.einsum('gjqk,qgjd->kgd', score_low, query_rows, preferred_element_typ...]
    all_gather x4 -> x0, waiting for transfers between devices: 222 us -> none  [the longest x1 147 us: per_device(): pair_all = lax.all_gather(pair_grad, 'col', axis=0, tiled=True)]
    reduce_scatter x4 -> x0, waiting for transfers between devices: 211 us -> none  [the longest x1 138 us: per_device(): lax.psum_scatter(jnp.dot(spread, w_pair, preferred_element_type=jnp.float...]
    ppermute x0 -> x21, waiting for transfers between devices: none -> 113 us  [the longest x10 54 us: halve(): arrived = lax.ppermute(sent, axis, pairs)]
    pallas_call x0 -> x3, Pallas kernels: none -> 102 us  [the longest x1 40.7 us: mlp(): pl.pallas_call(mlp_kernel, grid=(blocks,), in_specs=[pl.BlockSpec(memory_...]
    psum x2 -> x0, waiting for transfers between devices: 92.1 us -> none  [the longest x1 92.1 us: per_device(): lax.psum((qkv_grad, out_weight_grad, gain_one_grad, gain_two_grad), ('dp'...]
    dynamic_update_slice x6 -> x0, local copies, waits for them, and re-layouts: 50.5 us -> none  [the longest x4 48.8 us: attend_backward(): lax.scan(one_block, (zeros_kv, zeros_kv), (block_ids, logsums))]
    all_to_all x2 -> x0, blocking collectives: 35.7 us -> none  [the longest x1 19.1 us: per_device(): lax.all_to_all(normed_two, 'col', split_axis=1, concat_axis=0, tiled=True)]
  transfers between devices with their start and end apart: 12 -> 21, of which waited for: 9 -> 14; matrix products, arithmetic and copies ran while one was open for 33% -> 11% of each run, Pallas kernels for 0% -> 8%
where the time goes in v1:
time: 341 us; the launch traced here: 340 us
  waiting for transfers between devices  113 us (33%)
  Pallas kernels  102 us (30%)
  blocking collectives  41.5 us (12%)
  starting transfers between devices  29.7 us (9%)
  local copies, waits for them, and re-layouts  28.8 us (8%)
  other arithmetic  24.5 us (7%)
    ppermute x10, waiting for transfers between devices, halve(): arrived = lax.ppermute(sent, axis, pairs)  54 us
    psum x1, blocking collectives, per_device(): lax.psum((jnp.sum(gain_one_part, axis=0), jnp.sum(gain_two_part, axis=0))...  41.5 us
    pallas_call x1, Pallas kernels, mlp(): pl.pallas_call(mlp_kernel, grid=(blocks,), in_specs=[pl.BlockSpec(memory_...  40.7 us
    pallas_call x1, Pallas kernels, back(): pl.pallas_call(back_kernel, grid=(blocks,), in_specs=[pl.BlockSpec(q.shap...  32 us
    ppermute x8, waiting for transfers between devices, double(): arrived = lax.ppermute(data, axis, pairs)  31.7 us
    pallas_call x1, Pallas kernels, front(): pl.pallas_call(front_kernel, grid=(blocks,), in_specs=[pl.BlockSpec((BLOC...  28.8 us
    ppermute x1, waiting for transfers between devices, per_device(): side = lax.ppermute(own, 'col', SWAP)  26.8 us
    ppermute x10, starting transfers between devices, halve(): arrived = lax.ppermute(sent, axis, pairs)  14.3 us
  transfers between devices with their start and end apart: 21, of which 14 were waited for; matrix products, arithmetic and copies ran while one was open for 11% of the time, Pallas kernels for 8%

profile of v1, /device:TPU:0, one launch (start us, length us, event | category | flops | bytes accessed | tf_op | source)
XLA Modules:
  0.0 340.3 jit_solution(16126995419977623371)
XLA Ops:
  2.2 3.1 collective-permute-start
  7.7 26.8 %collective-permute-done.side_ref = bf16[3,288,768]{2,1,0:T(8,128)(2,1)} collective-permute-done((bf16[3,288,768]{2,1,0:T(8,128)(2,1)S(1)}, bf16[3,288,768]{2,1,0:T(8,128)(2,1)}, u32[]{:S(2)}, u32[]{:S(2)}) %collective-permute-start) | collective-permute-done | bytes 1327136 | tf_op jit(solution)/shard_map/ppermute | solution.py:473
  44.6 28.8 %front.1 = (bf16[9,1024,64]{2,1,0:T(8,128)(2,1)}, bf16[3,1024,64]{2,1,0:T(8,128)(2,1)}, bf16[3,1024,64]{2,1,0:T(8,128)(2,1)}, f32[16,1024]{1,0:T(8,128)}, bf16[1...) custom-call(bf16[1024,576]{1,0:T(8,128)(2,1)} %copy.33.inputs_ref, s32[1,1024]{1,0:T(1,128)} %bitcast.124, ...), custom_call_target="tpu_custom_call" | custom-call | flops 6000000000 | bytes 12000000 | tf_op jit(solution)/shard_map/front/pallas_call | solution.py:127
  73.4 40.7 %mlp.1 = (bf16[1024,576]{1,0:T(8,128)(2,1)}, f32[1024,576]{1,0:T(8,128)}, bf16[9,1024,64]{2,1,0:T(8,128)(2,1)}, f32[16,1024]{1,0:T(8,128)}, bf16[2,2,3,6,288,128...) custom-call(s32[2]{0:T(128)} %pad_add_fusion.place_ref, f32[1024,576]{1,0:T(8,128)} %get-tuple-element.25.mid_ref, ...), custom_call_target="tpu_custom_call" | custom-call | flops 17999998976 | bytes 24000000 | tf_op jit(solution)/shard_map/mlp/pallas_call | solution.py:253
  116.1 32.0 %back.1 = (f32[1024,576]{1,0:T(8,128)}, bf16[576,960]{1,0:T(8,128)(2,1)}, f32[8,576]{1,0:T(8,128)}) custom-call(bf16[9,1024,64]{2,1,0:T(8,128)(2,1)} %get-tuple-element.28.q_ref, bf16[3,1024,64]{2,1,0:T(8,128)(2,1)} %get-tuple-element.29.k_ref, bf16[3,1024,64]{2,1,0:T(8,128)(2,1)} %get-tuple-element.30.v_ref, bf16[9,1024,64]{2,1,0:T(8,128)(2,1)} %get-tuple-element.31.do_ref, ...), custom_call_target="tpu_custom_call" | custom-call | flops 8000000000 | bytes 16000000 | tf_op jit(solution)/shard_map/back/pallas_call | solution.py:381
  148.1 2.7 reshape.184
  156.4 11.0 %collective-permute-done.4 = bf16[1728,128]{1,0:T(8,128)(2,1)} collective-permute-done((bf16[1728,128]{1,0:T(8,128)(2,1)}, bf16[1728,128]{1,0:T(8,128)(2,1)}, u32[]{:S(2)}, u32[]{:S(2)}) %collective-permute-start.4) | collective-permute-done | bytes 442400 | tf_op jit(solution)/shard_map/ppermute | solution.py:449
  172.1 5.1 %collective-permute-done.5 = bf16[864,128]{1,0:T(8,128)(2,1)S(1)} collective-permute-done((bf16[864,128]{1,0:T(8,128)(2,1)S(1)}, bf16[864,128]{1,0:T(8,128)(2,1)S(1)}, u32[]{:S(2)}, u32[]{:S(2)}) %collective-permute-start.5) | collective-permute-done | bytes 221216 | tf_op jit(solution)/shard_map/ppermute | solution.py:449
  180.1 3.0 collective-permute-done.6
  183.1 2.9 collective-permute-start.7
  188.3 2.9 collective-permute-start.8
  191.2 2.9 fusion
  196.8 3.2 collective-permute-start.9
  200.0 2.7 collective-permute-done.9
  204.3 4.4 %collective-permute-done.10 = bf16[864,128]{1,0:T(8,128)(2,1)S(1)} collective-permute-done((bf16[864,128]{1,0:T(8,128)(2,1)S(1)}, bf16[864,128]{1,0:T(8,128)(2,1)S(1)}, u32[]{:S(2)}, u32[]{:S(2)}) %collective-permute-start.10) | collective-permute-done | bytes 221216 | tf_op jit(solution)/shard_map/ppermute | solution.py:456
  209.5 17.9 %collective-permute-done.14 = bf16[5184,128]{1,0:T(8,128)(2,1)} collective-permute-done((bf16[5184,128]{1,0:T(8,128)(2,1)}, bf16[5184,128]{1,0:T(8,128)(2,1)}, u32[]{:S(2)}, u32[]{:S(2)}) %collective-permute-start.14) | collective-permute-done | bytes 1327136 | tf_op jit(solution)/shard_map/ppermute | solution.py:449
  233.7 8.3 %collective-permute-done.15 = bf16[2592,128]{1,0:T(8,128)(2,1)} collective-permute-done((bf16[2592,128]{1,0:T(8,128)(2,1)}, bf16[2592,128]{1,0:T(8,128)(2,1)}, u32[]{:S(2)}, u32[]{:S(2)}) %collective-permute-start.15) | collective-permute-done | bytes 663584 | tf_op jit(solution)/shard_map/ppermute | solution.py:449
  245.6 6.3 %collective-permute-done.16 = bf16[1296,128]{1,0:T(8,128)(2,1)S(1)} collective-permute-done((bf16[1296,128]{1,0:T(8,128)(2,1)S(1)}, bf16[1296,128]{1,0:T(8,128)(2,1)S(1)}, u32[]{:S(2)}, u32[]{:S(2)}) %collective-permute-start.16) | collective-permute-done | bytes 331808 | tf_op jit(solution)/shard_map/ppermute | solution.py:449
  254.4 3.1 copy.40
  257.5 41.5 %all-reduce = (f32[576]{0:T(1024)}, f32[576]{0:T(1024)}) all-reduce(f32[576]{0:T(1024)S(1)} %reduce_sum.18, f32[576]{0:T(1024)S(1)} %reduce_sum.19), channel_id=1, replica_groups=mesh['dp'=8,'row'=2,'col'=2] {'dp','row','col'}, use_global_device_ids=true, to_apply=%region_3.4 | all-reduce | flops 1152 | bytes 9216 | tf_op jit(solution)/shard_map/psum | solution.py:496
  300.0 2.7 collective-permute-start.18
  304.2 5.8 %collective-permute-done.18 = bf16[648,128]{1,0:T(8,128)(2,1)S(1)} collective-permute-done((bf16[648,128]{1,0:T(8,128)(2,1)S(1)}, bf16[648,128]{1,0:T(8,128)(2,1)S(1)}, u32[]{:S(2)}, u32[]{:S(2)}) %collective-permute-start.18) | collective-permute-done | bytes 165920 | tf_op jit(solution)/shard_map/ppermute | solution.py:456
  312.7 6.9 %collective-permute-done.19 = bf16[1296,128]{1,0:T(8,128)(2,1)} collective-permute-done((bf16[1296,128]{1,0:T(8,128)(2,1)}, bf16[1296,128]{1,0:T(8,128)(2,1)}, u32[]{:S(2)}, u32[]{:S(2)}) %collective-permute-start.19) | collective-permute-done | bytes 331808 | tf_op jit(solution)/shard_map/ppermute | solution.py:456
  323.8 11.9 %collective-permute-done.20 = bf16[2592,128]{1,0:T(8,128)(2,1)} collective-permute-done((bf16[2592,128]{1,0:T(8,128)(2,1)S(1)}, bf16[2592,128]{1,0:T(8,128)(2,1)}, u32[]{:S(2)}, u32[]{:S(2)}) %collective-permute-start.20) | collective-permute-done | bytes 663584 | tf_op jit(solution)/shard_map/ppermute | solution.py:456
  (110 shorter events, 62.0 us)
Async XLA Ops:
  0.7 34.5 %copy-start.4 = (bf16[1024,576]{0,1:T(8,128)(2,1)S(1)}, bf16[1024,576]{0,1:T(8,128)(2,1)}, u32[]{:S(2)}) copy-start(bf16[1024,576]{0,1:T(8,128)(2,1)} %param.10) | copy-start | bytes 3538948
  2.2 37.4 %copy-start.2 = (bf16[3,288,768]{2,1,0:T(8,128)(2,1)}, bf16[3,288,768]{2,1,0:T(8,128)(2,1)S(1)}, u32[]{:S(2)}) copy-start(bf16[3,288,768]{2,1,0:T(8,128)(2,1)S(1)} %pad_maximum_fusion.1.own_ref) | copy-start | bytes 3981316
  2.2 34.4 %copy-start.8 = (f32[576]{0:T(1024)S(1)}, f32[576]{0:T(1024)}, u32[]{:S(2)}) copy-start(f32[576]{0:T(1024)} %param.12) | copy-start | bytes 6916
  2.2 32.3 %collective-permute-start = (bf16[3,288,768]{2,1,0:T(8,128)(2,1)S(1)}, bf16[3,288,768]{2,1,0:T(8,128)(2,1)}, u32[]{:S(2)}, u32[]{:S(2)}) collective-permute-start(bf16[3,288,768]{2,1,0:T(8,128)(2,1)S(1)} %pad_maximum_fusion.1.own_ref), channel_id=1, source_target_pairs={{0,1},{1,0},{2,3},{3,2},{4,5},{5,4},{6,7},{7,6},{8,9},{9,8},{10,11... | collective-permute-start | bytes 3981320 | tf_op jit(solution)/shard_map/ppermute | solution.py:473
  5.3 68.1 %collective-permute-start.1 = (bf16[3,288,768]{2,1,0:T(8,128)(2,1)S(1)}, bf16[3,288,768]{2,1,0:T(8,128)(2,1)}, u32[]{:S(2)}, u32[]{:S(2)}) collective-permute-start(bf16[3,288,768]{2,1,0:T(8,128)(2,1)S(1)} %pad_maximum_fusion.1.own_ref), channel_id=1, source_target_pairs={{0,2},{2,0},{1,3},{3,1},{4,6},{6,4},{5,7},{7,5},{8,10},{10,8},{9,1... | collective-permute-start | bytes 3981320 | tf_op jit(solution)/shard_map/ppermute | solution.py:474
  34.5 38.9 %collective-permute-start.2 = (bf16[3,288,768]{2,1,0:T(8,128)(2,1)}, bf16[3,288,768]{2,1,0:T(8,128)(2,1)}, u32[]{:S(2)}, u32[]{:S(2)}) collective-permute-start(bf16[3,288,768]{2,1,0:T(8,128)(2,1)} %collective-permute-done.side_ref), channel_id=1, source_target_pairs={{0,2},{2,0},{1,3},{3,1},{4,6},{6,4},{5,7},{7,5},{8,10},{10,8},{9,1... | collective-permute-start | bytes 3981320 | tf_op jit(solution)/shard_map/ppermute | solution.py:475
  151.0 2.6 collective-permute-start.3
  153.4 37.8 %collective-permute-start.13 = (bf16[10368,128]{1,0:T(8,128)(2,1)S(1)}, bf16[10368,128]{1,0:T(8,128)(2,1)}, u32[]{:S(2)}, u32[]{:S(2)}) collective-permute-start(bf16[10368,128]{1,0:T(8,128)(2,1)S(1)} %dynamic-slice_bitcast_fusion), channel_id=1, source_target_pairs={{0,2},{2,0},{1,3},{3,1},{4,6},{6,4},{5,7},{7,5},{8,10},{10,8},{9,1... | collective-permute-start | bytes 7962632 | tf_op jit(solution)/shard_map/ppermute | solution.py:449
  154.7 12.8 %collective-permute-start.4 = (bf16[1728,128]{1,0:T(8,128)(2,1)}, bf16[1728,128]{1,0:T(8,128)(2,1)}, u32[]{:S(2)}, u32[]{:S(2)}) collective-permute-start(bf16[1728,128]{1,0:T(8,128)(2,1)} %dynamic-slice_bitcast_fusion.4), channel_id=1, source_target_pairs={{0,1},{1,0},{2,3},{3,2},{4,5},{5,4},{6,7},{7,6},{8,9},{9,8},{10,11... | collective-permute-start | bytes 1327112 | tf_op jit(solution)/shard_map/ppermute | solution.py:449
  170.3 6.9 %collective-permute-start.5 = (bf16[864,128]{1,0:T(8,128)(2,1)S(1)}, bf16[864,128]{1,0:T(8,128)(2,1)S(1)}, u32[]{:S(2)}, u32[]{:S(2)}) collective-permute-start(bf16[864,128]{1,0:T(8,128)(2,1)S(1)} %dynamic-slice_bitcast_fusion.6), channel_id=1, source_target_pairs={{0,4},{4,0},{8,12},{12,8},{16,20},{20,16},{24,28},{28,24},{1,5},{5... | collective-permute-start | bytes 663560 | tf_op jit(solution)/shard_map/ppermute | solution.py:449
  178.3 4.8 %collective-permute-start.6 = (bf16[432,128]{1,0:T(8,128)(2,1)S(1)}, bf16[432,128]{1,0:T(8,128)(2,1)S(1)}, u32[]{:S(2)}, u32[]{:S(2)}) collective-permute-start(bf16[432,128]{1,0:T(8,128)(2,1)S(1)} %dynamic-slice_bitcast_fusion.8), channel_id=1, source_target_pairs={{0,8},{4,12},{8,0},{12,4},{16,24},{20,28},{24,16},{28,20},{1,9},{5... | collective-permute-start | bytes 331784 | tf_op jit(solution)/shard_map/ppermute | solution.py:449
  183.1 5.1 %collective-permute-start.7 = (bf16[216,128]{1,0:T(8,128)(2,1)S(1)}, bf16[216,128]{1,0:T(8,128)(2,1)S(1)}, u32[]{:S(2)}, u32[]{:S(2)}) collective-permute-start(bf16[216,128]{1,0:T(8,128)(2,1)S(1)} %dynamic-slice_bitcast_fusion.9), channel_id=1, source_target_pairs={{0,16},{4,20},{8,24},{12,28},{16,0},{20,4},{24,8},{28,12},{1,17},{... | collective-permute-start | bytes 165896 | tf_op jit(solution)/shard_map/ppermute | solution.py:449
  188.3 8.5 %collective-permute-start.8 = (bf16[216,128]{1,0:T(8,128)(2,1)S(1)}, bf16[216,128]{1,0:T(8,128)(2,1)S(1)}, u32[]{:S(2)}, u32[]{:S(2)}) collective-permute-start(bf16[216,128]{1,0:T(8,128)(2,1)S(1)} %fusion.11), channel_id=1, source_target_pairs={{0,16},{4,20},{8,24},{12,28},{16,0},{20,4},{24,8},{28,12},{1,17},{... | collective-permute-start | bytes 165896 | tf_op jit(solution)/shard_map/ppermute | solution.py:456
  195.3 32.2 %collective-permute-start.14 = (bf16[5184,128]{1,0:T(8,128)(2,1)}, bf16[5184,128]{1,0:T(8,128)(2,1)}, u32[]{:S(2)}, u32[]{:S(2)}) collective-permute-start(bf16[5184,128]{1,0:T(8,128)(2,1)} %dynamic-slice_bitcast_fusion.1), channel_id=1, source_target_pairs={{0,1},{1,0},{2,3},{3,2},{4,5},{5,4},{6,7},{7,6},{8,9},{9,8},{10,11... | collective-permute-start | bytes 3981320 | tf_op jit(solution)/shard_map/ppermute | solution.py:449
  196.8 5.9 %collective-permute-start.9 = (bf16[432,128]{1,0:T(8,128)(2,1)S(1)}, bf16[432,128]{1,0:T(8,128)(2,1)S(1)}, u32[]{:S(2)}, u32[]{:S(2)}) collective-permute-start(bf16[432,128]{1,0:T(8,128)(2,1)S(1)} %pad_maximum_fusion.10), channel_id=1, source_target_pairs={{0,8},{4,12},{8,0},{12,4},{16,24},{20,28},{24,16},{28,20},{1,9},{5... | collective-permute-start | bytes 331784 | tf_op jit(solution)/shard_map/ppermute | solution.py:456
  202.8 6.0 %collective-permute-start.10 = (bf16[864,128]{1,0:T(8,128)(2,1)S(1)}, bf16[864,128]{1,0:T(8,128)(2,1)S(1)}, u32[]{:S(2)}, u32[]{:S(2)}) collective-permute-start(bf16[864,128]{1,0:T(8,128)(2,1)S(1)} %pad_maximum_fusion.9), channel_id=1, source_target_pairs={{0,4},{4,0},{8,12},{12,8},{16,20},{20,16},{24,28},{28,24},{1,5},{5... | collective-permute-start | bytes 663560 | tf_op jit(solution)/shard_map/ppermute | solution.py:456
  208.9 23.6 %collective-permute-start.11 = (bf16[1728,128]{1,0:T(8,128)(2,1)S(1)}, bf16[1728,128]{1,0:T(8,128)(2,1)}, u32[]{:S(2)}, u32[]{:S(2)}) collective-permute-start(bf16[1728,128]{1,0:T(8,128)(2,1)S(1)} %pad_maximum_fusion.7), channel_id=1, source_target_pairs={{0,1},{1,0},{2,3},{3,2},{4,5},{5,4},{6,7},{7,6},{8,9},{9,8},{10,11... | collective-permute-start | bytes 1327112 | tf_op jit(solution)/shard_map/ppermute | solution.py:456
  231.0 11.0 %collective-permute-start.15 = (bf16[2592,128]{1,0:T(8,128)(2,1)}, bf16[2592,128]{1,0:T(8,128)(2,1)}, u32[]{:S(2)}, u32[]{:S(2)}) collective-permute-start(bf16[2592,128]{1,0:T(8,128)(2,1)} %dynamic-slice_bitcast_fusion.3), channel_id=1, source_target_pairs={{0,4},{4,0},{8,12},{12,8},{16,20},{20,16},{24,28},{28,24},{1,5},{5... | collective-permute-start | bytes 1990664 | tf_op jit(solution)/shard_map/ppermute | solution.py:449
  243.3 8.5 %collective-permute-start.16 = (bf16[1296,128]{1,0:T(8,128)(2,1)S(1)}, bf16[1296,128]{1,0:T(8,128)(2,1)S(1)}, u32[]{:S(2)}, u32[]{:S(2)}) collective-permute-start(bf16[1296,128]{1,0:T(8,128)(2,1)S(1)} %dynamic-slice_bitcast_fusion.5), channel_id=1, source_target_pairs={{0,8},{4,12},{8,0},{12,4},{16,24},{20,28},{24,16},{28,20},{1,9},{5... | collective-permute-start | bytes 995336 | tf_op jit(solution)/shard_map/ppermute | solution.py:449
  245.5 57.2 %collective-permute-start.12 = (bf16[3456,128]{1,0:T(8,128)(2,1)S(1)}, bf16[3456,128]{1,0:T(8,128)(2,1)}, u32[]{:S(2)}, u32[]{:S(2)}) collective-permute-start(bf16[3456,128]{1,0:T(8,128)(2,1)S(1)} %pad_maximum_fusion.3), channel_id=1, source_target_pairs={{0,2},{2,0},{1,3},{3,1},{4,6},{6,4},{5,7},{7,5},{8,10},{10,8},{9,1... | collective-permute-start | bytes 2654216 | tf_op jit(solution)/shard_map/ppermute | solution.py:456
  252.6 46.4 %collective-permute-start.17 = (bf16[648,128]{1,0:T(8,128)(2,1)}, bf16[648,128]{1,0:T(8,128)(2,1)}, u32[]{:S(2)}, u32[]{:S(2)}) collective-permute-start(bf16[648,128]{1,0:T(8,128)(2,1)} %dynamic-slice_bitcast_fusion.7), channel_id=1, source_target_pairs={{0,16},{4,20},{8,24},{12,28},{16,0},{20,4},{24,8},{28,12},{1,17},{... | collective-permute-start | bytes 497672 | tf_op jit(solution)/shard_map/ppermute | solution.py:449
  300.0 10.0 %collective-permute-start.18 = (bf16[648,128]{1,0:T(8,128)(2,1)S(1)}, bf16[648,128]{1,0:T(8,128)(2,1)S(1)}, u32[]{:S(2)}, u32[]{:S(2)}) collective-permute-start(bf16[648,128]{1,0:T(8,128)(2,1)S(1)} %fusion.8), channel_id=1, source_target_pairs={{0,16},{4,20},{8,24},{12,28},{16,0},{20,4},{24,8},{28,12},{1,17},{... | collective-permute-start | bytes 497672 | tf_op jit(solution)/shard_map/ppermute | solution.py:456
  310.8 8.8 %collective-permute-start.19 = (bf16[1296,128]{1,0:T(8,128)(2,1)}, bf16[1296,128]{1,0:T(8,128)(2,1)}, u32[]{:S(2)}, u32[]{:S(2)}) collective-permute-start(bf16[1296,128]{1,0:T(8,128)(2,1)} %pad_maximum_fusion.8), channel_id=1, source_target_pairs={{0,8},{4,12},{8,0},{12,4},{16,24},{20,28},{24,16},{28,20},{1,9},{5... | collective-permute-start | bytes 995336 | tf_op jit(solution)/shard_map/ppermute | solution.py:456
  320.8 14.9 %collective-permute-start.20 = (bf16[2592,128]{1,0:T(8,128)(2,1)S(1)}, bf16[2592,128]{1,0:T(8,128)(2,1)}, u32[]{:S(2)}, u32[]{:S(2)}) collective-permute-start(bf16[2592,128]{1,0:T(8,128)(2,1)S(1)} %pad_maximum_fusion.4), channel_id=1, source_target_pairs={{0,4},{4,0},{8,12},{12,8},{16,20},{20,16},{24,28},{28,24},{1,5},{5... | collective-permute-start | bytes 1990664 | tf_op jit(solution)/shard_map/ppermute | solution.py:456
  (7 other events, 35.6 us)

commit v2 on v1

--- a/solution.py
+++ b/solution.py
@@ -1,11 +1,10 @@
-import functools
-
 import jax
 import jax.numpy as jnp
 from jax import lax
 from jax.experimental import pallas as pl
 from jax.experimental.pallas import tpu as pltpu
 from jax.sharding import PartitionSpec as P
+
 
 HEADS = 9
 KV_HEADS = 3
@@ -166,7 +165,7 @@
 
 def mlp_kernel(
     place_ref, mid_ref, og_ref, att_ref, norm_ref, w_out_ref, own_ref, side_ref, row_ref, far_ref, sel_ref,
-    out_ref, mg_ref, do_ref, delta_ref, g3_ref, gout_ref, gain_ref,
+    out_ref, mg_ref, do_ref, delta_ref, g00_ref, g01_ref, g10_ref, g11_ref,
     weights, acc3, acc_out, acc_gain,
 ):
     i = pl.program_id(0)
@@ -210,7 +209,8 @@
         acc3[1, :, at] += dot_nn(normed_t, up_low)
         acc3[2, :, at] += dot_nn(og_t, hidden)
     out_ref[...] = (middle + mlp_out).astype(BF16)
-    acc_gain[...] += jnp.sum((normed_grad * middle * scale).reshape(BLOCK // 8, 8, middle.shape[1]), axis=0)
+    width = middle.shape[1]
+    acc_gain[:, :width] += jnp.sum((normed_grad * middle * scale).reshape(BLOCK // 8, 8, width), axis=0)
     weighted = normed_grad * gain
     inner = jnp.sum(weighted * middle, axis=-1, keepdims=True)
     middle_grad = (
@@ -220,7 +220,7 @@
     mg_ref[...] = middle_grad
     middle_low = middle_grad.astype(BF16)
     attended = att_ref[...]
-    acc_out[...] += dot_tn(attended, middle_low)
+    acc_out[:, :width] += dot_tn(attended, middle_low)
     att_low = dot_nt(middle_low, w_out_ref[...]).astype(BF16)
     for h in range(HEADS):
         do_ref[h] = att_low[:, h * HEAD:(h + 1) * HEAD]
@@ -231,21 +231,45 @@
 
     @pl.when(i == pl.num_programs(0) - 1)
     def _():
-        for r in range(2):
-            for c in range(2):
-                for t in range(3):
-                    for part in range(cols_half // LANES):
-                        lane = r * cols_half + part * LANES
-                        g3_ref[r, c, t, part] = acc3[t, c * rows_half:(c + 1) * rows_half, lane:lane + LANES].astype(BF16)
-        gout_ref[...] = acc_out[...].astype(BF16)
-        gain_ref[...] = acc_gain[...]
-
-
-def mlp(place, middle, out_grad, attended, norm_two, w_out, own, side, across, far, selector):
+        quarter = width // 4
+        chunks = acc_out.shape[1] // LANES
+        for ref, c, r in ((g00_ref, col, row), (g01_ref, 1 - col, row), (g10_ref, col, 1 - row), (g11_ref, 1 - col, 1 - row)):
+            at_row = pl.multiple_of(c * rows_half, 32)
+            base = 0
+            for t in range(3):
+                for part in range(cols_half // LANES):
+                    lane = pl.ds(pl.multiple_of(r * cols_half + part * LANES, LANES), LANES)
+                    ref[base:base + rows_half, :] = acc3[t, pl.ds(at_row, rows_half), lane].astype(BF16)
+                    base += rows_half
+            at_row = pl.multiple_of((2 * r + c) * quarter, 16)
+            for part in range(chunks):
+                at = slice(part * LANES, (part + 1) * LANES)
+                ref[base:base + quarter, :] = acc_out[pl.ds(at_row, quarter), at].astype(BF16)
+                base += quarter
+            share = jnp.where((r == 0) & (c == 0), 1.0, 0.0)
+            for part in range(chunks):
+                at = slice(part * LANES, (part + 1) * LANES)
+                gains = acc_gain[:, at] * share
+                ref[base:base + 16, :] = jnp.concatenate([gains, jnp.zeros_like(gains)], axis=0).astype(BF16)
+                base += 16
+            ref[base:, :] = jnp.zeros((ref.shape[0] - base, LANES), BF16)
+
+
+def padded_width(width):
+    return -(-width // LANES) * LANES
+
+
+def round_up(count, unit):
+    return -(-count // unit) * unit
+
+
+def mlp(unit, place, middle, out_grad, attended, norm_two, w_out, own, side, across, far, selector):
     tokens, width = middle.shape
     rows_half, cols_half = own.shape[1:]
     blocks = tokens // BLOCK
-    parts = cols_half // LANES
+    chunks = padded_width(width) // LANES
+    tall = round_up(3 * cols_half // LANES * rows_half + chunks * (width // 4 + 16), unit)
+    block = pl.BlockSpec((tall, LANES), lambda i: (0, 0), pipeline_mode=pl.Buffered(1))
     rows = lambda i: (i, 0)
     whole = lambda i: (0, 0)
     whole3 = lambda i: (0, 0, 0)
@@ -271,24 +295,19 @@
             pl.BlockSpec((BLOCK, width), rows),
             pl.BlockSpec((HEADS, BLOCK, HEAD), lambda i: (0, i, 0)),
             pl.BlockSpec((16, BLOCK), lambda i: (0, i)),
-            pl.BlockSpec((2, 2, 3, parts, rows_half, LANES), lambda i: (0,) * 6, pipeline_mode=once),
-            pl.BlockSpec(w_out.shape, whole, pipeline_mode=once),
-            pl.BlockSpec((8, width), whole),
+            block, block, block, block,
         ],
         out_shape=[
             jax.ShapeDtypeStruct((tokens, width), BF16),
             jax.ShapeDtypeStruct((tokens, width), F32),
             jax.ShapeDtypeStruct((HEADS, tokens, HEAD), BF16),
             jax.ShapeDtypeStruct((16, tokens), F32),
-            jax.ShapeDtypeStruct((2, 2, 3, parts, rows_half, LANES), BF16),
-            jax.ShapeDtypeStruct(w_out.shape, BF16),
-            jax.ShapeDtypeStruct((8, width), F32),
-        ],
+        ] + [jax.ShapeDtypeStruct((tall, LANES), BF16)] * 4,
         scratch_shapes=[
             pltpu.VMEM((3, 2 * rows_half, 2 * cols_half), BF16),
             pltpu.VMEM((3, 2 * rows_half, 2 * cols_half), F32),
-            pltpu.VMEM(w_out.shape, F32),
-            pltpu.VMEM((8, width), F32),
+            pltpu.VMEM((width, padded_width(width)), F32),
+            pltpu.VMEM((8, padded_width(width)), F32),
         ],
         cost_estimate=pl.CostEstimate(flops=18 * 10**9, bytes_accessed=24 * 10**6, transcendentals=2 * 10**6),
         name="mlp",
@@ -296,9 +315,9 @@
 
 
 def back_kernel(
-    q_ref, k_ref, v_ref, do_ref, lse_ref, delta_ref, start_ref, cos_ref, sin_ref,
+    place_ref, q_ref, k_ref, v_ref, do_ref, lse_ref, delta_ref, start_ref, cos_ref, sin_ref,
     inputs_ref, mg_ref, norm_ref, w_qkv_ref,
-    ig_ref, gqkv_ref, gain_ref,
+    ig_ref, keep_ref, send_ref,
     dq_all, dk, dv, acc_qkv, acc_gain,
 ):
     j = pl.program_id(0)
@@ -358,30 +377,47 @@
     gain = norm_ref[...]
     scale = lax.rsqrt(jnp.mean(x * x, axis=-1, keepdims=True) + EPS)
     normed = (x * scale * gain).astype(BF16)
-    acc_qkv[...] += dot_tn(normed, joined_low)
+    acc_qkv[:, :joined_low.shape[1]] += dot_tn(normed, joined_low)
     normed_grad = dot_nt(joined_low, w_qkv_ref[...])
-    acc_gain[...] += jnp.sum((normed_grad * x * scale).reshape(BLOCK // 8, 8, x.shape[1]), axis=0)
+    acc_gain[:, :x.shape[1]] += jnp.sum((normed_grad * x * scale).reshape(BLOCK // 8, 8, x.shape[1]), axis=0)
     weighted = normed_grad * gain
     inner = jnp.sum(weighted * x, axis=-1, keepdims=True)
     ig_ref[...] = mg_ref[...] + scale * weighted - x * (scale * scale * scale) * inner / x.shape[1]
 
     @pl.when(j == blocks - 1)
     def _():
-        gqkv_ref[...] = acc_qkv[...].astype(BF16)
-        gain_ref[...] = acc_gain[...]
-
-
-def back(q, k, v, do, lse, delta, start, cosine, sine, inputs, middle_grad, norm_one, w_qkv):
+        row = place_ref[1]
+        width = x.shape[1]
+        half = acc_qkv.shape[1] // 2
+        for ref, r in ((keep_ref, row), (send_ref, 1 - row)):
+            base = 0
+            for part in range(half // LANES):
+                lane = pl.ds(pl.multiple_of(r * half + part * LANES, LANES), LANES)
+                ref[base:base + width, :] = acc_qkv[:, lane].astype(BF16)
+                base += width
+            share = jnp.where(r == 0, 1.0, 0.0)
+            for part in range(acc_gain.shape[1] // LANES):
+                gains = acc_gain[:, part * LANES:(part + 1) * LANES] * share
+                ref[base:base + 16, :] = jnp.concatenate([gains, jnp.zeros_like(gains)], axis=0).astype(BF16)
+                base += 16
+            ref[base:, :] = jnp.zeros((ref.shape[0] - base, LANES), BF16)
+
+
+def back(unit, place, q, k, v, do, lse, delta, start, cosine, sine, inputs, middle_grad, norm_one, w_qkv):
     tokens, width = inputs.shape
     blocks = tokens // BLOCK
     rows = lambda j: (j, 0)
     whole = lambda j: (0, 0)
     whole3 = lambda j: (0, 0, 0)
     mine3 = lambda j: (0, j, 0)
+    wide = round_up(w_qkv.shape[1], 2 * LANES)
+    tall = round_up(wide // 2 // LANES * width + 16 * padded_width(width) // LANES, unit)
+    block = pl.BlockSpec((tall, LANES), whole)
     return pl.pallas_call(
         back_kernel,
         grid=(blocks,),
         in_specs=[
+            pl.BlockSpec(memory_space=pltpu.SMEM),
             pl.BlockSpec(q.shape, whole3),
             pl.BlockSpec((KV_HEADS, BLOCK, HEAD), mine3),
             pl.BlockSpec((KV_HEADS, BLOCK, HEAD), mine3),
@@ -398,24 +434,23 @@
         ],
         out_specs=[
             pl.BlockSpec((BLOCK, width), rows),
-            pl.BlockSpec(w_qkv.shape, whole),
-            pl.BlockSpec((8, width), whole),
+            block, block,
         ],
         out_shape=[
             jax.ShapeDtypeStruct((tokens, width), F32),
-            jax.ShapeDtypeStruct(w_qkv.shape, BF16),
-            jax.ShapeDtypeStruct((8, width), F32),
+            jax.ShapeDtypeStruct((tall, LANES), BF16),
+            jax.ShapeDtypeStruct((tall, LANES), BF16),
         ],
         scratch_shapes=[
             pltpu.VMEM((blocks, KV_HEADS, HEAD, GROUP * BLOCK), F32),
             pltpu.VMEM((KV_HEADS, BLOCK, HEAD), F32),
             pltpu.VMEM((KV_HEADS, BLOCK, HEAD), F32),
-            pltpu.VMEM(w_qkv.shape, F32),
-            pltpu.VMEM((8, width), F32),
+            pltpu.VMEM((width, wide), F32),
+            pltpu.VMEM((8, padded_width(width)), F32),
         ],
         cost_estimate=pl.CostEstimate(flops=8 * 10**9, bytes_accessed=16 * 10**6, transcendentals=6 * 10**6),
         name="back",
-    )(q, k, v, do, lse, delta, start, cosine, sine, inputs, middle_grad, norm_one, w_qkv)
+    )(place, q, k, v, do, lse, delta, start, cosine, sine, inputs, middle_grad, norm_one, w_qkv)
 
 
 def places(seq_ids):
@@ -437,25 +472,70 @@
     )
 
 
-SWAP = [(0, 1), (1, 0)]
-
-
-def halve(data, axis, bit, size):
-    pairs = [(n, n ^ bit) for n in range(size)]
-    mine = (lax.axis_index(axis) // bit) % 2
-    halves = data.reshape((2, data.shape[0] // 2) + data.shape[1:])
-    sent = lax.dynamic_index_in_dim(halves, 1 - mine, 0, keepdims=False)
-    kept = lax.dynamic_index_in_dim(halves, mine, 0, keepdims=False)
-    arrived = lax.ppermute(sent, axis, pairs)
-    return (kept.astype(F32) + arrived.astype(F32)).astype(BF16)
-
-
-def double(data, axis, bit, size):
-    pairs = [(n, n ^ bit) for n in range(size)]
-    mine = (lax.axis_index(axis) // bit) % 2
-    arrived = lax.ppermute(data, axis, pairs)
-    lower = mine == 0
-    return jnp.concatenate([jnp.where(lower, data, arrived), jnp.where(lower, arrived, data)], axis=0)
+def merge(flows):
+    turns = jnp.stack([jnp.int32(0) if bit is None else bit for _, bit in flows]).astype(jnp.int32)
+    counts = [len(terms) for terms, _ in flows]
+    splits = [bit is not None for _, bit in flows]
+    shapes = []
+    for (terms, _), split in zip(flows, splits):
+        rows = terms[0].shape[0] // (2 if split else 1)
+        shapes += [jax.ShapeDtypeStruct((rows, LANES), BF16)] * (2 if split else 1)
+
+    def kernel(turn_ref, *refs):
+        ins, outs = refs[:sum(counts)], refs[sum(counts):]
+        for n, (count, split) in enumerate(zip(counts, splits)):
+            mine, ins = ins[:count], ins[count:]
+            for side in range(2 if split else 1):
+                out, outs = outs[0], outs[1:]
+                rows = out.shape[0]
+                if split:
+                    part = turn_ref[n] if side == 0 else 1 - turn_ref[n]
+                    span = pl.ds(pl.multiple_of(part * rows, 16), rows)
+                else:
+                    span = pl.ds(0, rows)
+                value = mine[0][span, :].astype(F32)
+                for ref in mine[1:]:
+                    value += ref[span, :].astype(F32)
+                out[...] = value.astype(BF16)
+
+    vmem = pl.BlockSpec(memory_space=pltpu.VMEM)
+    operands = [term for terms, _ in flows for term in terms]
+    size = sum(term.size for term in operands)
+    outs = pl.pallas_call(
+        kernel,
+        in_specs=[pl.BlockSpec(memory_space=pltpu.SMEM)] + [vmem] * len(operands),
+        out_specs=[vmem] * len(shapes),
+        out_shape=shapes,
+        cost_estimate=pl.CostEstimate(flops=size, bytes_accessed=3 * size, transcendentals=0),
+    )(turns, *operands)
+    result = []
+    for split in splits:
+        result.append(tuple(outs[:2]) if split else outs[0])
+        outs = outs[2 if split else 1:]
+    return result
+
+
+def join(flows):
+    turns = jnp.stack([bit for _, _, bit in flows]).astype(jnp.int32)
+    shapes = [jax.ShapeDtypeStruct((2 * mine.shape[0], LANES), BF16) for mine, _, _ in flows]
+
+    def kernel(turn_ref, *refs):
+        ins, outs = refs[:2 * len(flows)], refs[2 * len(flows):]
+        for n, out in enumerate(outs):
+            rows = out.shape[0] // 2
+            out[pl.ds(pl.multiple_of(turn_ref[n] * rows, 16), rows), :] = ins[2 * n][...]
+            out[pl.ds(pl.multiple_of((1 - turn_ref[n]) * rows, 16), rows), :] = ins[2 * n + 1][...]
+
+    vmem = pl.BlockSpec(memory_space=pltpu.VMEM)
+    operands = [part for mine, arrived, _ in flows for part in (mine, arrived)]
+    size = sum(part.size for part in operands)
+    return pl.pallas_call(
+        kernel,
+        in_specs=[pl.BlockSpec(memory_space=pltpu.SMEM)] + [vmem] * len(operands),
+        out_specs=[vmem] * len(shapes),
+        out_shape=shapes,
+        cost_estimate=pl.CostEstimate(flops=0, bytes_accessed=4 * size, transcendentals=0),
+    )(turns, *operands)
 
 
 def bits(size):
@@ -466,62 +546,119 @@
     return out
 
 
-def per_device(inputs, seq_ids, norm_one, w_qkv, w_out, norm_two, w_gate, w_up, w_down, out_grad):
-    dp_size, row_size, col_size = (lax.axis_size(name) for name in ("dp", "row", "col"))
+def swap_with(data, axis, bit):
+    size = lax.axis_size(axis)
+    return lax.ppermute(data, axis, [(n, n ^ bit) for n in range(size)])
+
+
+def own_bit(axis, bit):
+    return (lax.axis_index(axis) // bit) % 2
+
+
+def layer(inputs, seq_ids, norm_one, w_qkv, w_out, norm_two, w_gate, w_up, w_down, out_grad):
+    dp_bits = [("dp", bit) for bit in bits(lax.axis_size("dp"))]
+    stages = len(dp_bits)
+    unit = 32 * lax.axis_size("dp")
     width = inputs.shape[1]
     own = jnp.stack([w_gate, w_up, w_down.T])
-    side = lax.ppermute(own, "col", SWAP)
-    across = lax.ppermute(own, "row", SWAP)
-    far = lax.ppermute(side, "row", SWAP)
+    side = swap_with(own, "col", 1)
+    across = swap_with(own, "row", 1)
     start, place = places(seq_ids)
     start = start[None, :]
     cosine, sine = tables(place)
     gain_one, gain_two = norm_one[None, :], norm_two[None, :]
     q, k, v, lse, attended, middle = front(inputs, start, cosine, sine, gain_one, w_qkv, w_out)
+    far = swap_with(side, "row", 1)
     selector = (jnp.arange(16)[:, None] == jnp.arange(width)[None, :] // HEAD).astype(BF16)
     spot = jnp.stack([lax.axis_index("col"), lax.axis_index("row")]).astype(jnp.int32)
-    outputs, middle_grad, do, delta, grads, gout, gain_two_part = mlp(
-        spot, middle, out_grad, attended, gain_two, w_out, own, side, across, far, selector
+    outputs, middle_grad, do, delta, keep_keep, keep_send, send_keep, send_send = mlp(
+        unit, spot, middle, out_grad, attended, gain_two, w_out, own, side, across, far, selector
     )
-    grads = grads.reshape(-1, LANES)
-    grads = halve(grads, "row", 1, row_size)
-    grads = halve(grads, "col", 1, col_size)
-    for bit in bits(dp_size):
-        grads = halve(grads, "dp", bit, dp_size)
-    for bit in reversed(bits(dp_size)):
-        grads = double(grads, "dp", bit, dp_size)
-    input_grad, gqkv, gain_one_part = back(
-        q, k, v, do, lse, delta, start, cosine, sine, inputs, middle_grad, gain_one, w_qkv
+    row_send = swap_with(send_send, "row", 1)
+    row_keep = swap_with(send_keep, "row", 1)
+    (to_col,) = merge([((keep_send, row_send), None)])
+    from_col = swap_with(to_col, "col", 1)
+    input_grad, shared_keep, shared_send = back(
+        unit, spot, q, k, v, do, lse, delta, start, cosine, sine, inputs, middle_grad, gain_one, w_qkv
     )
-    gains = lax.psum((jnp.sum(gain_one_part, axis=0), jnp.sum(gain_two_part, axis=0)), ("dp", "row", "col"))
-    shared = jnp.concatenate([gqkv.reshape(-1, LANES), gout.reshape(-1, LANES)], axis=0)
-    extra = -shared.shape[0] % (8 * dp_size * row_size * col_size)
-    rows_shared = shared.shape[0]
-    shared = jnp.pad(shared, ((0, extra), (0, 0)))
-    shared = halve(shared, "row", 1, row_size)
-    shared = halve(shared, "col", 1, col_size)
-    for bit in bits(dp_size):
-        shared = halve(shared, "dp", bit, dp_size)
-    for bit in reversed(bits(dp_size)):
-        shared = double(shared, "dp", bit, dp_size)
-    shared = double(shared, "col", 1, col_size)
-    shared = double(shared, "row", 1, row_size)
-    cut = gqkv.size // LANES
-    grad_qkv = shared[:cut].reshape(gqkv.shape).astype(F32)
-    grad_out = shared[cut:rows_shared].reshape(gout.shape).astype(F32)
-    parts = w_gate.shape[1] // LANES
-    grads = grads.reshape(3, parts, w_gate.shape[0], LANES).astype(F32)
+    shared_row = swap_with(shared_send, "row", 1)
+
+    half = keep_keep.shape[0] // 2
+    order_a = dp_bits
+    order_b = dp_bits[1:2] + dp_bits[:1] + dp_bits[2:]
+    order_s = [("col", 1)] + dp_bits
+    terms = (keep_keep, row_keep, from_col)
+    halves = [tuple(term[at:at + half] for term in terms) for at in (0, half)]
+    (a, b) = merge([(halves[0], own_bit(*order_a[0])), (halves[1], own_bit(*order_b[0]))])
+    (s,) = merge([((shared_keep, shared_row), own_bit(*order_s[0]))])
+    for n in range(stages):
+        a_in = swap_with(a[1], *order_a[n])
+        b_in = swap_with(b[1], *order_b[n])
+        s_in = swap_with(s[1], *order_s[n])
+        last = n == stages - 1
+        a, b, s = merge(
+            [
+                ((a[0], a_in), None if last else own_bit(*order_a[n + 1])),
+                ((b[0], b_in), None if last else own_bit(*order_b[n + 1])),
+                ((s[0], s_in), own_bit(*order_s[n + 1])),
+            ],
+        )
+    for n in reversed(range(stages)):
+        a_in = swap_with(a, *order_a[n])
+        b_in = swap_with(b, *order_b[n])
+        pairs = [(a, a_in, own_bit(*order_a[n])), (b, b_in, own_bit(*order_b[n]))]
+        if n == stages - 1:
+            s_in = swap_with(s[1], *order_s[n + 1])
+            (s,) = merge([((s[0], s_in), None)])
+        else:
+            s_in = swap_with(s, *order_s[n + 2])
+            pairs.append((s, s_in, own_bit(*order_s[n + 2])))
+        joined = join(pairs)
+        a, b = joined[:2]
+        if n < stages - 1:
+            s = joined[2]
+    grads = jnp.concatenate([a, b], axis=0)
+    used = 3 * w_gate.size // LANES
+    rest = grads[used:]
+    for n in (1, 0):
+        s_in = swap_with(s, *order_s[n])
+        pairs = [(s, s_in, own_bit(*order_s[n]))]
+        if n == 0:
+            rest_in = swap_with(rest, "col", 1)
+            pairs.append((rest, rest_in, own_bit("col", 1)))
+        joined = join(pairs)
+        s = joined[0]
+    rest = joined[1]
+    s_in = swap_with(s, "row", 1)
+    rest_in = swap_with(rest, "row", 1)
+    row_bit = own_bit("row", 1)
+    s, rest = join([(s, s_in, row_bit), (rest, rest_in, row_bit)])
+
+    def flat(block, rows):
+        return jnp.concatenate([block[at:at + rows] for at in range(0, block.shape[0], rows)], axis=1)
+
+    chunks = padded_width(width) // LANES
+    s = s.reshape(2, -1, LANES)
+    reach = round_up(w_qkv.shape[1], 2 * LANES) // 2 // LANES * width
+    grad_qkv = jnp.concatenate([flat(s[0, :reach], width), flat(s[1, :reach], width)], axis=1)[:, :w_qkv.shape[1]].astype(F32)
+    grad_norm_one = jnp.sum(flat(s[0, reach:reach + 16 * chunks], 16)[:8, :width].astype(F32), axis=0)
+    rest = rest.reshape(4, -1, LANES)
+    quarter = width // 4
+    reach = chunks * quarter
+    grad_out = jnp.concatenate([flat(rest[n, :reach], quarter)[:, :width] for n in range(4)], axis=0).astype(F32)
+    grad_norm_two = jnp.sum(flat(rest[0, reach:reach + 16 * chunks], 16)[:8, :width].astype(F32), axis=0)
+    grads = grads[:used].reshape(3, -1, w_gate.shape[0], LANES).astype(F32)
     grad_gate = grads[0].transpose(1, 0, 2).reshape(w_gate.shape)
     grad_up = grads[1].transpose(1, 0, 2).reshape(w_up.shape)
     grad_down = grads[2].transpose(0, 2, 1).reshape(w_down.shape)
-    return (outputs, input_grad, gains[0], grad_qkv, grad_out, gains[1], grad_gate, grad_up, grad_down)
+    return (outputs, input_grad, grad_norm_one, grad_qkv, grad_out, grad_norm_two, grad_gate, grad_up, grad_down)
 
 
 def solution(mesh):
     tokens = P(("dp", "row", "col"), None)
     grid, turned = P("col", "row"), P("row", "col")
     return jax.shard_map(
-        per_device,
+        layer,
         mesh=mesh,
         in_specs=(tokens, P(("dp", "row", "col")), P(), P(), P(), P(), grid, grid, turned, tokens),
         out_specs=(tokens, tokens, P(), P(), P(), P(), grid, grid, turned),

time: 341 us -> 308 us (0.903)
  waiting for transfers between devices: 113 us -> 70.8 us
  blocking collectives: 41.5 us -> 0 us
  Pallas kernels: 102 us -> 134 us
  local copies, waits for them, and re-layouts: 28.8 us -> 49.7 us
  other arithmetic: 24.5 us -> 16.8 us
  starting transfers between devices: 29.7 us -> 33.5 us
    ppermute x21 -> x30, waiting for transfers between devices: 113 us -> 70.8 us  [swap_with(): return lax.ppermute(data, axis, [(n, n ^ bit) for n in range(size)])]
    psum x1 -> x0, blocking collectives: 41.5 us -> none  [per_device(): lax.psum((jnp.sum(gain_one_part, axis=0), jnp.sum(gain_two_part, axis=0))...]
    pallas_call x1 -> x14, Pallas kernels: 32 us -> 63.9 us  [the longest x1 32.4 us: back(): pl.pallas_call(back_kernel, grid=(blocks,), in_specs=[pl.BlockSpec(memory...]
    unnamed x24 -> x98, local copies, waits for them, and re-layouts: 9.48 us -> 37 us
    reshape x5 -> x0, local copies, waits for them, and re-layouts: 7.54 us -> none  [the longest x1 2.72 us: per_device(): gqkv.reshape(-1, LANES)]
    convert_element_type x14 -> x4, other arithmetic: 11.1 us -> 3.68 us  [the longest x1 1.69 us: layer(): jnp.concatenate([flat(s[0, :reach], width), flat(s[1, :reach], width)], a...]
    slice x2 -> x6, local copies, waits for them, and re-layouts: 0.25 us -> 6.3 us  [the longest x3 5.09 us: layer(): halves = [tuple((term[at:at + half] for term in terms)) for at in (0, half)]]
    select_n x9 -> x1, other arithmetic: 5.42 us -> 0.01 us  [layer(): jnp.arange(width)[None, :] // HEAD]
  transfers between devices with their start and end apart: 21 -> 30, of which waited for: 14 -> 14; matrix products, arithmetic and copies ran while one was open for 11% -> 11% of each run, Pallas kernels for 8% -> 24%
where the time goes in v2:
time: 308 us; the launch traced here: 307 us
  Pallas kernels  134 us (44%)
  waiting for transfers between devices  70.8 us (23%)
  local copies, waits for them, and re-layouts  49.7 us (16%)
  starting transfers between devices  33.5 us (11%)
  other arithmetic  16.8 us (5%)
    ppermute x30, waiting for transfers between devices, swap_with(): return lax.ppermute(data, axis, [(n, n ^ bit) for n in range(size)])  70.8 us
    pallas_call x1, Pallas kernels, mlp(): pl.pallas_call(mlp_kernel, grid=(blocks,), in_specs=[pl.BlockSpec(memory_...  41.6 us
    unnamed x98, local copies, waits for them, and re-layouts  37 us
    ppermute x30, starting transfers between devices, swap_with(): return lax.ppermute(data, axis, [(n, n ^ bit) for n in range(size)])  33.5 us
    pallas_call x1, Pallas kernels, back(): pl.pallas_call(back_kernel, grid=(blocks,), in_specs=[pl.BlockSpec(memory...  32.4 us
    pallas_call x1, Pallas kernels, front(): pl.pallas_call(front_kernel, grid=(blocks,), in_specs=[pl.BlockSpec((BLOC...  28.8 us
    pallas_call x7, Pallas kernels, merge(): pl.pallas_call(kernel, in_specs=[pl.BlockSpec(memory_space=pltpu.SMEM)] +...  17.7 us
    pallas_call x6, Pallas kernels, join(): pl.pallas_call(kernel, in_specs=[pl.BlockSpec(memory_space=pltpu.SMEM)] +...  13.8 us
  transfers between devices with their start and end apart: 30, of which 14 were waited for; matrix products, arithmetic and copies ran while one was open for 11% of the time, Pallas kernels for 24%

profile of v2, /device:TPU:0, one launch (start us, length us, event | category | flops | bytes accessed | tf_op | source)
XLA Modules:
  0.0 306.8 jit_solution(4898372643090384775)
XLA Ops:
  2.2 3.1 collective-permute-start
  7.7 26.8 %collective-permute-done.side_ref = bf16[3,288,768]{2,1,0:T(8,128)(2,1)} collective-permute-done((bf16[3,288,768]{2,1,0:T(8,128)(2,1)S(1)}, bf16[3,288,768]{2,1,0:T(8,128)(2,1)}, u32[]{:S(2)}, u32[]{:S(2)}) %collective-permute-start) | collective-permute-done | bytes 1327136 | tf_op jit(solution)/shard_map/ppermute | solution.py:551
  37.2 2.4 copy.37.og_ref
  44.5 28.8 %front.1 = (bf16[9,1024,64]{2,1,0:T(8,128)(2,1)}, bf16[3,1024,64]{2,1,0:T(8,128)(2,1)}, bf16[3,1024,64]{2,1,0:T(8,128)(2,1)}, f32[16,1024]{1,0:T(8,128)}, bf16[1...) custom-call(bf16[1024,576]{1,0:T(8,128)(2,1)} %copy.36.inputs_ref, s32[1,1024]{1,0:T(1,128)} %bitcast.238, ...), custom_call_target="tpu_custom_call" | custom-call | flops 6000000000 | bytes 12000000 | tf_op jit(solution)/shard_map/front/pallas_call | solution.py:126
  73.4 41.6 %mlp.1 = (bf16[1024,576]{1,0:T(8,128)(2,1)}, f32[1024,576]{1,0:T(8,128)}, bf16[9,1024,64]{2,1,0:T(8,128)(2,1)}, f32[16,1024]{1,0:T(8,128)}, bf16[6144,128]{1,0:T...) custom-call(s32[2]{0:T(128)} %pad_add_fusion.place_ref, ...), custom_call_target="tpu_custom_call" | custom-call | flops 17999998976 | bytes 24000000 | tf_op jit(solution)/shard_map/mlp/pallas_call | solution.py:277
  116.3 2.5 collective-permute-done.4.refs_1_
  119.9 3.4 %shard_map.169 = bf16[6144,128]{1,0:T(8,128)(2,1)} custom-call(s32[1]{0:T(128)} %constant.185.clone.1.turn_ref, bf16[6144,128]{1,0:T(8,128)(2,1)} %get-tuple-element.73.refs_0_, bf16[6144,128]{1,0:T(8,128)(2,1)} %copy-done.1), custom_call_target="tpu_custom_call" | custom-call | flops 1572864 | bytes 4718592 | tf_op jit(solution)/shard_map/pallas_call | solution.py:504
  125.1 32.4 %back.1 = (f32[1024,576]{1,0:T(8,128)}, bf16[2560,128]{1,0:T(8,128)(2,1)}, bf16[2560,128]{1,0:T(8,128)(2,1)}) custom-call(s32[2]{0:T(128)} %pad_add_fusion.place_ref, bf16[9,1024,64]{2,1,0:T(8,128)(2,1)} %get-tuple-element.63.q_ref, bf16[3,1024,64]{2,1,0:T(8,128)(2,1)} %get-tuple-element.64.k_ref, bf16[3,1024,64]{2,1,0:T(8,128)(2,1)} %get-tuple-element.65.v_ref, ...), custom_call_target="tpu_custom_call" | custom-call | flops 8000000000 | bytes 16000000 | tf_op jit(solution)/shard_map/back/pallas_call | solution.py:416
  160.3 2.6 fusion.17
  162.9 4.0 %shard_map.170 = (bf16[1536,128]{1,0:T(8,128)(2,1)}, bf16[1536,128]{1,0:T(8,128)(2,1)}, bf16[1536,128]{1,0:T(8,128)(2,1)}, bf16[1536,128]{1,0:T(8,128)(2,1)}) custom-call(s32[2]{0:T(128)} %pad_add_fusion.6.turn_ref, bf16[3072,128]{1,0:T(8,128)(2,1)} %get-tuple-element.148.refs_0_, bf16[3072,128]{1,0:T(8,128)(2,1)} %get-tuple-element.146.refs_1_, ...), custom_call_target="tpu_custom_call" | custom-call | flops 2359296 | bytes 7077888 | tf_op jit(solution)/shard_map/pallas_call | solution.py:504
  174.5 7.2 %collective-permute-done.9.refs_5_ = bf16[1280,128]{1,0:T(8,128)(2,1)S(1)} collective-permute-done((bf16[1280,128]{1,0:T(8,128)(2,1)}, bf16[1280,128]{1,0:T(8,128)(2,1)S(1)}, u32[]{:S(2)}, u32[]{:S(2)}) %collective-permute-start.9) | collective-permute-done | bytes 327712 | tf_op jit(solution)/shard_map/ppermute | solution.py:551
  182.7 2.7 shard_map.172
  188.5 6.2 %collective-permute-done.12.refs_5_ = bf16[640,128]{1,0:T(8,128)(2,1)S(1)} collective-permute-done((bf16[640,128]{1,0:T(8,128)(2,1)}, bf16[640,128]{1,0:T(8,128)(2,1)S(1)}, u32[]{:S(2)}, u32[]{:S(2)}) %collective-permute-start.12) | collective-permute-done | bytes 163872 | tf_op jit(solution)/shard_map/ppermute | solution.py:551
  197.7 2.6 collective-permute-start.13
  202.8 3.6 %collective-permute-done.15.refs_5_ = bf16[320,128]{1,0:T(8,128)(2,1)S(1)} collective-permute-done((bf16[320,128]{1,0:T(8,128)(2,1)}, bf16[320,128]{1,0:T(8,128)(2,1)S(1)}, u32[]{:S(2)}, u32[]{:S(2)}) %collective-permute-start.15) | collective-permute-done | bytes 81952 | tf_op jit(solution)/shard_map/ppermute | solution.py:551
  209.9 2.4 collective-permute-start.16
  213.4 4.3 %collective-permute-done.16.refs_1_ = bf16[384,128]{1,0:T(8,128)(2,1)S(1)} collective-permute-done((bf16[384,128]{1,0:T(8,128)(2,1)}, bf16[384,128]{1,0:T(8,128)(2,1)S(1)}, u32[]{:S(2)}, u32[]{:S(2)}) %collective-permute-start.16) | collective-permute-done | bytes 98336 | tf_op jit(solution)/shard_map/ppermute | solution.py:551
  225.7 3.0 collective-permute-done.20.refs_1_
  233.5 2.3 collective-permute-done.21.refs_5_
  243.7 6.2 %collective-permute-done.24.refs_5_ = bf16[320,128]{1,0:T(8,128)(2,1)S(1)} collective-permute-done((bf16[320,128]{1,0:T(8,128)(2,1)}, bf16[320,128]{1,0:T(8,128)(2,1)S(1)}, u32[]{:S(2)}, u32[]{:S(2)}) %collective-permute-start.24) | collective-permute-done | bytes 81952 | tf_op jit(solution)/shard_map/ppermute | solution.py:551
  251.4 2.7 shard_map.178
  254.4 5.2 %collective-permute-done.25.refs_1_ = bf16[640,128]{1,0:T(8,128)(2,1)S(1)} collective-permute-done((bf16[640,128]{1,0:T(8,128)(2,1)}, bf16[640,128]{1,0:T(8,128)(2,1)S(1)}, u32[]{:S(2)}, u32[]{:S(2)}) %collective-permute-start.25) | collective-permute-done | bytes 163872 | tf_op jit(solution)/shard_map/ppermute | solution.py:551
  268.3 2.5 copy.42
  283.9 3.1 %shard_map.181 = (bf16[5120,128]{1,0:T(8,128)(2,1)}, bf16[3840,128]{1,0:T(8,128)(2,1)}) custom-call(s32[2]{0:T(128)} %pad_add_fusion.1.turn_ref, bf16[2560,128]{1,0:T(8,128)(2,1)} %get-tuple-element.106.refs_0_, bf16[2560,128]{1,0:T(8,128)(2,1)} %copy-done.8, bf16[1920,128]{1,0:T(8,128)(2,1)} %get-tuple-element.107.refs_2_, bf16[1920,128]{1,0:T(8,128)(2,1)} %copy-done.11), custom_call_target="tpu_custom_call" | custom-call | bytes 4587520 | tf_op jit(solution)/shard_map/pallas_call | solution.py:532
  (192 shorter events, 103.7 us)
Async XLA Ops:
  2.2 32.3 %collective-permute-start = (bf16[3,288,768]{2,1,0:T(8,128)(2,1)S(1)}, bf16[3,288,768]{2,1,0:T(8,128)(2,1)}, u32[]{:S(2)}, u32[]{:S(2)}) collective-permute-start(bf16[3,288,768]{2,1,0:T(8,128)(2,1)S(1)} %pad_maximum_fusion.1.own_ref), channel_id=1, source_target_pairs={{0,1},{1,0},{2,3},{3,2},{4,5},{5,4},{6,7},{7,6},{8,9},{9,8},{10,11... | collective-permute-start | bytes 3981320 | tf_op jit(solution)/shard_map/ppermute | solution.py:551
  5.3 68.1 %collective-permute-start.1 = (bf16[3,288,768]{2,1,0:T(8,128)(2,1)S(1)}, bf16[3,288,768]{2,1,0:T(8,128)(2,1)}, u32[]{:S(2)}, u32[]{:S(2)}) collective-permute-start(bf16[3,288,768]{2,1,0:T(8,128)(2,1)S(1)} %pad_maximum_fusion.1.own_ref), channel_id=1, source_target_pairs={{0,2},{2,0},{1,3},{3,1},{4,6},{6,4},{5,7},{7,5},{8,10},{10,8},{9,1... | collective-permute-start | bytes 3981320 | tf_op jit(solution)/shard_map/ppermute | solution.py:551
  34.5 38.8 %collective-permute-start.2 = (bf16[3,288,768]{2,1,0:T(8,128)(2,1)}, bf16[3,288,768]{2,1,0:T(8,128)(2,1)}, u32[]{:S(2)}, u32[]{:S(2)}) collective-permute-start(bf16[3,288,768]{2,1,0:T(8,128)(2,1)} %collective-permute-done.side_ref), channel_id=1, source_target_pairs={{0,2},{2,0},{1,3},{3,1},{4,6},{6,4},{5,7},{7,5},{8,10},{10,8},{9,1... | collective-permute-start | bytes 3981320 | tf_op jit(solution)/shard_map/ppermute | solution.py:551
  115.5 43.4 %collective-permute-start.3 = (bf16[6144,128]{1,0:T(8,128)(2,1)}, bf16[6144,128]{1,0:T(8,128)(2,1)S(1)}, u32[]{:S(2)}, u32[]{:S(2)}) collective-permute-start(bf16[6144,128]{1,0:T(8,128)(2,1)} %get-tuple-element.72), channel_id=1, source_target_pairs={{0,2},{2,0},{1,3},{3,1},{4,6},{6,4},{5,7},{7,5},{8,10},{10,8},{9,1... | collective-permute-start | bytes 4718600 | tf_op jit(solution)/shard_map/ppermute | solution.py:551
  123.3 37.0 %collective-permute-start.5 = (bf16[6144,128]{1,0:T(8,128)(2,1)}, bf16[6144,128]{1,0:T(8,128)(2,1)}, u32[]{:S(2)}, u32[]{:S(2)}) collective-permute-start(bf16[6144,128]{1,0:T(8,128)(2,1)} %shard_map.169), channel_id=1, source_target_pairs={{0,1},{1,0},{2,3},{3,2},{4,5},{5,4},{6,7},{7,6},{8,9},{9,8},{10,11... | collective-permute-start | bytes 4718600 | tf_op jit(solution)/shard_map/ppermute | solution.py:551
  157.5 12.7 %collective-permute-start.8 = (bf16[2560,128]{1,0:T(8,128)(2,1)}, bf16[2560,128]{1,0:T(8,128)(2,1)}, u32[]{:S(2)}, u32[]{:S(2)}) collective-permute-start(bf16[2560,128]{1,0:T(8,128)(2,1)} %get-tuple-element.80), channel_id=1, source_target_pairs={{0,2},{2,0},{1,3},{3,1},{4,6},{6,4},{5,7},{7,5},{8,10},{10,8},{9,1... | collective-permute-start | bytes 1966088 | tf_op jit(solution)/shard_map/ppermute | solution.py:551
  166.9 14.8 %collective-permute-start.6 = (bf16[1536,128]{1,0:T(8,128)(2,1)}, bf16[1536,128]{1,0:T(8,128)(2,1)S(1)}, u32[]{:S(2)}, u32[]{:S(2)}) collective-permute-start(bf16[1536,128]{1,0:T(8,128)(2,1)} %get-tuple-element.76), channel_id=1, source_target_pairs={{0,4},{4,0},{8,12},{12,8},{16,20},{20,16},{24,28},{28,24},{1,5},{5... | collective-permute-start | bytes 1179656 | tf_op jit(solution)/shard_map/ppermute | solution.py:551
  168.6 13.1 %collective-permute-start.7 = (bf16[1536,128]{1,0:T(8,128)(2,1)}, bf16[1536,128]{1,0:T(8,128)(2,1)S(1)}, u32[]{:S(2)}, u32[]{:S(2)}) collective-permute-start(bf16[1536,128]{1,0:T(8,128)(2,1)} %get-tuple-element.78), channel_id=1, source_target_pairs={{0,8},{4,12},{8,0},{12,4},{16,24},{20,28},{24,16},{28,20},{1,9},{5... | collective-permute-start | bytes 1179656 | tf_op jit(solution)/shard_map/ppermute | solution.py:551
  172.4 9.3 %collective-permute-start.9 = (bf16[1280,128]{1,0:T(8,128)(2,1)}, bf16[1280,128]{1,0:T(8,128)(2,1)S(1)}, u32[]{:S(2)}, u32[]{:S(2)}) collective-permute-start(bf16[1280,128]{1,0:T(8,128)(2,1)} %get-tuple-element.82), channel_id=1, source_target_pairs={{0,1},{1,0},{2,3},{3,2},{4,5},{5,4},{6,7},{7,6},{8,9},{9,8},{10,11... | collective-permute-start | bytes 983048 | tf_op jit(solution)/shard_map/ppermute | solution.py:551
  185.4 9.3 %collective-permute-start.10 = (bf16[768,128]{1,0:T(8,128)(2,1)}, bf16[768,128]{1,0:T(8,128)(2,1)S(1)}, u32[]{:S(2)}, u32[]{:S(2)}) collective-permute-start(bf16[768,128]{1,0:T(8,128)(2,1)} %get-tuple-element.84), channel_id=1, source_target_pairs={{0,8},{4,12},{8,0},{12,4},{16,24},{20,28},{24,16},{28,20},{1,9},{5... | collective-permute-start | bytes 589832 | tf_op jit(solution)/shard_map/ppermute | solution.py:551
  185.8 8.9 %collective-permute-start.11 = (bf16[768,128]{1,0:T(8,128)(2,1)}, bf16[768,128]{1,0:T(8,128)(2,1)S(1)}, u32[]{:S(2)}, u32[]{:S(2)}) collective-permute-start(bf16[768,128]{1,0:T(8,128)(2,1)} %get-tuple-element.86), channel_id=1, source_target_pairs={{0,4},{4,0},{8,12},{12,8},{16,20},{20,16},{24,28},{28,24},{1,5},{5... | collective-permute-start | bytes 589832 | tf_op jit(solution)/shard_map/ppermute | solution.py:551
  186.4 8.3 %collective-permute-start.12 = (bf16[640,128]{1,0:T(8,128)(2,1)}, bf16[640,128]{1,0:T(8,128)(2,1)S(1)}, u32[]{:S(2)}, u32[]{:S(2)}) collective-permute-start(bf16[640,128]{1,0:T(8,128)(2,1)} %get-tuple-element.88), channel_id=1, source_target_pairs={{0,4},{4,0},{8,12},{12,8},{16,20},{20,16},{24,28},{28,24},{1,5},{5... | collective-permute-start | bytes 491528 | tf_op jit(solution)/shard_map/ppermute | solution.py:551
  197.7 8.7 %collective-permute-start.13 = (bf16[384,128]{1,0:T(8,128)(2,1)}, bf16[384,128]{1,0:T(8,128)(2,1)S(1)}, u32[]{:S(2)}, u32[]{:S(2)}) collective-permute-start(bf16[384,128]{1,0:T(8,128)(2,1)} %get-tuple-element.90), channel_id=1, source_target_pairs={{0,16},{4,20},{8,24},{12,28},{16,0},{20,4},{24,8},{28,12},{1,17},{... | collective-permute-start | bytes 294920 | tf_op jit(solution)/shard_map/ppermute | solution.py:551
  200.2 7.2 %collective-permute-start.14 = (bf16[384,128]{1,0:T(8,128)(2,1)}, bf16[384,128]{1,0:T(8,128)(2,1)S(1)}, u32[]{:S(2)}, u32[]{:S(2)}) collective-permute-start(bf16[384,128]{1,0:T(8,128)(2,1)} %get-tuple-element.92), channel_id=1, source_target_pairs={{0,16},{4,20},{8,24},{12,28},{16,0},{20,4},{24,8},{28,12},{1,17},{... | collective-permute-start | bytes 294920 | tf_op jit(solution)/shard_map/ppermute | solution.py:551
  209.9 7.8 %collective-permute-start.16 = (bf16[384,128]{1,0:T(8,128)(2,1)}, bf16[384,128]{1,0:T(8,128)(2,1)S(1)}, u32[]{:S(2)}, u32[]{:S(2)}) collective-permute-start(bf16[384,128]{1,0:T(8,128)(2,1)} %get-tuple-element.95.refs_0_), channel_id=1, source_target_pairs={{0,16},{4,20},{8,24},{12,28},{16,0},{20,4},{24,8},{28,12},{1,17},{... | collective-permute-start | bytes 294920 | tf_op jit(solution)/shard_map/ppermute | solution.py:551
  212.3 6.5 %collective-permute-start.17 = (bf16[384,128]{1,0:T(8,128)(2,1)}, bf16[384,128]{1,0:T(8,128)(2,1)S(1)}, u32[]{:S(2)}, u32[]{:S(2)}) collective-permute-start(bf16[384,128]{1,0:T(8,128)(2,1)} %get-tuple-element.96.refs_2_), channel_id=1, source_target_pairs={{0,16},{4,20},{8,24},{12,28},{16,0},{20,4},{24,8},{28,12},{1,17},{... | collective-permute-start | bytes 294920 | tf_op jit(solution)/shard_map/ppermute | solution.py:551
  221.3 14.5 %collective-permute-start.18 = (bf16[768,128]{1,0:T(8,128)(2,1)}, bf16[768,128]{1,0:T(8,128)(2,1)S(1)}, u32[]{:S(2)}, u32[]{:S(2)}) collective-permute-start(bf16[768,128]{1,0:T(8,128)(2,1)} %get-tuple-element.97.refs_0_), channel_id=1, source_target_pairs={{0,8},{4,12},{8,0},{12,4},{16,24},{20,28},{24,16},{28,20},{1,9},{5... | collective-permute-start | bytes 589832 | tf_op jit(solution)/shard_map/ppermute | solution.py:551
  222.9 12.9 %collective-permute-start.19 = (bf16[768,128]{1,0:T(8,128)(2,1)}, bf16[768,128]{1,0:T(8,128)(2,1)S(1)}, u32[]{:S(2)}, u32[]{:S(2)}) collective-permute-start(bf16[768,128]{1,0:T(8,128)(2,1)} %get-tuple-element.98.refs_2_), channel_id=1, source_target_pairs={{0,4},{4,0},{8,12},{12,8},{16,20},{20,16},{24,28},{28,24},{1,5},{5... | collective-permute-start | bytes 589832 | tf_op jit(solution)/shard_map/ppermute | solution.py:551
  239.3 10.6 %collective-permute-start.22 = (bf16[1536,128]{1,0:T(8,128)(2,1)}, bf16[1536,128]{1,0:T(8,128)(2,1)S(1)}, u32[]{:S(2)}, u32[]{:S(2)}) collective-permute-start(bf16[1536,128]{1,0:T(8,128)(2,1)} %get-tuple-element.101.refs_0_), channel_id=1, source_target_pairs={{0,4},{4,0},{8,12},{12,8},{16,20},{20,16},{24,28},{28,24},{1,5},{5... | collective-permute-start | bytes 1179656 | tf_op jit(solution)/shard_map/ppermute | solution.py:551
  241.0 8.9 %collective-permute-start.23 = (bf16[1536,128]{1,0:T(8,128)(2,1)}, bf16[1536,128]{1,0:T(8,128)(2,1)S(1)}, u32[]{:S(2)}, u32[]{:S(2)}) collective-permute-start(bf16[1536,128]{1,0:T(8,128)(2,1)} %get-tuple-element.102.refs_2_), channel_id=1, source_target_pairs={{0,8},{4,12},{8,0},{12,4},{16,24},{20,28},{24,16},{28,20},{1,9},{5... | collective-permute-start | bytes 1179656 | tf_op jit(solution)/shard_map/ppermute | solution.py:551
  241.2 8.7 %collective-permute-start.24 = (bf16[320,128]{1,0:T(8,128)(2,1)}, bf16[320,128]{1,0:T(8,128)(2,1)S(1)}, u32[]{:S(2)}, u32[]{:S(2)}) collective-permute-start(bf16[320,128]{1,0:T(8,128)(2,1)} %get-tuple-element.103.refs_4_), channel_id=1, source_target_pairs={{0,8},{4,12},{8,0},{12,4},{16,24},{20,28},{24,16},{28,20},{1,9},{5... | collective-permute-start | bytes 245768 | tf_op jit(solution)/shard_map/ppermute | solution.py:551
  262.0 9.9 %collective-permute-start.26 = (bf16[1280,128]{1,0:T(8,128)(2,1)}, bf16[1280,128]{1,0:T(8,128)(2,1)S(1)}, u32[]{:S(2)}, u32[]{:S(2)}) collective-permute-start(bf16[1280,128]{1,0:T(8,128)(2,1)} %shard_map.179.refs_0_), channel_id=1, source_target_pairs={{0,1},{1,0},{2,3},{3,2},{4,5},{5,4},{6,7},{7,6},{8,9},{9,8},{10,11... | collective-permute-start | bytes 983048 | tf_op jit(solution)/shard_map/ppermute | solution.py:551
  263.0 8.9 %collective-permute-start.27 = (bf16[960,128]{1,0:T(8,128)(2,1)S(1)}, bf16[960,128]{1,0:T(8,128)(2,1)S(1)}, u32[]{:S(2)}, u32[]{:S(2)}) collective-permute-start(bf16[960,128]{1,0:T(8,128)(2,1)S(1)} %slice.354.refs_2_), channel_id=1, source_target_pairs={{0,1},{1,0},{2,3},{3,2},{4,5},{5,4},{6,7},{7,6},{8,9},{9,8},{10,11... | collective-permute-start | bytes 737288 | tf_op jit(solution)/shard_map/ppermute | solution.py:551
  275.7 6.6 %collective-permute-start.28 = (bf16[2560,128]{1,0:T(8,128)(2,1)}, bf16[2560,128]{1,0:T(8,128)(2,1)S(1)}, u32[]{:S(2)}, u32[]{:S(2)}) collective-permute-start(bf16[2560,128]{1,0:T(8,128)(2,1)} %get-tuple-element.106.refs_0_), channel_id=1, source_target_pairs={{0,2},{2,0},{1,3},{3,1},{4,6},{6,4},{5,7},{7,5},{8,10},{10,8},{9,1... | collective-permute-start | bytes 1966088 | tf_op jit(solution)/shard_map/ppermute | solution.py:551
  (42 other events, 245.1 us)

commit v3 on v2

--- a/solution.py
+++ b/solution.py
@@ -472,94 +472,202 @@
     )
 
 
-def merge(flows):
-    turns = jnp.stack([jnp.int32(0) if bit is None else bit for _, bit in flows]).astype(jnp.int32)
-    counts = [len(terms) for terms, _ in flows]
-    splits = [bit is not None for _, bit in flows]
+VMEM_SPEC = pl.BlockSpec(memory_space=pltpu.VMEM)
+SMEM_SPEC = pl.BlockSpec(memory_space=pltpu.SMEM)
+
+
+def merge(where, flows):
     shapes = []
-    for (terms, _), split in zip(flows, splits):
-        rows = terms[0].shape[0] // (2 if split else 1)
-        shapes += [jax.ShapeDtypeStruct((rows, LANES), BF16)] * (2 if split else 1)
-
-    def kernel(turn_ref, *refs):
+    for _, _, rows, ways, _ in flows:
+        shapes += [jax.ShapeDtypeStruct((rows // ways, LANES), BF16)] * ways
+    counts = [len(flow[0]) for flow in flows]
+
+    def kernel(where_ref, *refs):
         ins, outs = refs[:sum(counts)], refs[sum(counts):]
-        for n, (count, split) in enumerate(zip(counts, splits)):
-            mine, ins = ins[:count], ins[count:]
-            for side in range(2 if split else 1):
+        for terms, first, rows, ways, slot in flows:
+            mine, ins = ins[:len(terms)], ins[len(terms):]
+            size = rows // ways
+            for k in range(ways):
                 out, outs = outs[0], outs[1:]
-                rows = out.shape[0]
-                if split:
-                    part = turn_ref[n] if side == 0 else 1 - turn_ref[n]
-                    span = pl.ds(pl.multiple_of(part * rows, 16), rows)
-                else:
-                    span = pl.ds(0, rows)
+                part = (where_ref[slot] ^ k) if ways > 1 else 0
+                span = pl.ds(pl.multiple_of(first + part * size, 16), size)
                 value = mine[0][span, :].astype(F32)
                 for ref in mine[1:]:
                     value += ref[span, :].astype(F32)
                 out[...] = value.astype(BF16)
 
-    vmem = pl.BlockSpec(memory_space=pltpu.VMEM)
-    operands = [term for terms, _ in flows for term in terms]
-    size = sum(term.size for term in operands)
+    operands = [term for flow in flows for term in flow[0]]
+    size = sum(flow[2] * LANES * len(flow[0]) for flow in flows)
     outs = pl.pallas_call(
         kernel,
-        in_specs=[pl.BlockSpec(memory_space=pltpu.SMEM)] + [vmem] * len(operands),
-        out_specs=[vmem] * len(shapes),
+        in_specs=[SMEM_SPEC] + [VMEM_SPEC] * len(operands),
+        out_specs=[VMEM_SPEC] * len(shapes),
         out_shape=shapes,
         cost_estimate=pl.CostEstimate(flops=size, bytes_accessed=3 * size, transcendentals=0),
-    )(turns, *operands)
+    )(where, *operands)
     result = []
-    for split in splits:
-        result.append(tuple(outs[:2]) if split else outs[0])
-        outs = outs[2 if split else 1:]
+    for flow in flows:
+        result.append(list(outs[:flow[3]]))
+        outs = outs[flow[3]:]
     return result
 
 
-def join(flows):
-    turns = jnp.stack([bit for _, _, bit in flows]).astype(jnp.int32)
-    shapes = [jax.ShapeDtypeStruct((2 * mine.shape[0], LANES), BF16) for mine, _, _ in flows]
-
-    def kernel(turn_ref, *refs):
-        ins, outs = refs[:2 * len(flows)], refs[2 * len(flows):]
-        for n, out in enumerate(outs):
-            rows = out.shape[0] // 2
-            out[pl.ds(pl.multiple_of(turn_ref[n] * rows, 16), rows), :] = ins[2 * n][...]
-            out[pl.ds(pl.multiple_of((1 - turn_ref[n]) * rows, 16), rows), :] = ins[2 * n + 1][...]
-
-    vmem = pl.BlockSpec(memory_space=pltpu.VMEM)
-    operands = [part for mine, arrived, _ in flows for part in (mine, arrived)]
+def put_parts(where_ref, parts, slot, out, first):
+    size = parts[0].shape[0]
+    for k, part in enumerate(parts):
+        at = first + (where_ref[slot] ^ k) * size
+        out[pl.ds(pl.multiple_of(at, 16), size), :] = part[...]
+
+
+def join(where, flows):
+    shapes = [jax.ShapeDtypeStruct((len(parts) * parts[0].shape[0], LANES), BF16) for parts, _ in flows]
+    operands = [part for parts, _ in flows for part in parts]
+
+    def kernel(where_ref, *refs):
+        ins, outs = refs[:len(operands)], refs[len(operands):]
+        for (parts, slot), out in zip(flows, outs):
+            put_parts(where_ref, ins[:len(parts)], slot, out, 0)
+            ins = ins[len(parts):]
+
     size = sum(part.size for part in operands)
     return pl.pallas_call(
         kernel,
-        in_specs=[pl.BlockSpec(memory_space=pltpu.SMEM)] + [vmem] * len(operands),
-        out_specs=[vmem] * len(shapes),
+        in_specs=[SMEM_SPEC] + [VMEM_SPEC] * len(operands),
+        out_specs=[VMEM_SPEC] * len(shapes),
         out_shape=shapes,
         cost_estimate=pl.CostEstimate(flops=0, bytes_accessed=4 * size, transcendentals=0),
-    )(turns, *operands)
-
-
-def bits(size):
-    out, bit = [], 1
+    )(where, *operands)
+
+
+def finish_ffn(where, flows, half_shape):
+    rows_half, cols_half = half_shape
+    operands = [part for parts, _ in flows for part in parts]
+    total = sum(part.shape[0] for part in operands)
+    used = 3 * rows_half * cols_half // LANES
+
+    def kernel(where_ref, *refs):
+        ins = refs[:len(operands)]
+        gate_ref, up_ref, down_ref, rest_ref, grads = refs[len(operands):]
+        first = 0
+        for parts, slot in flows:
+            put_parts(where_ref, ins[:len(parts)], slot, grads, first)
+            ins = ins[len(parts):]
+            first += len(parts) * parts[0].shape[0]
+        base = 0
+        for t, ref in enumerate((gate_ref, up_ref, down_ref)):
+            for part in range(cols_half // LANES):
+                tile = grads[base:base + rows_half, :].astype(F32)
+                if t < 2:
+                    ref[:, part * LANES:(part + 1) * LANES] = tile
+                else:
+                    ref[part * LANES:(part + 1) * LANES, :] = tile.T
+                base += rows_half
+        rest_ref[...] = grads[used:, :]
+
+    return pl.pallas_call(
+        kernel,
+        in_specs=[SMEM_SPEC] + [VMEM_SPEC] * len(operands),
+        out_specs=[VMEM_SPEC] * 4,
+        out_shape=[
+            jax.ShapeDtypeStruct((rows_half, cols_half), F32),
+            jax.ShapeDtypeStruct((rows_half, cols_half), F32),
+            jax.ShapeDtypeStruct((cols_half, rows_half), F32),
+            jax.ShapeDtypeStruct((total - used, LANES), BF16),
+        ],
+        scratch_shapes=[pltpu.VMEM((total, LANES), BF16)],
+        cost_estimate=pl.CostEstimate(flops=0, bytes_accessed=5 * 10**6, transcendentals=0),
+    )(where, *operands)
+
+
+def finish_shared(where, shared, rest, slot, width, columns):
+    operands = list(shared) + list(rest)
+    chunks = padded_width(width) // LANES
+    quarter = width // 4
+    per_half = round_up(columns, 2 * LANES) // 2 // LANES
+
+    def kernel(where_ref, s0, s1, r0, r1, qkv_ref, out_ref, one_ref, two_ref, s_all, r_all):
+        put_parts(where_ref, (s0, s1), slot, s_all, 0)
+        put_parts(where_ref, (r0, r1), slot, r_all, 0)
+        half_rows, quarter_rows = s0.shape[0], r0.shape[0] // 2
+        for half in range(2):
+            for part in range(per_half):
+                lane = (half * per_half + part) * LANES
+                base = half * half_rows + part * width
+                lanes = min(LANES, columns - lane)
+                if lanes > 0:
+                    qkv_ref[:, lane:lane + lanes] = s_all[base:base + width, :].astype(F32)[:, :lanes]
+        for n in range(4):
+            for part in range(chunks):
+                lanes = min(LANES, width - part * LANES)
+                base = n * quarter_rows + part * quarter
+                out_ref[n * quarter:(n + 1) * quarter, part * LANES:part * LANES + lanes] = (
+                    r_all[base:base + quarter, :].astype(F32)[:, :lanes]
+                )
+        for ref, source, first in ((one_ref, s_all, per_half * width), (two_ref, r_all, chunks * quarter)):
+            for part in range(chunks):
+                lanes = min(LANES, width - part * LANES)
+                base = first + 16 * part
+                total = jnp.sum(source[base:base + 16, :].astype(F32), axis=0, keepdims=True)
+                ref[:, part * LANES:part * LANES + lanes] = total[:, :lanes]
+
+    return pl.pallas_call(
+        kernel,
+        in_specs=[SMEM_SPEC] + [VMEM_SPEC] * 4,
+        out_specs=[VMEM_SPEC] * 4,
+        out_shape=[
+            jax.ShapeDtypeStruct((width, columns), F32),
+            jax.ShapeDtypeStruct((width, width), F32),
+            jax.ShapeDtypeStruct((1, width), F32),
+            jax.ShapeDtypeStruct((1, width), F32),
+        ],
+        scratch_shapes=[
+            pltpu.VMEM((2 * shared[0].shape[0], LANES), BF16),
+            pltpu.VMEM((2 * rest[0].shape[0], LANES), BF16),
+        ],
+        cost_estimate=pl.CostEstimate(flops=0, bytes_accessed=5 * 10**6, transcendentals=0),
+    )(where, *operands)
+
+
+def dp_stages(size):
+    masks, bit = [], 1
     while bit < size:
-        out.append(bit)
+        masks.append(bit)
         bit *= 2
-    return out
-
-
-def swap_with(data, axis, bit):
+    return [tuple(masks[:1])] + [tuple(masks[n:n + 2]) for n in range(1, len(masks), 2)]
+
+
+def swap_with(data, axis, mask):
     size = lax.axis_size(axis)
-    return lax.ppermute(data, axis, [(n, n ^ bit) for n in range(size)])
-
-
-def own_bit(axis, bit):
-    return (lax.axis_index(axis) // bit) % 2
+    return lax.ppermute(data, axis, [(n, n ^ mask) for n in range(size)])
+
+
+def stage_ways(stage):
+    return 2 ** len(stage[1])
+
+
+def stage_mask(stage, k):
+    return sum(bit for n, bit in enumerate(stage[1]) if k >> n & 1)
+
+
+def stage_index(stage):
+    index = lax.axis_index(stage[0])
+    return sum((index // bit % 2) * 2**n for n, bit in enumerate(stage[1]))
+
+
+def send_parts(parts, stage):
+    return [swap_with(parts[k], stage[0], stage_mask(stage, k)) for k in range(1, stage_ways(stage))]
+
+
+def spread_part(part, stage):
+    return [part] + [swap_with(part, stage[0], stage_mask(stage, k)) for k in range(1, stage_ways(stage))]
 
 
 def layer(inputs, seq_ids, norm_one, w_qkv, w_out, norm_two, w_gate, w_up, w_down, out_grad):
-    dp_bits = [("dp", bit) for bit in bits(lax.axis_size("dp"))]
-    stages = len(dp_bits)
     unit = 32 * lax.axis_size("dp")
     width = inputs.shape[1]
+    col, row = ("col", (1,)), ("row", (1,))
+    over_dp = [("dp", masks) for masks in dp_stages(lax.axis_size("dp"))]
+    slots = {stage: n for n, stage in enumerate([col, row] + over_dp)}
     own = jnp.stack([w_gate, w_up, w_down.T])
     side = swap_with(own, "col", 1)
     across = swap_with(own, "row", 1)
@@ -570,88 +678,79 @@
     q, k, v, lse, attended, middle = front(inputs, start, cosine, sine, gain_one, w_qkv, w_out)
     far = swap_with(side, "row", 1)
     selector = (jnp.arange(16)[:, None] == jnp.arange(width)[None, :] // HEAD).astype(BF16)
-    spot = jnp.stack([lax.axis_index("col"), lax.axis_index("row")]).astype(jnp.int32)
+    where = jnp.stack([stage_index(stage) for stage in slots]).astype(jnp.int32)
     outputs, middle_grad, do, delta, keep_keep, keep_send, send_keep, send_send = mlp(
-        unit, spot, middle, out_grad, attended, gain_two, w_out, own, side, across, far, selector
+        unit, where, middle, out_grad, attended, gain_two, w_out, own, side, across, far, selector
     )
     row_send = swap_with(send_send, "row", 1)
     row_keep = swap_with(send_keep, "row", 1)
-    (to_col,) = merge([((keep_send, row_send), None)])
+    tall = keep_keep.shape[0]
+    ((to_col,),) = merge(where, [((keep_send, row_send), 0, tall, 1, 0)])
     from_col = swap_with(to_col, "col", 1)
     input_grad, shared_keep, shared_send = back(
-        unit, spot, q, k, v, do, lse, delta, start, cosine, sine, inputs, middle_grad, gain_one, w_qkv
+        unit, where, q, k, v, do, lse, delta, start, cosine, sine, inputs, middle_grad, gain_one, w_qkv
     )
     shared_row = swap_with(shared_send, "row", 1)
 
-    half = keep_keep.shape[0] // 2
-    order_a = dp_bits
-    order_b = dp_bits[1:2] + dp_bits[:1] + dp_bits[2:]
-    order_s = [("col", 1)] + dp_bits
+    def flow(terms, first, rows, stage):
+        if stage is None:
+            return (terms, first, rows, 1, 0)
+        return (terms, first, rows, stage_ways(stage), slots[stage])
+
+    order_a = over_dp
+    order_b = over_dp[1:2] + over_dp[:1] + over_dp[2:]
+    order_s = [col] + over_dp
+    count = len(over_dp)
+    cut = round_up(2 * tall // 3, unit)
     terms = (keep_keep, row_keep, from_col)
-    halves = [tuple(term[at:at + half] for term in terms) for at in (0, half)]
-    (a, b) = merge([(halves[0], own_bit(*order_a[0])), (halves[1], own_bit(*order_b[0]))])
-    (s,) = merge([((shared_keep, shared_row), own_bit(*order_s[0]))])
-    for n in range(stages):
-        a_in = swap_with(a[1], *order_a[n])
-        b_in = swap_with(b[1], *order_b[n])
-        s_in = swap_with(s[1], *order_s[n])
-        last = n == stages - 1
+    a, b = merge(where, [flow(terms, 0, cut, order_a[0]), flow(terms, cut, tall - cut, order_b[0])])
+    rows_s = shared_keep.shape[0]
+    (s,) = merge(where, [flow((shared_keep, shared_row), 0, rows_s, order_s[0])])
+    for n in range(count):
+        a_in = send_parts(a, order_a[n])
+        b_in = send_parts(b, order_b[n])
+        s_in = send_parts(s, order_s[n])
+        more = n < count - 1
         a, b, s = merge(
+            where,
             [
-                ((a[0], a_in), None if last else own_bit(*order_a[n + 1])),
-                ((b[0], b_in), None if last else own_bit(*order_b[n + 1])),
-                ((s[0], s_in), own_bit(*order_s[n + 1])),
+                flow([a[0]] + a_in, 0, a[0].shape[0], order_a[n + 1] if more else None),
+                flow([b[0]] + b_in, 0, b[0].shape[0], order_b[n + 1] if more else None),
+                flow([s[0]] + s_in, 0, s[0].shape[0], order_s[n + 1]),
             ],
         )
-    for n in reversed(range(stages)):
-        a_in = swap_with(a, *order_a[n])
-        b_in = swap_with(b, *order_b[n])
-        pairs = [(a, a_in, own_bit(*order_a[n])), (b, b_in, own_bit(*order_b[n]))]
-        if n == stages - 1:
-            s_in = swap_with(s[1], *order_s[n + 1])
-            (s,) = merge([((s[0], s_in), None)])
+    a, b = a[0], b[0]
+    for n in reversed(range(count)):
+        a_parts = spread_part(a, order_a[n])
+        b_parts = spread_part(b, order_b[n])
+        if n == count - 1:
+            s_in = send_parts(s, order_s[count])
+            ((s,),) = merge(where, [flow([s[0]] + s_in, 0, s[0].shape[0], None)])
         else:
-            s_in = swap_with(s, *order_s[n + 2])
-            pairs.append((s, s_in, own_bit(*order_s[n + 2])))
-        joined = join(pairs)
-        a, b = joined[:2]
-        if n < stages - 1:
-            s = joined[2]
-    grads = jnp.concatenate([a, b], axis=0)
-    used = 3 * w_gate.size // LANES
-    rest = grads[used:]
-    for n in (1, 0):
-        s_in = swap_with(s, *order_s[n])
-        pairs = [(s, s_in, own_bit(*order_s[n]))]
-        if n == 0:
-            rest_in = swap_with(rest, "col", 1)
-            pairs.append((rest, rest_in, own_bit("col", 1)))
-        joined = join(pairs)
-        s = joined[0]
-    rest = joined[1]
-    s_in = swap_with(s, "row", 1)
-    rest_in = swap_with(rest, "row", 1)
-    row_bit = own_bit("row", 1)
-    s, rest = join([(s, s_in, row_bit), (rest, rest_in, row_bit)])
-
-    def flat(block, rows):
-        return jnp.concatenate([block[at:at + rows] for at in range(0, block.shape[0], rows)], axis=1)
-
-    chunks = padded_width(width) // LANES
-    s = s.reshape(2, -1, LANES)
-    reach = round_up(w_qkv.shape[1], 2 * LANES) // 2 // LANES * width
-    grad_qkv = jnp.concatenate([flat(s[0, :reach], width), flat(s[1, :reach], width)], axis=1)[:, :w_qkv.shape[1]].astype(F32)
-    grad_norm_one = jnp.sum(flat(s[0, reach:reach + 16 * chunks], 16)[:8, :width].astype(F32), axis=0)
-    rest = rest.reshape(4, -1, LANES)
-    quarter = width // 4
-    reach = chunks * quarter
-    grad_out = jnp.concatenate([flat(rest[n, :reach], quarter)[:, :width] for n in range(4)], axis=0).astype(F32)
-    grad_norm_two = jnp.sum(flat(rest[0, reach:reach + 16 * chunks], 16)[:8, :width].astype(F32), axis=0)
-    grads = grads[:used].reshape(3, -1, w_gate.shape[0], LANES).astype(F32)
-    grad_gate = grads[0].transpose(1, 0, 2).reshape(w_gate.shape)
-    grad_up = grads[1].transpose(1, 0, 2).reshape(w_up.shape)
-    grad_down = grads[2].transpose(0, 2, 1).reshape(w_down.shape)
-    return (outputs, input_grad, grad_norm_one, grad_qkv, grad_out, grad_norm_two, grad_gate, grad_up, grad_down)
+            s_parts = spread_part(s, order_s[n + 2])
+        flows = [(a_parts, slots[order_a[n]]), (b_parts, slots[order_b[n]])]
+        if n > 0:
+            if n < count - 1:
+                a, b, s = join(where, flows + [(s_parts, slots[order_s[n + 2]])])
+            else:
+                a, b = join(where, flows)
+        else:
+            grad_gate, grad_up, grad_down, rest = finish_ffn(where, flows, w_gate.shape)
+            if n < count - 1:
+                (s,) = join(where, [(s_parts, slots[order_s[n + 2]])])
+    rest_parts = spread_part(rest, col)
+    s_parts = spread_part(s, order_s[1])
+    (s,) = join(where, [(s_parts, slots[order_s[1]])])
+    s_parts = spread_part(s, col)
+    s, rest = join(where, [(s_parts, slots[col]), (rest_parts, slots[col])])
+    s_parts = spread_part(s, row)
+    rest_parts = spread_part(rest, row)
+    grad_qkv, grad_out, grad_norm_one, grad_norm_two = finish_shared(
+        where, s_parts, rest_parts, slots[row], width, w_qkv.shape[1]
+    )
+    return (
+        outputs, input_grad, grad_norm_one[0], grad_qkv, grad_out, grad_norm_two[0], grad_gate, grad_up, grad_down
+    )
 
 
 def solution(mesh):

time: 308 us -> 285 us (0.925)
  local copies, waits for them, and re-layouts: 49.7 us -> 23.3 us
  starting transfers between devices: 33.5 us -> 42.3 us
  other arithmetic: 16.8 us -> 10.2 us
    unnamed x98 -> x79, local copies, waits for them, and re-layouts: 37 us -> 21.5 us
    ppermute x30 -> x36, starting transfers between devices: 33.5 us -> 42.3 us  [swap_with(): return lax.ppermute(data, axis, [(n, n ^ mask) for n in range(size)])]
    slice x6 -> x1, local copies, waits for them, and re-layouts: 6.3 us -> 0.07 us  [the longest x3 5.09 us: layer(): halves = [tuple((term[at:at + half] for term in terms)) for at in (0, half)]]
    another operation x11 -> x3, other arithmetic: 5.89 us -> 0.97 us  [the longest x1 0.66 us: layer(): where = jnp.stack([stage_index(stage) for stage in slots]).astype(jnp.int32)]
    ppermute x30 -> x36, waiting for transfers between devices: 70.8 us -> 72.1 us  [swap_with(): return lax.ppermute(data, axis, [(n, n ^ mask) for n in range(size)])]
    pallas_call x13 -> x12, Pallas kernels: 31.5 us -> 32.2 us  [the longest x6 17.4 us: merge(): pl.pallas_call(kernel, in_specs=[SMEM_SPEC] + [VMEM_SPEC] * len(operands)...]
  transfers between devices with their start and end apart: 30 -> 36, of which waited for: 14 -> 17; matrix products, arithmetic and copies ran while one was open for 11% -> 7% of each run, Pallas kernels for 24% -> 28%
where the time goes in v3:
time: 285 us; the launch traced here: 284 us
  Pallas kernels  135 us (47%)
  waiting for transfers between devices  72.1 us (25%)
  starting transfers between devices  42.3 us (15%)
  local copies, waits for them, and re-layouts  23.3 us (8%)
  other arithmetic  10.2 us (4%)
    ppermute x36, waiting for transfers between devices, swap_with(): return lax.ppermute(data, axis, [(n, n ^ mask) for n in range(size)])  72.1 us
    ppermute x36, starting transfers between devices, swap_with(): return lax.ppermute(data, axis, [(n, n ^ mask) for n in range(size)])  42.3 us
    pallas_call x1, Pallas kernels, mlp(): pl.pallas_call(mlp_kernel, grid=(blocks,), in_specs=[pl.BlockSpec(memory_...  41.6 us
    pallas_call x1, Pallas kernels, back(): pl.pallas_call(back_kernel, grid=(blocks,), in_specs=[pl.BlockSpec(memory...  32.3 us
    pallas_call x1, Pallas kernels, front(): pl.pallas_call(front_kernel, grid=(blocks,), in_specs=[pl.BlockSpec((BLOC...  28.8 us
    unnamed x79, local copies, waits for them, and re-layouts  21.5 us
    pallas_call x6, Pallas kernels, merge(): pl.pallas_call(kernel, in_specs=[SMEM_SPEC] + [VMEM_SPEC] * len(operands)...  17.4 us
    pallas_call x4, Pallas kernels, join(): pl.pallas_call(kernel, in_specs=[SMEM_SPEC] + [VMEM_SPEC] * len(operands)...  7.73 us
  transfers between devices with their start and end apart: 36, of which 17 were waited for; matrix products, arithmetic and copies ran while one was open for 7% of the time, Pallas kernels for 28%

profile of v3, /device:TPU:0, one launch (start us, length us, event | category | flops | bytes accessed | tf_op | source)
XLA Modules:
  0.0 284.4 jit_solution(7017740923521020650)
XLA Ops:
  2.2 3.1 %collective-permute-start = (bf16[3,288,768]{2,1,0:T(8,128)(2,1)S(1)}, bf16[3,288,768]{2,1,0:T(8,128)(2,1)}, u32[]{:S(2)}, u32[]{:S(2)}) collective-permute-start(bf16[3,288,768]{2,1,0:T(8,128)(2,1)S(1)} %pad_maximum_fusion.own_ref), channel_id=1, source_target_pairs={{0,1},{1,0},{2,3},{3,2},{4,5},{5,4},{6,7},{7,6},{8,9},{9,8},{10,11... | collective-permute-start | bytes 3981320 | tf_op jit(solution)/shard_map/ppermute | solution.py:641
  7.7 26.8 %collective-permute-done.side_ref = bf16[3,288,768]{2,1,0:T(8,128)(2,1)} collective-permute-done((bf16[3,288,768]{2,1,0:T(8,128)(2,1)S(1)}, bf16[3,288,768]{2,1,0:T(8,128)(2,1)}, u32[]{:S(2)}, u32[]{:S(2)}) %collective-permute-start) | collective-permute-done | bytes 1327136 | tf_op jit(solution)/shard_map/ppermute | solution.py:641
  44.6 28.8 %front.1 = (bf16[9,1024,64]{2,1,0:T(8,128)(2,1)}, bf16[3,1024,64]{2,1,0:T(8,128)(2,1)}, bf16[3,1024,64]{2,1,0:T(8,128)(2,1)}, f32[16,1024]{1,0:T(8,128)}, bf16[1...) custom-call(bf16[1024,576]{1,0:T(8,128)(2,1)} %copy.32.inputs_ref, s32[1,1024]{1,0:T(1,128)} %bitcast.21, ...), custom_call_target="tpu_custom_call" | custom-call | flops 6000000000 | bytes 12000000 | tf_op jit(solution)/shard_map/front/pallas_call | solution.py:126
  73.4 41.6 %mlp.1 = (bf16[1024,576]{1,0:T(8,128)(2,1)}, f32[1024,576]{1,0:T(8,128)}, bf16[9,1024,64]{2,1,0:T(8,128)(2,1)}, f32[16,1024]{1,0:T(8,128)}, bf16[6144,128]{1,0:T...) custom-call(s32[4]{0:T(128)} %pad_add_fusion.place_ref.where_ref, ...), custom_call_target="tpu_custom_call" | custom-call | flops 17999998976 | bytes 24000000 | tf_op jit(solution)/shard_map/mlp/pallas_call | solution.py:277
  115.7 3.2 %collective-permute-done.4.refs_1_ = bf16[6144,128]{1,0:T(8,128)(2,1)S(1)} collective-permute-done((bf16[6144,128]{1,0:T(8,128)(2,1)}, bf16[6144,128]{1,0:T(8,128)(2,1)S(1)}, u32[]{:S(2)}, u32[]{:S(2)}) %collective-permute-start.4) | collective-permute-done | bytes 1572896 | tf_op jit(solution)/shard_map/ppermute | solution.py:641
  120.0 3.4 %shard_map.169 = bf16[6144,128]{1,0:T(8,128)(2,1)} custom-call(s32[4]{0:T(128)} %pad_add_fusion.place_ref.where_ref, bf16[6144,128]{1,0:T(8,128)(2,1)} %get-tuple-element.73.refs_0_, bf16[6144,128]{1,0:T(8,128)(2,1)} %copy-done.3), custom_call_target="tpu_custom_call" | custom-call | flops 1572864 | bytes 4718592 | tf_op jit(solution)/shard_map/pallas_call | solution.py:501
  125.2 32.3 %back.1 = (f32[1024,576]{1,0:T(8,128)}, bf16[2560,128]{1,0:T(8,128)(2,1)}, bf16[2560,128]{1,0:T(8,128)(2,1)}) custom-call(s32[4]{0:T(128)} %pad_add_fusion.place_ref.where_ref, bf16[9,1024,64]{2,1,0:T(8,128)(2,1)} %get-tuple-element.63.q_ref, bf16[3,1024,64]{2,1,0:T(8,128)(2,1)} %get-tuple-element.64.k_ref, bf16[3,1024,64]{2,1,0:T(8,128)(2,1)} %get-tuple-element.65.v_ref, ...), custom_call_target="tpu_custom_call" | custom-call | flops 8000000000 | bytes 16000000 | tf_op jit(solution)/shard_map/back/pallas_call | solution.py:416
  157.7 2.7 collective-permute-done.5.refs_2_.refs_5_
  161.5 5.6 %shard_map.170 = (bf16[2048,128]{1,0:T(8,128)(2,1)}, bf16[2048,128]{1,0:T(8,128)(2,1)}, bf16[512,128]{1,0:T(8,128)(2,1)}, bf16[512,128]{1,0:T(8,128)(2,1)}, bf16...) custom-call(s32[4]{0:T(128)} %pad_add_fusion.place_ref.where_ref, bf16[6144,128]{1,0:T(8,128)(2,1)} %get-tuple-element.71.refs_0_.refs_3_, ...), custom_call_target="tpu_custom_call" | custom-call | flops 2359296 | bytes 7077888 | tf_op jit(solution)/shard_map/pallas_call | solution.py:501
  174.1 2.6 collective-permute-start.8
  176.9 3.2 %collective-permute-done.11.refs_7_ = bf16[1280,128]{1,0:T(8,128)(2,1)S(1)} collective-permute-done((bf16[1280,128]{1,0:T(8,128)(2,1)}, bf16[1280,128]{1,0:T(8,128)(2,1)S(1)}, u32[]{:S(2)}, u32[]{:S(2)}) %collective-permute-start.11) | collective-permute-done | bytes 327712 | tf_op jit(solution)/shard_map/ppermute | solution.py:641
  180.0 6.3 %collective-permute-done.8.refs_4_ = bf16[512,128]{1,0:T(8,128)(2,1)S(1)} collective-permute-done((bf16[512,128]{1,0:T(8,128)(2,1)}, bf16[512,128]{1,0:T(8,128)(2,1)S(1)}, u32[]{:S(2)}, u32[]{:S(2)}) %collective-permute-start.8) | collective-permute-done | bytes 131104 | tf_op jit(solution)/shard_map/ppermute | solution.py:641
  187.2 2.6 shard_map.172
  196.2 3.0 %collective-permute-done.15.refs_5_ = bf16[256,128]{1,0:T(8,128)(2,1)S(1)} collective-permute-done((bf16[256,128]{1,0:T(8,128)(2,1)}, bf16[256,128]{1,0:T(8,128)(2,1)S(1)}, u32[]{:S(2)}, u32[]{:S(2)}) %collective-permute-start.15) | collective-permute-done | bytes 65568 | tf_op jit(solution)/shard_map/ppermute | solution.py:641
  199.2 4.3 %collective-permute-done.13.refs_2_ = bf16[512,128]{1,0:T(8,128)(2,1)S(1)} collective-permute-done((bf16[512,128]{1,0:T(8,128)(2,1)}, bf16[512,128]{1,0:T(8,128)(2,1)S(1)}, u32[]{:S(2)}, u32[]{:S(2)}) %collective-permute-start.13) | collective-permute-done | bytes 131104 | tf_op jit(solution)/shard_map/ppermute | solution.py:641
  212.3 3.0 %collective-permute-done.28.refs_5_ = bf16[256,128]{1,0:T(8,128)(2,1)S(1)} collective-permute-done((bf16[256,128]{1,0:T(8,128)(2,1)}, bf16[256,128]{1,0:T(8,128)(2,1)S(1)}, u32[]{:S(2)}, u32[]{:S(2)}) %collective-permute-start.28) | collective-permute-done | bytes 65568 | tf_op jit(solution)/shard_map/ppermute | solution.py:641
  215.3 4.0 %collective-permute-done.26.refs_2_ = bf16[512,128]{1,0:T(8,128)(2,1)S(1)} collective-permute-done((bf16[512,128]{1,0:T(8,128)(2,1)}, bf16[512,128]{1,0:T(8,128)(2,1)S(1)}, u32[]{:S(2)}, u32[]{:S(2)}) %collective-permute-start.26) | collective-permute-done | bytes 131104 | tf_op jit(solution)/shard_map/ppermute | solution.py:641
  224.1 3.1 %collective-permute-start.18 = (bf16[160,128]{1,0:T(8,128)(2,1)}, bf16[160,128]{1,0:T(8,128)(2,1)S(1)}, u32[]{:S(2)}, u32[]{:S(2)}) collective-permute-start(bf16[160,128]{1,0:T(8,128)(2,1)} %get-tuple-element.95), channel_id=1, source_target_pairs={{0,16},{4,20},{8,24},{12,28},{16,0},{20,4},{24,8},{28,12},{1,17},{... | collective-permute-start | bytes 122888 | tf_op jit(solution)/shard_map/ppermute | solution.py:641
  229.4 3.8 %collective-permute-done.19.refs_3_ = bf16[160,128]{1,0:T(8,128)(2,1)S(1)} collective-permute-done((bf16[160,128]{1,0:T(8,128)(2,1)}, bf16[160,128]{1,0:T(8,128)(2,1)S(1)}, u32[]{:S(2)}, u32[]{:S(2)}) %collective-permute-start.19) | collective-permute-done | bytes 40992 | tf_op jit(solution)/shard_map/ppermute | solution.py:641
  236.6 3.1 %collective-permute-start.20 = (bf16[160,128]{1,0:T(8,128)(2,1)}, bf16[160,128]{1,0:T(8,128)(2,1)S(1)}, u32[]{:S(2)}, u32[]{:S(2)}) collective-permute-start(bf16[160,128]{1,0:T(8,128)(2,1)} %shard_map.174.refs_0_), channel_id=1, source_target_pairs={{0,8},{4,12},{8,0},{12,4},{16,24},{20,28},{24,16},{28,20},{1,9},{5... | collective-permute-start | bytes 122888 | tf_op jit(solution)/shard_map/ppermute | solution.py:641
  256.9 3.4 %shard_map.178 = (f32[288,768]{1,0:T(8,128)}, f32[288,768]{1,0:T(8,128)}, f32[768,288]{1,0:T(8,128)}, bf16[960,128]{1,0:T(8,128)(2,1)}) custom-call(s32[4]{0:T(128)} %pad_add_fusion.place_ref.where_ref, bf16[2048,128]{1,0:T(8,128)(2,1)} %get-tuple-element.99.refs_0_, bf16[2048,128]{1,0:T(8,128)(2,1)} %copy-done.8, ...), custom_call_target="tpu_custom_call" | custom-call | bytes 5000000 | tf_op jit(solution)/shard_map/pallas_call | solution.py:567
  262.9 3.8 %collective-permute-done.33.refs_3_ = bf16[960,128]{1,0:T(8,128)(2,1)S(1)} collective-permute-done((bf16[960,128]{1,0:T(8,128)(2,1)}, bf16[960,128]{1,0:T(8,128)(2,1)S(1)}, u32[]{:S(2)}, u32[]{:S(2)}) %collective-permute-start.33) | collective-permute-done | bytes 245792 | tf_op jit(solution)/shard_map/ppermute | solution.py:641
  274.7 2.5 copy.37
  278.2 3.7 %shard_map.180 = (f32[576,960]{1,0:T(8,128)}, f32[576,576]{1,0:T(8,128)}, f32[1,576]{1,0:T(1,128)}, f32[1,576]{1,0:T(1,128)}) custom-call(s32[4]{0:T(128)} %pad_add_fusion.place_ref.where_ref, bf16[2560,128]{1,0:T(8,128)(2,1)} %get-tuple-element.102.s0, bf16[2560,128]{1,0:T(8,128)(2,1)} %copy-done.6, bf16[1920,128]{1,0:T(8,128)(2,1)} %get-tuple-element.103.r0, ...), custom_call_target="tpu_custom_call" | custom-call | bytes 5000000 | tf_op jit(solution)/shard_map/pallas_call | solution.py:613
  (160 shorter events, 83.2 us)
Async XLA Ops:
  2.2 32.3 %collective-permute-start = (bf16[3,288,768]{2,1,0:T(8,128)(2,1)S(1)}, bf16[3,288,768]{2,1,0:T(8,128)(2,1)}, u32[]{:S(2)}, u32[]{:S(2)}) collective-permute-start(bf16[3,288,768]{2,1,0:T(8,128)(2,1)S(1)} %pad_maximum_fusion.own_ref), channel_id=1, source_target_pairs={{0,1},{1,0},{2,3},{3,2},{4,5},{5,4},{6,7},{7,6},{8,9},{9,8},{10,11... | collective-permute-start | bytes 3981320 | tf_op jit(solution)/shard_map/ppermute | solution.py:641
  5.3 68.1 %collective-permute-start.1 = (bf16[3,288,768]{2,1,0:T(8,128)(2,1)S(1)}, bf16[3,288,768]{2,1,0:T(8,128)(2,1)}, u32[]{:S(2)}, u32[]{:S(2)}) collective-permute-start(bf16[3,288,768]{2,1,0:T(8,128)(2,1)S(1)} %pad_maximum_fusion.own_ref), channel_id=1, source_target_pairs={{0,2},{2,0},{1,3},{3,1},{4,6},{6,4},{5,7},{7,5},{8,10},{10,8},{9,1... | collective-permute-start | bytes 3981320 | tf_op jit(solution)/shard_map/ppermute | solution.py:641
  34.5 38.9 %collective-permute-start.2 = (bf16[3,288,768]{2,1,0:T(8,128)(2,1)}, bf16[3,288,768]{2,1,0:T(8,128)(2,1)}, u32[]{:S(2)}, u32[]{:S(2)}) collective-permute-start(bf16[3,288,768]{2,1,0:T(8,128)(2,1)} %collective-permute-done.side_ref), channel_id=1, source_target_pairs={{0,2},{2,0},{1,3},{3,1},{4,6},{6,4},{5,7},{7,5},{8,10},{10,8},{9,1... | collective-permute-start | bytes 3981320 | tf_op jit(solution)/shard_map/ppermute | solution.py:641
  115.6 42.1 %collective-permute-start.3 = (bf16[6144,128]{1,0:T(8,128)(2,1)}, bf16[6144,128]{1,0:T(8,128)(2,1)S(1)}, u32[]{:S(2)}, u32[]{:S(2)}) collective-permute-start(bf16[6144,128]{1,0:T(8,128)(2,1)} %get-tuple-element.72), channel_id=1, source_target_pairs={{0,2},{2,0},{1,3},{3,1},{4,6},{6,4},{5,7},{7,5},{8,10},{10,8},{9,1... | collective-permute-start | bytes 4718600 | tf_op jit(solution)/shard_map/ppermute | solution.py:641
  123.4 36.9 %collective-permute-start.5 = (bf16[6144,128]{1,0:T(8,128)(2,1)}, bf16[6144,128]{1,0:T(8,128)(2,1)S(1)}, u32[]{:S(2)}, u32[]{:S(2)}) collective-permute-start(bf16[6144,128]{1,0:T(8,128)(2,1)} %shard_map.169), channel_id=1, source_target_pairs={{0,1},{1,0},{2,3},{3,2},{4,5},{5,4},{6,7},{7,6},{8,9},{9,8},{10,11... | collective-permute-start | bytes 4718600 | tf_op jit(solution)/shard_map/ppermute | solution.py:641
  157.4 11.3 %collective-permute-start.10 = (bf16[2560,128]{1,0:T(8,128)(2,1)}, bf16[2560,128]{1,0:T(8,128)(2,1)}, u32[]{:S(2)}, u32[]{:S(2)}) collective-permute-start(bf16[2560,128]{1,0:T(8,128)(2,1)} %get-tuple-element.82), channel_id=1, source_target_pairs={{0,2},{2,0},{1,3},{3,1},{4,6},{6,4},{5,7},{7,5},{8,10},{10,8},{9,1... | collective-permute-start | bytes 1966088 | tf_op jit(solution)/shard_map/ppermute | solution.py:641
  167.0 19.3 %collective-permute-start.6 = (bf16[2048,128]{1,0:T(8,128)(2,1)}, bf16[2048,128]{1,0:T(8,128)(2,1)S(1)}, u32[]{:S(2)}, u32[]{:S(2)}) collective-permute-start(bf16[2048,128]{1,0:T(8,128)(2,1)} %get-tuple-element.76), channel_id=1, source_target_pairs={{0,4},{4,0},{8,12},{12,8},{16,20},{20,16},{24,28},{28,24},{1,5},{5... | collective-permute-start | bytes 1572872 | tf_op jit(solution)/shard_map/ppermute | solution.py:641
  171.0 9.1 %collective-permute-start.11 = (bf16[1280,128]{1,0:T(8,128)(2,1)}, bf16[1280,128]{1,0:T(8,128)(2,1)S(1)}, u32[]{:S(2)}, u32[]{:S(2)}) collective-permute-start(bf16[1280,128]{1,0:T(8,128)(2,1)} %get-tuple-element.84), channel_id=1, source_target_pairs={{0,1},{1,0},{2,3},{3,2},{4,5},{5,4},{6,7},{7,6},{8,9},{9,8},{10,11... | collective-permute-start | bytes 983048 | tf_op jit(solution)/shard_map/ppermute | solution.py:641
  172.5 7.6 %collective-permute-start.7 = (bf16[512,128]{1,0:T(8,128)(2,1)}, bf16[512,128]{1,0:T(8,128)(2,1)S(1)}, u32[]{:S(2)}, u32[]{:S(2)}) collective-permute-start(bf16[512,128]{1,0:T(8,128)(2,1)} %get-tuple-element.78), channel_id=1, source_target_pairs={{0,8},{4,12},{8,0},{12,4},{16,24},{20,28},{24,16},{28,20},{1,9},{5... | collective-permute-start | bytes 393224 | tf_op jit(solution)/shard_map/ppermute | solution.py:641
  174.1 12.3 %collective-permute-start.8 = (bf16[512,128]{1,0:T(8,128)(2,1)}, bf16[512,128]{1,0:T(8,128)(2,1)S(1)}, u32[]{:S(2)}, u32[]{:S(2)}) collective-permute-start(bf16[512,128]{1,0:T(8,128)(2,1)} %get-tuple-element.79), channel_id=1, source_target_pairs={{0,16},{4,20},{8,24},{12,28},{16,0},{20,4},{24,8},{28,12},{1,17},{... | collective-permute-start | bytes 393224 | tf_op jit(solution)/shard_map/ppermute | solution.py:641
  176.6 9.7 %collective-permute-start.9 = (bf16[512,128]{1,0:T(8,128)(2,1)}, bf16[512,128]{1,0:T(8,128)(2,1)S(1)}, u32[]{:S(2)}, u32[]{:S(2)}) collective-permute-start(bf16[512,128]{1,0:T(8,128)(2,1)} %get-tuple-element.80), channel_id=1, source_target_pairs={{0,24},{4,28},{8,16},{12,20},{16,8},{20,12},{24,0},{28,4},{1,25},{... | collective-permute-start | bytes 393224 | tf_op jit(solution)/shard_map/ppermute | solution.py:641
  189.8 13.7 %collective-permute-start.16 = (bf16[640,128]{1,0:T(8,128)(2,1)}, bf16[640,128]{1,0:T(8,128)(2,1)S(1)}, u32[]{:S(2)}, u32[]{:S(2)}) collective-permute-start(bf16[640,128]{1,0:T(8,128)(2,1)} %get-tuple-element.92), channel_id=1, source_target_pairs={{0,4},{4,0},{8,12},{12,8},{16,20},{20,16},{24,28},{28,24},{1,5},{5... | collective-permute-start | bytes 491528 | tf_op jit(solution)/shard_map/ppermute | solution.py:641
  190.4 8.9 %collective-permute-start.12 = (bf16[512,128]{1,0:T(8,128)(2,1)}, bf16[512,128]{1,0:T(8,128)(2,1)S(1)}, u32[]{:S(2)}, u32[]{:S(2)}) collective-permute-start(bf16[512,128]{1,0:T(8,128)(2,1)} %get-tuple-element.86), channel_id=1, source_target_pairs={{0,8},{4,12},{8,0},{12,4},{16,24},{20,28},{24,16},{28,20},{1,9},{5... | collective-permute-start | bytes 393224 | tf_op jit(solution)/shard_map/ppermute | solution.py:641
  192.3 11.3 %collective-permute-start.13 = (bf16[512,128]{1,0:T(8,128)(2,1)}, bf16[512,128]{1,0:T(8,128)(2,1)S(1)}, u32[]{:S(2)}, u32[]{:S(2)}) collective-permute-start(bf16[512,128]{1,0:T(8,128)(2,1)} %get-tuple-element.87), channel_id=1, source_target_pairs={{0,16},{4,20},{8,24},{12,28},{16,0},{20,4},{24,8},{28,12},{1,17},{... | collective-permute-start | bytes 393224 | tf_op jit(solution)/shard_map/ppermute | solution.py:641
  193.4 10.2 %collective-permute-start.14 = (bf16[512,128]{1,0:T(8,128)(2,1)}, bf16[512,128]{1,0:T(8,128)(2,1)S(1)}, u32[]{:S(2)}, u32[]{:S(2)}) collective-permute-start(bf16[512,128]{1,0:T(8,128)(2,1)} %get-tuple-element.88), channel_id=1, source_target_pairs={{0,24},{4,28},{8,16},{12,20},{16,8},{20,12},{24,0},{28,4},{1,25},{... | collective-permute-start | bytes 393224 | tf_op jit(solution)/shard_map/ppermute | solution.py:641
  206.4 8.9 %collective-permute-start.27 = (bf16[512,128]{1,0:T(8,128)(2,1)}, bf16[512,128]{1,0:T(8,128)(2,1)S(1)}, u32[]{:S(2)}, u32[]{:S(2)}) collective-permute-start(bf16[512,128]{1,0:T(8,128)(2,1)} %get-tuple-element.97.refs_0_), channel_id=1, source_target_pairs={{0,24},{4,28},{8,16},{12,20},{16,8},{20,12},{24,0},{28,4},{1,25},{... | collective-permute-start | bytes 393224 | tf_op jit(solution)/shard_map/ppermute | solution.py:641
  208.5 10.8 %collective-permute-start.26 = (bf16[512,128]{1,0:T(8,128)(2,1)}, bf16[512,128]{1,0:T(8,128)(2,1)S(1)}, u32[]{:S(2)}, u32[]{:S(2)}) collective-permute-start(bf16[512,128]{1,0:T(8,128)(2,1)} %get-tuple-element.97.refs_0_), channel_id=1, source_target_pairs={{0,16},{4,20},{8,24},{12,28},{16,0},{20,4},{24,8},{28,12},{1,17},{... | collective-permute-start | bytes 393224 | tf_op jit(solution)/shard_map/ppermute | solution.py:641
  209.9 9.4 %collective-permute-start.25 = (bf16[512,128]{1,0:T(8,128)(2,1)}, bf16[512,128]{1,0:T(8,128)(2,1)S(1)}, u32[]{:S(2)}, u32[]{:S(2)}) collective-permute-start(bf16[512,128]{1,0:T(8,128)(2,1)} %get-tuple-element.97.refs_0_), channel_id=1, source_target_pairs={{0,8},{4,12},{8,0},{12,4},{16,24},{20,28},{24,16},{28,20},{1,9},{5... | collective-permute-start | bytes 393224 | tf_op jit(solution)/shard_map/ppermute | solution.py:641
  222.6 32.8 %collective-permute-start.29 = (bf16[2048,128]{1,0:T(8,128)(2,1)}, bf16[2048,128]{1,0:T(8,128)(2,1)S(1)}, u32[]{:S(2)}, u32[]{:S(2)}) collective-permute-start(bf16[2048,128]{1,0:T(8,128)(2,1)} %get-tuple-element.99.refs_0_), channel_id=1, source_target_pairs={{0,4},{4,0},{8,12},{12,8},{16,20},{20,16},{24,28},{28,24},{1,5},{5... | collective-permute-start | bytes 1572872 | tf_op jit(solution)/shard_map/ppermute | solution.py:641
  245.6 7.9 %collective-permute-start.32 = (bf16[512,128]{1,0:T(8,128)(2,1)}, bf16[512,128]{1,0:T(8,128)(2,1)S(1)}, u32[]{:S(2)}, u32[]{:S(2)}) collective-permute-start(bf16[512,128]{1,0:T(8,128)(2,1)} %get-tuple-element.100.refs_2_), channel_id=1, source_target_pairs={{0,24},{4,28},{8,16},{12,20},{16,8},{20,12},{24,0},{28,4},{1,25},{... | collective-permute-start | bytes 393224 | tf_op jit(solution)/shard_map/ppermute | solution.py:641
  247.5 7.9 %collective-permute-start.31 = (bf16[512,128]{1,0:T(8,128)(2,1)}, bf16[512,128]{1,0:T(8,128)(2,1)S(1)}, u32[]{:S(2)}, u32[]{:S(2)}) collective-permute-start(bf16[512,128]{1,0:T(8,128)(2,1)} %get-tuple-element.100.refs_2_), channel_id=1, source_target_pairs={{0,16},{4,20},{8,24},{12,28},{16,0},{20,4},{24,8},{28,12},{1,17},{... | collective-permute-start | bytes 393224 | tf_op jit(solution)/shard_map/ppermute | solution.py:641
  253.0 9.9 %collective-permute-start.24 = (bf16[1280,128]{1,0:T(8,128)(2,1)}, bf16[1280,128]{1,0:T(8,128)(2,1)S(1)}, u32[]{:S(2)}, u32[]{:S(2)}) collective-permute-start(bf16[1280,128]{1,0:T(8,128)(2,1)} %shard_map.176.refs_0_), channel_id=1, source_target_pairs={{0,1},{1,0},{2,3},{3,2},{4,5},{5,4},{6,7},{7,6},{8,9},{9,8},{10,11... | collective-permute-start | bytes 983048 | tf_op jit(solution)/shard_map/ppermute | solution.py:641
  269.9 7.4 %collective-permute-start.34 = (bf16[2560,128]{1,0:T(8,128)(2,1)}, bf16[2560,128]{1,0:T(8,128)(2,1)S(1)}, u32[]{:S(2)}, u32[]{:S(2)}) collective-permute-start(bf16[2560,128]{1,0:T(8,128)(2,1)} %get-tuple-element.102.s0), channel_id=1, source_target_pairs={{0,2},{2,0},{1,3},{3,1},{4,6},{6,4},{5,7},{7,5},{8,10},{10,8},{9,1... | collective-permute-start | bytes 1966088 | tf_op jit(solution)/shard_map/ppermute | solution.py:641
  269.9 7.4 %collective-permute-start.35 = (bf16[1920,128]{1,0:T(8,128)(2,1)}, bf16[1920,128]{1,0:T(8,128)(2,1)}, u32[]{:S(2)}, u32[]{:S(2)}) collective-permute-start(bf16[1920,128]{1,0:T(8,128)(2,1)} %get-tuple-element.103.r0), channel_id=1, source_target_pairs={{0,2},{2,0},{1,3},{3,1},{4,6},{6,4},{5,7},{7,5},{8,10},{10,8},{9,1... | collective-permute-start | bytes 1474568 | tf_op jit(solution)/shard_map/ppermute | solution.py:641
  (49 other events, 277.6 us)

commit v4 on v3

--- a/solution.py
+++ b/solution.py
@@ -208,7 +208,7 @@
         acc3[0, :, at] += dot_nn(normed_t, gate_low)
         acc3[1, :, at] += dot_nn(normed_t, up_low)
         acc3[2, :, at] += dot_nn(og_t, hidden)
-    out_ref[...] = (middle + mlp_out).astype(BF16)
+    out_ref[...] = (middle + mlp_out).T.astype(BF16)
     width = middle.shape[1]
     acc_gain[:, :width] += jnp.sum((normed_grad * middle * scale).reshape(BLOCK // 8, 8, width), axis=0)
     weighted = normed_grad * gain
@@ -291,14 +291,14 @@
             pl.BlockSpec(selector.shape, whole),
         ],
         out_specs=[
-            pl.BlockSpec((BLOCK, width), rows),
+            pl.BlockSpec((width, BLOCK), lambda i: (0, i)),
             pl.BlockSpec((BLOCK, width), rows),
             pl.BlockSpec((HEADS, BLOCK, HEAD), lambda i: (0, i, 0)),
             pl.BlockSpec((16, BLOCK), lambda i: (0, i)),
             block, block, block, block,
         ],
         out_shape=[
-            jax.ShapeDtypeStruct((tokens, width), BF16),
+            jax.ShapeDtypeStruct((width, tokens), BF16),
             jax.ShapeDtypeStruct((tokens, width), F32),
             jax.ShapeDtypeStruct((HEADS, tokens, HEAD), BF16),
             jax.ShapeDtypeStruct((16, tokens), F32),
@@ -382,7 +382,8 @@
     acc_gain[:, :x.shape[1]] += jnp.sum((normed_grad * x * scale).reshape(BLOCK // 8, 8, x.shape[1]), axis=0)
     weighted = normed_grad * gain
     inner = jnp.sum(weighted * x, axis=-1, keepdims=True)
-    ig_ref[...] = mg_ref[...] + scale * weighted - x * (scale * scale * scale) * inner / x.shape[1]
+    input_grad = mg_ref[...] + scale * weighted - x * (scale * scale * scale) * inner / x.shape[1]
+    ig_ref[...] = input_grad.T
 
     @pl.when(j == blocks - 1)
     def _():
@@ -433,11 +434,11 @@
             pl.BlockSpec(w_qkv.shape, whole),
         ],
         out_specs=[
-            pl.BlockSpec((BLOCK, width), rows),
+            pl.BlockSpec((width, BLOCK), lambda j: (0, j)),
             block, block,
         ],
         out_shape=[
-            jax.ShapeDtypeStruct((tokens, width), F32),
+            jax.ShapeDtypeStruct((width, tokens), F32),
             jax.ShapeDtypeStruct((tall, LANES), BF16),
             jax.ShapeDtypeStruct((tall, LANES), BF16),
         ],
@@ -554,13 +555,10 @@
             ins = ins[len(parts):]
             first += len(parts) * parts[0].shape[0]
         base = 0
-        for t, ref in enumerate((gate_ref, up_ref, down_ref)):
+        for ref in (gate_ref, up_ref, down_ref):
             for part in range(cols_half // LANES):
                 tile = grads[base:base + rows_half, :].astype(F32)
-                if t < 2:
-                    ref[:, part * LANES:(part + 1) * LANES] = tile
-                else:
-                    ref[part * LANES:(part + 1) * LANES, :] = tile.T
+                ref[:, part * LANES:(part + 1) * LANES] = tile
                 base += rows_half
         rest_ref[...] = grads[used:, :]
 
@@ -571,7 +569,7 @@
         out_shape=[
             jax.ShapeDtypeStruct((rows_half, cols_half), F32),
             jax.ShapeDtypeStruct((rows_half, cols_half), F32),
-            jax.ShapeDtypeStruct((cols_half, rows_half), F32),
+            jax.ShapeDtypeStruct((rows_half, cols_half), F32),
             jax.ShapeDtypeStruct((total - used, LANES), BF16),
         ],
         scratch_shapes=[pltpu.VMEM((total, LANES), BF16)],
@@ -749,7 +747,8 @@
         where, s_parts, rest_parts, slots[row], width, w_qkv.shape[1]
     )
     return (
-        outputs, input_grad, grad_norm_one[0], grad_qkv, grad_out, grad_norm_two[0], grad_gate, grad_up, grad_down
+        outputs.T, input_grad.T, grad_norm_one.reshape(width), grad_qkv, grad_out, grad_norm_two.reshape(width),
+        grad_gate, grad_up, grad_down.T
     )
 
 

time: 285 us -> 281 us (0.986)
  local copies, waits for them, and re-layouts: 23.3 us -> 17.4 us
    unnamed x79 -> x76, local copies, waits for them, and re-layouts: 21.5 us -> 15.5 us
  transfers between devices with their start and end apart: 36 -> 36, of which waited for: 17 -> 18; matrix products, arithmetic and copies ran while one was open for 7% -> 4% of each run, Pallas kernels for 28% -> 29%
where the time goes in v4:
time: 281 us
  Pallas kernels  135 us (48%)
  waiting for transfers between devices  74.1 us (26%)
  starting transfers between devices  42.3 us (15%)
  local copies, waits for them, and re-layouts  17.4 us (6%)
  other arithmetic  10.2 us (4%)
    ppermute x36, waiting for transfers between devices, swap_with(): return lax.ppermute(data, axis, [(n, n ^ mask) for n in range(size)])  74.1 us
    ppermute x36, starting transfers between devices, swap_with(): return lax.ppermute(data, axis, [(n, n ^ mask) for n in range(size)])  42.3 us
    pallas_call x1, Pallas kernels, mlp(): pl.pallas_call(mlp_kernel, grid=(blocks,), in_specs=[pl.BlockSpec(memory_...  42 us
    pallas_call x1, Pallas kernels, back(): pl.pallas_call(back_kernel, grid=(blocks,), in_specs=[pl.BlockSpec(memory...  32.8 us
    pallas_call x1, Pallas kernels, front(): pl.pallas_call(front_kernel, grid=(blocks,), in_specs=[pl.BlockSpec((BLOC...  28.8 us
    pallas_call x6, Pallas kernels, merge(): pl.pallas_call(kernel, in_specs=[SMEM_SPEC] + [VMEM_SPEC] * len(operands)...  17.3 us
    unnamed x76, local copies, waits for them, and re-layouts  15.5 us
    pallas_call x4, Pallas kernels, join(): pl.pallas_call(kernel, in_specs=[SMEM_SPEC] + [VMEM_SPEC] * len(operands)...  7.6 us
  transfers between devices with their start and end apart: 36, of which 18 were waited for; matrix products, arithmetic and copies ran while one was open for 4% of the time, Pallas kernels for 29%

profile of v4, /device:TPU:0, one launch (start us, length us, event | category | flops | bytes accessed | tf_op | source)
XLA Modules:
  0.0 280.7 jit_solution(13418555124268436705)
XLA Ops:
  2.2 3.1 %collective-permute-start = (bf16[3,288,768]{2,1,0:T(8,128)(2,1)S(1)}, bf16[3,288,768]{2,1,0:T(8,128)(2,1)}, u32[]{:S(2)}, u32[]{:S(2)}) collective-permute-start(bf16[3,288,768]{2,1,0:T(8,128)(2,1)S(1)} %pad_maximum_fusion.own_ref), channel_id=1, source_target_pairs={{0,1},{1,0},{2,3},{3,2},{4,5},{5,4},{6,7},{7,6},{8,9},{9,8},{10,11... | collective-permute-start | bytes 3981320 | tf_op jit(solution)/shard_map/ppermute | solution.py:639
  7.7 26.8 %collective-permute-done.side_ref = bf16[3,288,768]{2,1,0:T(8,128)(2,1)} collective-permute-done((bf16[3,288,768]{2,1,0:T(8,128)(2,1)S(1)}, bf16[3,288,768]{2,1,0:T(8,128)(2,1)}, u32[]{:S(2)}, u32[]{:S(2)}) %collective-permute-start) | collective-permute-done | bytes 1327136 | tf_op jit(solution)/shard_map/ppermute | solution.py:639
  37.8 2.4 copy.27.og_ref
  44.6 28.8 %front.1 = (bf16[9,1024,64]{2,1,0:T(8,128)(2,1)}, bf16[3,1024,64]{2,1,0:T(8,128)(2,1)}, bf16[3,1024,64]{2,1,0:T(8,128)(2,1)}, f32[16,1024]{1,0:T(8,128)}, bf16[1...) custom-call(bf16[1024,576]{1,0:T(8,128)(2,1)} %copy.26.inputs_ref, s32[1,1024]{1,0:T(1,128)} %bitcast.24, ...), custom_call_target="tpu_custom_call" | custom-call | flops 6000000000 | bytes 12000000 | tf_op jit(solution)/shard_map/front/pallas_call | solution.py:126
  73.5 42.0 %mlp.1 = (bf16[576,1024]{1,0:T(8,128)(2,1)}, f32[1024,576]{1,0:T(8,128)}, bf16[9,1024,64]{2,1,0:T(8,128)(2,1)}, f32[16,1024]{1,0:T(8,128)}, bf16[6144,128]{1,0:T...) custom-call(s32[4]{0:T(128)} %pad_add_fusion.place_ref.where_ref, ...), custom_call_target="tpu_custom_call" | custom-call | flops 17999998976 | bytes 24000000 | tf_op jit(solution)/shard_map/mlp/pallas_call | solution.py:277
  116.1 3.2 %collective-permute-done.4.refs_1_ = bf16[6144,128]{1,0:T(8,128)(2,1)S(1)} collective-permute-done((bf16[6144,128]{1,0:T(8,128)(2,1)}, bf16[6144,128]{1,0:T(8,128)(2,1)S(1)}, u32[]{:S(2)}, u32[]{:S(2)}) %collective-permute-start.4) | collective-permute-done | bytes 1572896 | tf_op jit(solution)/shard_map/ppermute | solution.py:639
  120.5 3.4 %shard_map.169 = bf16[6144,128]{1,0:T(8,128)(2,1)} custom-call(s32[4]{0:T(128)} %pad_add_fusion.place_ref.where_ref, bf16[6144,128]{1,0:T(8,128)(2,1)} %get-tuple-element.73.refs_0_, bf16[6144,128]{1,0:T(8,128)(2,1)} %copy-done.2), custom_call_target="tpu_custom_call" | custom-call | flops 1572864 | bytes 4718592 | tf_op jit(solution)/shard_map/pallas_call | solution.py:502
  125.6 32.8 %back.1 = (f32[576,1024]{1,0:T(8,128)}, bf16[2560,128]{1,0:T(8,128)(2,1)}, bf16[2560,128]{1,0:T(8,128)(2,1)}) custom-call(s32[4]{0:T(128)} %pad_add_fusion.place_ref.where_ref, bf16[9,1024,64]{2,1,0:T(8,128)(2,1)} %get-tuple-element.63.q_ref, bf16[3,1024,64]{2,1,0:T(8,128)(2,1)} %get-tuple-element.64.k_ref, bf16[3,1024,64]{2,1,0:T(8,128)(2,1)} %get-tuple-element.65.v_ref, ...), custom_call_target="tpu_custom_call" | custom-call | flops 8000000000 | bytes 16000000 | tf_op jit(solution)/shard_map/back/pallas_call | solution.py:417
  162.0 5.5 %shard_map.170 = (bf16[2048,128]{1,0:T(8,128)(2,1)}, bf16[2048,128]{1,0:T(8,128)(2,1)}, bf16[512,128]{1,0:T(8,128)(2,1)}, bf16[512,128]{1,0:T(8,128)(2,1)}, bf16...) custom-call(s32[4]{0:T(128)} %pad_add_fusion.place_ref.where_ref, bf16[6144,128]{1,0:T(8,128)(2,1)} %get-tuple-element.71.refs_0_.refs_3_, ...), custom_call_target="tpu_custom_call" | custom-call | flops 2359296 | bytes 7077888 | tf_op jit(solution)/shard_map/pallas_call | solution.py:502
  174.4 2.6 collective-permute-start.8
  177.3 3.2 %collective-permute-done.11.refs_7_ = bf16[1280,128]{1,0:T(8,128)(2,1)S(1)} collective-permute-done((bf16[1280,128]{1,0:T(8,128)(2,1)}, bf16[1280,128]{1,0:T(8,128)(2,1)S(1)}, u32[]{:S(2)}, u32[]{:S(2)}) %collective-permute-start.11) | collective-permute-done | bytes 327712 | tf_op jit(solution)/shard_map/ppermute | solution.py:639
  180.4 6.3 %collective-permute-done.8.refs_4_ = bf16[512,128]{1,0:T(8,128)(2,1)S(1)} collective-permute-done((bf16[512,128]{1,0:T(8,128)(2,1)}, bf16[512,128]{1,0:T(8,128)(2,1)S(1)}, u32[]{:S(2)}, u32[]{:S(2)}) %collective-permute-start.8) | collective-permute-done | bytes 131104 | tf_op jit(solution)/shard_map/ppermute | solution.py:639
  187.6 2.6 shard_map.172
  196.7 3.0 %collective-permute-done.15.refs_5_ = bf16[256,128]{1,0:T(8,128)(2,1)S(1)} collective-permute-done((bf16[256,128]{1,0:T(8,128)(2,1)}, bf16[256,128]{1,0:T(8,128)(2,1)S(1)}, u32[]{:S(2)}, u32[]{:S(2)}) %collective-permute-start.15) | collective-permute-done | bytes 65568 | tf_op jit(solution)/shard_map/ppermute | solution.py:639
  199.6 4.3 %collective-permute-done.13.refs_2_ = bf16[512,128]{1,0:T(8,128)(2,1)S(1)} collective-permute-done((bf16[512,128]{1,0:T(8,128)(2,1)}, bf16[512,128]{1,0:T(8,128)(2,1)S(1)}, u32[]{:S(2)}, u32[]{:S(2)}) %collective-permute-start.13) | collective-permute-done | bytes 131104 | tf_op jit(solution)/shard_map/ppermute | solution.py:639
  212.7 3.0 %collective-permute-done.28.refs_5_ = bf16[256,128]{1,0:T(8,128)(2,1)S(1)} collective-permute-done((bf16[256,128]{1,0:T(8,128)(2,1)}, bf16[256,128]{1,0:T(8,128)(2,1)S(1)}, u32[]{:S(2)}, u32[]{:S(2)}) %collective-permute-start.28) | collective-permute-done | bytes 65568 | tf_op jit(solution)/shard_map/ppermute | solution.py:639
  215.7 4.0 %collective-permute-done.26.refs_2_ = bf16[512,128]{1,0:T(8,128)(2,1)S(1)} collective-permute-done((bf16[512,128]{1,0:T(8,128)(2,1)}, bf16[512,128]{1,0:T(8,128)(2,1)S(1)}, u32[]{:S(2)}, u32[]{:S(2)}) %collective-permute-start.26) | collective-permute-done | bytes 131104 | tf_op jit(solution)/shard_map/ppermute | solution.py:639
  224.5 3.1 %collective-permute-start.18 = (bf16[160,128]{1,0:T(8,128)(2,1)}, bf16[160,128]{1,0:T(8,128)(2,1)S(1)}, u32[]{:S(2)}, u32[]{:S(2)}) collective-permute-start(bf16[160,128]{1,0:T(8,128)(2,1)} %get-tuple-element.95), channel_id=1, source_target_pairs={{0,16},{4,20},{8,24},{12,28},{16,0},{20,4},{24,8},{28,12},{1,17},{... | collective-permute-start | bytes 122888 | tf_op jit(solution)/shard_map/ppermute | solution.py:639
  229.8 3.8 %collective-permute-done.19.refs_3_ = bf16[160,128]{1,0:T(8,128)(2,1)S(1)} collective-permute-done((bf16[160,128]{1,0:T(8,128)(2,1)}, bf16[160,128]{1,0:T(8,128)(2,1)S(1)}, u32[]{:S(2)}, u32[]{:S(2)}) %collective-permute-start.19) | collective-permute-done | bytes 40992 | tf_op jit(solution)/shard_map/ppermute | solution.py:639
  237.0 3.1 %collective-permute-start.20 = (bf16[160,128]{1,0:T(8,128)(2,1)}, bf16[160,128]{1,0:T(8,128)(2,1)S(1)}, u32[]{:S(2)}, u32[]{:S(2)}) collective-permute-start(bf16[160,128]{1,0:T(8,128)(2,1)} %shard_map.174.refs_0_), channel_id=1, source_target_pairs={{0,8},{4,12},{8,0},{12,4},{16,24},{20,28},{24,16},{28,20},{1,9},{5... | collective-permute-start | bytes 122888 | tf_op jit(solution)/shard_map/ppermute | solution.py:639
  257.3 3.1 %shard_map.178 = (f32[288,768]{1,0:T(8,128)}, f32[288,768]{1,0:T(8,128)}, f32[288,768]{1,0:T(8,128)}, bf16[960,128]{1,0:T(8,128)(2,1)}) custom-call(s32[4]{0:T(128)} %pad_add_fusion.place_ref.where_ref, bf16[2048,128]{1,0:T(8,128)(2,1)} %get-tuple-element.99.refs_0_, bf16[2048,128]{1,0:T(8,128)(2,1)} %copy-done.7, ...), custom_call_target="tpu_custom_call" | custom-call | bytes 5000000 | tf_op jit(solution)/shard_map/pallas_call | solution.py:565
  263.3 3.5 %collective-permute-done.33.refs_3_ = bf16[960,128]{1,0:T(8,128)(2,1)S(1)} collective-permute-done((bf16[960,128]{1,0:T(8,128)(2,1)}, bf16[960,128]{1,0:T(8,128)(2,1)S(1)}, u32[]{:S(2)}, u32[]{:S(2)}) %collective-permute-start.33) | collective-permute-done | bytes 245792 | tf_op jit(solution)/shard_map/ppermute | solution.py:639
  270.4 2.5 collective-permute-done.35.r1
  274.5 3.7 %shard_map.180 = (f32[576,960]{1,0:T(8,128)}, f32[576,576]{1,0:T(8,128)}, f32[1,576]{1,0:T(1,128)}, f32[1,576]{1,0:T(1,128)}) custom-call(s32[4]{0:T(128)} %pad_add_fusion.place_ref.where_ref, bf16[2560,128]{1,0:T(8,128)(2,1)} %get-tuple-element.102.s0, bf16[2560,128]{1,0:T(8,128)(2,1)} %copy-done.5, bf16[1920,128]{1,0:T(8,128)(2,1)} %get-tuple-element.103.r0, ...), custom_call_target="tpu_custom_call" | custom-call | bytes 5000000 | tf_op jit(solution)/shard_map/pallas_call | solution.py:611
  (157 shorter events, 79.6 us)
Async XLA Ops:
  2.2 32.3 %collective-permute-start = (bf16[3,288,768]{2,1,0:T(8,128)(2,1)S(1)}, bf16[3,288,768]{2,1,0:T(8,128)(2,1)}, u32[]{:S(2)}, u32[]{:S(2)}) collective-permute-start(bf16[3,288,768]{2,1,0:T(8,128)(2,1)S(1)} %pad_maximum_fusion.own_ref), channel_id=1, source_target_pairs={{0,1},{1,0},{2,3},{3,2},{4,5},{5,4},{6,7},{7,6},{8,9},{9,8},{10,11... | collective-permute-start | bytes 3981320 | tf_op jit(solution)/shard_map/ppermute | solution.py:639
  5.3 68.2 %collective-permute-start.1 = (bf16[3,288,768]{2,1,0:T(8,128)(2,1)S(1)}, bf16[3,288,768]{2,1,0:T(8,128)(2,1)}, u32[]{:S(2)}, u32[]{:S(2)}) collective-permute-start(bf16[3,288,768]{2,1,0:T(8,128)(2,1)S(1)} %pad_maximum_fusion.own_ref), channel_id=1, source_target_pairs={{0,2},{2,0},{1,3},{3,1},{4,6},{6,4},{5,7},{7,5},{8,10},{10,8},{9,1... | collective-permute-start | bytes 3981320 | tf_op jit(solution)/shard_map/ppermute | solution.py:639
  34.5 38.9 %collective-permute-start.2 = (bf16[3,288,768]{2,1,0:T(8,128)(2,1)}, bf16[3,288,768]{2,1,0:T(8,128)(2,1)}, u32[]{:S(2)}, u32[]{:S(2)}) collective-permute-start(bf16[3,288,768]{2,1,0:T(8,128)(2,1)} %collective-permute-done.side_ref), channel_id=1, source_target_pairs={{0,2},{2,0},{1,3},{3,1},{4,6},{6,4},{5,7},{7,5},{8,10},{10,8},{9,1... | collective-permute-start | bytes 3981320 | tf_op jit(solution)/shard_map/ppermute | solution.py:639
  116.0 42.6 %collective-permute-start.3 = (bf16[6144,128]{1,0:T(8,128)(2,1)}, bf16[6144,128]{1,0:T(8,128)(2,1)S(1)}, u32[]{:S(2)}, u32[]{:S(2)}) collective-permute-start(bf16[6144,128]{1,0:T(8,128)(2,1)} %get-tuple-element.72), channel_id=1, source_target_pairs={{0,2},{2,0},{1,3},{3,1},{4,6},{6,4},{5,7},{7,5},{8,10},{10,8},{9,1... | collective-permute-start | bytes 4718600 | tf_op jit(solution)/shard_map/ppermute | solution.py:639
  123.9 36.9 %collective-permute-start.5 = (bf16[6144,128]{1,0:T(8,128)(2,1)}, bf16[6144,128]{1,0:T(8,128)(2,1)S(1)}, u32[]{:S(2)}, u32[]{:S(2)}) collective-permute-start(bf16[6144,128]{1,0:T(8,128)(2,1)} %shard_map.169), channel_id=1, source_target_pairs={{0,1},{1,0},{2,3},{3,2},{4,5},{5,4},{6,7},{7,6},{8,9},{9,8},{10,11... | collective-permute-start | bytes 4718600 | tf_op jit(solution)/shard_map/ppermute | solution.py:639
  158.5 10.7 %collective-permute-start.10 = (bf16[2560,128]{1,0:T(8,128)(2,1)}, bf16[2560,128]{1,0:T(8,128)(2,1)}, u32[]{:S(2)}, u32[]{:S(2)}) collective-permute-start(bf16[2560,128]{1,0:T(8,128)(2,1)} %get-tuple-element.82), channel_id=1, source_target_pairs={{0,2},{2,0},{1,3},{3,1},{4,6},{6,4},{5,7},{7,5},{8,10},{10,8},{9,1... | collective-permute-start | bytes 1966088 | tf_op jit(solution)/shard_map/ppermute | solution.py:639
  167.4 19.3 %collective-permute-start.6 = (bf16[2048,128]{1,0:T(8,128)(2,1)}, bf16[2048,128]{1,0:T(8,128)(2,1)S(1)}, u32[]{:S(2)}, u32[]{:S(2)}) collective-permute-start(bf16[2048,128]{1,0:T(8,128)(2,1)} %get-tuple-element.76), channel_id=1, source_target_pairs={{0,4},{4,0},{8,12},{12,8},{16,20},{20,16},{24,28},{28,24},{1,5},{5... | collective-permute-start | bytes 1572872 | tf_op jit(solution)/shard_map/ppermute | solution.py:639
  171.4 9.1 %collective-permute-start.11 = (bf16[1280,128]{1,0:T(8,128)(2,1)}, bf16[1280,128]{1,0:T(8,128)(2,1)S(1)}, u32[]{:S(2)}, u32[]{:S(2)}) collective-permute-start(bf16[1280,128]{1,0:T(8,128)(2,1)} %get-tuple-element.84), channel_id=1, source_target_pairs={{0,1},{1,0},{2,3},{3,2},{4,5},{5,4},{6,7},{7,6},{8,9},{9,8},{10,11... | collective-permute-start | bytes 983048 | tf_op jit(solution)/shard_map/ppermute | solution.py:639
  172.9 7.6 %collective-permute-start.7 = (bf16[512,128]{1,0:T(8,128)(2,1)}, bf16[512,128]{1,0:T(8,128)(2,1)S(1)}, u32[]{:S(2)}, u32[]{:S(2)}) collective-permute-start(bf16[512,128]{1,0:T(8,128)(2,1)} %get-tuple-element.78), channel_id=1, source_target_pairs={{0,8},{4,12},{8,0},{12,4},{16,24},{20,28},{24,16},{28,20},{1,9},{5... | collective-permute-start | bytes 393224 | tf_op jit(solution)/shard_map/ppermute | solution.py:639
  174.4 12.3 %collective-permute-start.8 = (bf16[512,128]{1,0:T(8,128)(2,1)}, bf16[512,128]{1,0:T(8,128)(2,1)S(1)}, u32[]{:S(2)}, u32[]{:S(2)}) collective-permute-start(bf16[512,128]{1,0:T(8,128)(2,1)} %get-tuple-element.79), channel_id=1, source_target_pairs={{0,16},{4,20},{8,24},{12,28},{16,0},{20,4},{24,8},{28,12},{1,17},{... | collective-permute-start | bytes 393224 | tf_op jit(solution)/shard_map/ppermute | solution.py:639
  177.0 9.7 %collective-permute-start.9 = (bf16[512,128]{1,0:T(8,128)(2,1)}, bf16[512,128]{1,0:T(8,128)(2,1)S(1)}, u32[]{:S(2)}, u32[]{:S(2)}) collective-permute-start(bf16[512,128]{1,0:T(8,128)(2,1)} %get-tuple-element.80), channel_id=1, source_target_pairs={{0,24},{4,28},{8,16},{12,20},{16,8},{20,12},{24,0},{28,4},{1,25},{... | collective-permute-start | bytes 393224 | tf_op jit(solution)/shard_map/ppermute | solution.py:639
  190.2 13.8 %collective-permute-start.16 = (bf16[640,128]{1,0:T(8,128)(2,1)}, bf16[640,128]{1,0:T(8,128)(2,1)S(1)}, u32[]{:S(2)}, u32[]{:S(2)}) collective-permute-start(bf16[640,128]{1,0:T(8,128)(2,1)} %get-tuple-element.92), channel_id=1, source_target_pairs={{0,4},{4,0},{8,12},{12,8},{16,20},{20,16},{24,28},{28,24},{1,5},{5... | collective-permute-start | bytes 491528 | tf_op jit(solution)/shard_map/ppermute | solution.py:639
  190.8 8.9 %collective-permute-start.12 = (bf16[512,128]{1,0:T(8,128)(2,1)}, bf16[512,128]{1,0:T(8,128)(2,1)S(1)}, u32[]{:S(2)}, u32[]{:S(2)}) collective-permute-start(bf16[512,128]{1,0:T(8,128)(2,1)} %get-tuple-element.86), channel_id=1, source_target_pairs={{0,8},{4,12},{8,0},{12,4},{16,24},{20,28},{24,16},{28,20},{1,9},{5... | collective-permute-start | bytes 393224 | tf_op jit(solution)/shard_map/ppermute | solution.py:639
  192.7 11.3 %collective-permute-start.13 = (bf16[512,128]{1,0:T(8,128)(2,1)}, bf16[512,128]{1,0:T(8,128)(2,1)S(1)}, u32[]{:S(2)}, u32[]{:S(2)}) collective-permute-start(bf16[512,128]{1,0:T(8,128)(2,1)} %get-tuple-element.87), channel_id=1, source_target_pairs={{0,16},{4,20},{8,24},{12,28},{16,0},{20,4},{24,8},{28,12},{1,17},{... | collective-permute-start | bytes 393224 | tf_op jit(solution)/shard_map/ppermute | solution.py:639
  193.8 10.2 %collective-permute-start.14 = (bf16[512,128]{1,0:T(8,128)(2,1)}, bf16[512,128]{1,0:T(8,128)(2,1)S(1)}, u32[]{:S(2)}, u32[]{:S(2)}) collective-permute-start(bf16[512,128]{1,0:T(8,128)(2,1)} %get-tuple-element.88), channel_id=1, source_target_pairs={{0,24},{4,28},{8,16},{12,20},{16,8},{20,12},{24,0},{28,4},{1,25},{... | collective-permute-start | bytes 393224 | tf_op jit(solution)/shard_map/ppermute | solution.py:639
  206.8 8.9 %collective-permute-start.27 = (bf16[512,128]{1,0:T(8,128)(2,1)}, bf16[512,128]{1,0:T(8,128)(2,1)S(1)}, u32[]{:S(2)}, u32[]{:S(2)}) collective-permute-start(bf16[512,128]{1,0:T(8,128)(2,1)} %get-tuple-element.97.refs_0_), channel_id=1, source_target_pairs={{0,24},{4,28},{8,16},{12,20},{16,8},{20,12},{24,0},{28,4},{1,25},{... | collective-permute-start | bytes 393224 | tf_op jit(solution)/shard_map/ppermute | solution.py:639
  208.9 10.8 %collective-permute-start.26 = (bf16[512,128]{1,0:T(8,128)(2,1)}, bf16[512,128]{1,0:T(8,128)(2,1)S(1)}, u32[]{:S(2)}, u32[]{:S(2)}) collective-permute-start(bf16[512,128]{1,0:T(8,128)(2,1)} %get-tuple-element.97.refs_0_), channel_id=1, source_target_pairs={{0,16},{4,20},{8,24},{12,28},{16,0},{20,4},{24,8},{28,12},{1,17},{... | collective-permute-start | bytes 393224 | tf_op jit(solution)/shard_map/ppermute | solution.py:639
  210.3 9.4 %collective-permute-start.25 = (bf16[512,128]{1,0:T(8,128)(2,1)}, bf16[512,128]{1,0:T(8,128)(2,1)S(1)}, u32[]{:S(2)}, u32[]{:S(2)}) collective-permute-start(bf16[512,128]{1,0:T(8,128)(2,1)} %get-tuple-element.97.refs_0_), channel_id=1, source_target_pairs={{0,8},{4,12},{8,0},{12,4},{16,24},{20,28},{24,16},{28,20},{1,9},{5... | collective-permute-start | bytes 393224 | tf_op jit(solution)/shard_map/ppermute | solution.py:639
  223.0 32.8 %collective-permute-start.29 = (bf16[2048,128]{1,0:T(8,128)(2,1)}, bf16[2048,128]{1,0:T(8,128)(2,1)S(1)}, u32[]{:S(2)}, u32[]{:S(2)}) collective-permute-start(bf16[2048,128]{1,0:T(8,128)(2,1)} %get-tuple-element.99.refs_0_), channel_id=1, source_target_pairs={{0,4},{4,0},{8,12},{12,8},{16,20},{20,16},{24,28},{28,24},{1,5},{5... | collective-permute-start | bytes 1572872 | tf_op jit(solution)/shard_map/ppermute | solution.py:639
  246.0 7.9 %collective-permute-start.32 = (bf16[512,128]{1,0:T(8,128)(2,1)}, bf16[512,128]{1,0:T(8,128)(2,1)S(1)}, u32[]{:S(2)}, u32[]{:S(2)}) collective-permute-start(bf16[512,128]{1,0:T(8,128)(2,1)} %get-tuple-element.100.refs_2_), channel_id=1, source_target_pairs={{0,24},{4,28},{8,16},{12,20},{16,8},{20,12},{24,0},{28,4},{1,25},{... | collective-permute-start | bytes 393224 | tf_op jit(solution)/shard_map/ppermute | solution.py:639
  247.9 7.9 %collective-permute-start.31 = (bf16[512,128]{1,0:T(8,128)(2,1)}, bf16[512,128]{1,0:T(8,128)(2,1)S(1)}, u32[]{:S(2)}, u32[]{:S(2)}) collective-permute-start(bf16[512,128]{1,0:T(8,128)(2,1)} %get-tuple-element.100.refs_2_), channel_id=1, source_target_pairs={{0,16},{4,20},{8,24},{12,28},{16,0},{20,4},{24,8},{28,12},{1,17},{... | collective-permute-start | bytes 393224 | tf_op jit(solution)/shard_map/ppermute | solution.py:639
  248.5 7.4 %collective-permute-start.30 = (bf16[512,128]{1,0:T(8,128)(2,1)}, bf16[512,128]{1,0:T(8,128)(2,1)S(1)}, u32[]{:S(2)}, u32[]{:S(2)}) collective-permute-start(bf16[512,128]{1,0:T(8,128)(2,1)} %get-tuple-element.100.refs_2_), channel_id=1, source_target_pairs={{0,8},{4,12},{8,0},{12,4},{16,24},{20,28},{24,16},{28,20},{1,9},{5... | collective-permute-start | bytes 393224 | tf_op jit(solution)/shard_map/ppermute | solution.py:639
  253.4 9.9 %collective-permute-start.24 = (bf16[1280,128]{1,0:T(8,128)(2,1)}, bf16[1280,128]{1,0:T(8,128)(2,1)S(1)}, u32[]{:S(2)}, u32[]{:S(2)}) collective-permute-start(bf16[1280,128]{1,0:T(8,128)(2,1)} %shard_map.176.refs_0_), channel_id=1, source_target_pairs={{0,1},{1,0},{2,3},{3,2},{4,5},{5,4},{6,7},{7,6},{8,9},{9,8},{10,11... | collective-permute-start | bytes 983048 | tf_op jit(solution)/shard_map/ppermute | solution.py:639
  260.4 6.4 %collective-permute-start.33 = (bf16[960,128]{1,0:T(8,128)(2,1)}, bf16[960,128]{1,0:T(8,128)(2,1)S(1)}, u32[]{:S(2)}, u32[]{:S(2)}) collective-permute-start(bf16[960,128]{1,0:T(8,128)(2,1)} %get-tuple-element.101.refs_2_), channel_id=1, source_target_pairs={{0,1},{1,0},{2,3},{3,2},{4,5},{5,4},{6,7},{7,6},{8,9},{9,8},{10,11... | collective-permute-start | bytes 737288 | tf_op jit(solution)/shard_map/ppermute | solution.py:639
  (49 other events, 264.6 us)
